TPU v7x, 256 devices: a whole 4x4x8 slice. The times are simulated.
256 devices in a mesh: tiles: 64 (over y, z, core), rep: 4 (over x).
Axes of the slice: x: 4, y: 4, z: 8, core: 2. Of those that a mesh axis runs over, the one named last changes fastest.
Arguments:
- fields: bfloat16 [4, 64, 200, 768], P('rep', 'tiles'), may hold values from -6 to 6
- wet_bits: int32 [64, 6, 5], P('tiles'), may hold values from 0 to 1073741823, as said below
- neighbours: int32 [64, 8], P('tiles'), may hold values from -1 to 63, as said below
- kernel: float32 [200, 49], replicated, may hold values from -0.875 to 0.875
- conv_bias: float32 [200], replicated, may hold values from -3 to 3
- ln_gain: float32 [200], replicated, may hold values from 0.5 to 1.5
- ln_shift: float32 [200], replicated, may hold values from -3 to 3
- in_weight: bfloat16 [200, 800], replicated, may hold values from -0.4375 to 0.4375
- in_bias: float32 [800], replicated, may hold values from -3 to 3
- out_weight: bfloat16 [800, 200], replicated, may hold values from -0.21875 to 0.21875
- out_bias: float32 [200], replicated, may hold values from -3 to 3
- cotangent: bfloat16 [4, 64, 200, 768], P('rep', 'tiles'), may hold values from -6 to 6
Outputs:
- out_field: bfloat16 [4, 64, 200, 768], P('rep', 'tiles')
- input_grad: bfloat16 [4, 64, 200, 768], P('rep', 'tiles')
- grad_kernel: float32 [200, 49], replicated
- grad_conv_bias: float32 [200], replicated
- grad_gain: float32 [200], replicated
- grad_shift: float32 [200], replicated
- grad_in_weight: float32 [200, 800], replicated
- grad_in_bias: float32 [800], replicated
- grad_out_weight: float32 [800, 200], replicated
- grad_out_bias: float32 [200], replicated
Inputs may be any that keep to these rules, and one draw needn't show every extreme that they name: `neighbours`: tile slot s lies in band s; the slots of a band sit at increasing columns of a periodic row of 2 tile columns, the other columns being land. Entry k of row s names the slot of the wet tile beside tile s to the north (band - 1), south (band + 1), west, east, north-west, north-east, south-west or south-east (columns taken modulo 2), or -1 where that tile is land or lies beyond the first or last band. `wet_bits`: bit j (j < 30) of word w of row r of tile s is 1 where the cell in column 30 * w + j of that row is wet; bits for columns at or beyond 128 are ignored.
All inputs are finite; a program needn't handle non-finite values.
Results may differ from a plain program's by a relative error of at most 0.006.
Values may be sent and summed in bfloat16 or wider, within the bound.
No kernel may reach another device: no remote copies, remote signals or barrier semaphores. Data moves between devices by JAX's collectives and lax.ppermute only.
A program may use at most 128 MiB of HBM per device.

v0:
```python
import jax
import jax.numpy as jnp
from jax import lax
from jax.sharding import PartitionSpec as P

KERNEL_DILATION = 2
HALO = 6


gelu_scale = 0.7978845608028654


def shifted(value, axis, steps):
    count = lax.axis_size(axis)
    initial, last = (max(0, -steps), min(count, count - steps))
    return lax.ppermute(value, axis, [(source, source + steps) for source in range(initial, last)])


def gelu_pair(hidden):
    tanh_arg = gelu_scale * (hidden + 0.044715 * hidden * hidden * hidden)
    tanh_val = jnp.tanh(tanh_arg)
    active = 0.5 * hidden * (1.0 + tanh_val)
    derivative = 0.5 * (1.0 + tanh_val) + 0.5 * hidden * (
        1.0 - tanh_val * tanh_val
    ) * gelu_scale * (1.0 + 3.0 * 0.044715 * hidden * hidden)
    return (active, derivative)


def unpack_wet(packed, columns):
    spread = jnp.repeat(packed, 30, axis=-1)[..., :columns]
    offsets = jnp.arange(columns, dtype=jnp.int32) % 30
    return jnp.bitwise_and(jnp.right_shift(spread, offsets), 1)


def taps_sum(padded_field, kernel, tile_row_count, tile_column_count):
    summed = jnp.zeros(padded_field.shape[:2] + (tile_row_count, tile_column_count), jnp.float32)
    for first_operand in range(7):
        for second_operand in range(7):
            kernel_window = padded_field[
                :,
                :,
                KERNEL_DILATION * first_operand : KERNEL_DILATION * first_operand + tile_row_count,
                KERNEL_DILATION * second_operand : KERNEL_DILATION * second_operand
                + tile_column_count,
            ].astype(jnp.float32)
            summed = (
                summed
                + kernel_window * kernel[:, 7 * first_operand + second_operand][None, :, None, None]
            )
    return summed


def pad_cols(block, before, after):
    return jnp.pad(block, ((0, 0), (0, 0), (0, 0), (before, after)))


def body(
    fields,
    wet_bits,
    neighbours,
    kernel,
    conv_bias,
    ln_gain,
    ln_shift,
    in_weight,
    in_bias,
    out_weight,
    out_bias,
    cotangent,
):
    tiles_here = fields.shape[1]
    channels = fields.shape[2]
    cells = fields.shape[3]
    tile_row_count = wet_bits.shape[1]
    tile_column_count = cells // tile_row_count
    margin = HALO
    tile_shape = (tiles_here, channels, tile_row_count, tile_column_count)
    wet_mask = unpack_wet(wet_bits, tile_column_count).astype(jnp.bfloat16)[:, None]
    wet_float = wet_mask.astype(jnp.float32)
    masked = fields[0].reshape(tile_shape) * wet_mask
    first_slot = lax.axis_index("tiles") * tiles_here
    slot_ids = jnp.arange(tiles_here, dtype=jnp.int32)
    band_steps = (-1, 1, 0, 0, -1, -1, 1, 1)
    choosers = [
        neighbours[:, k][:, None] == (first_slot + band_steps[k] * tiles_here + slot_ids)[None, :]
        for k in range(8)
    ]

    def borrow(k, source):
        chooser = choosers[k].astype(source.dtype)
        return jnp.einsum(
            "ts,scrw->tcrw",
            chooser,
            source,
            preferred_element_type=jnp.float32,
            precision=lax.Precision.HIGHEST,
        ).astype(source.dtype)

    def deliver(k, region):
        chooser = choosers[k].astype(jnp.float32)
        return jnp.einsum(
            "ts,tcrw->scrw",
            chooser,
            region,
            preferred_element_type=jnp.float32,
            precision=lax.Precision.HIGHEST,
        )

    from_north = shifted(masked, "tiles", 1)
    from_south = shifted(masked, "tiles", -1)
    upper_band = jnp.concatenate(
        [
            borrow(4, from_north[..., tile_column_count - margin :]),
            borrow(0, from_north),
            borrow(5, from_north[..., :margin]),
        ],
        axis=3,
    )
    middle = jnp.concatenate(
        [
            borrow(2, masked[..., tile_column_count - margin :]),
            masked,
            borrow(3, masked[..., :margin]),
        ],
        axis=3,
    )
    lower_band = jnp.concatenate(
        [
            borrow(6, from_south[..., tile_column_count - margin :]),
            borrow(1, from_south),
            borrow(7, from_south[..., :margin]),
        ],
        axis=3,
    )
    padded_field = jnp.concatenate([upper_band, middle, lower_band], axis=2)
    convolved = conv_bias[None, :, None, None] + taps_sum(
        padded_field, kernel, tile_row_count, tile_column_count
    )
    centred = convolved - jnp.mean(convolved, axis=1, keepdims=True)
    inv_std = lax.rsqrt(jnp.mean(centred * centred, axis=1, keepdims=True) + 1e-06)
    normed = centred * inv_std
    normout = (normed * ln_gain[None, :, None, None] + ln_shift[None, :, None, None]).astype(
        jnp.bfloat16
    )
    flattened = normout.reshape(tiles_here, channels, cells)
    hidden = (
        jnp.einsum("tcn,ch->thn", flattened, in_weight, preferred_element_type=jnp.float32)
        + in_bias[None, :, None]
    )
    active, derivative = gelu_pair(hidden)
    active_b = active.astype(jnp.bfloat16)
    update = (
        jnp.einsum("thn,hc->tcn", active_b, out_weight, preferred_element_type=jnp.float32)
        + out_bias[None, :, None]
    )
    wet_flat = wet_float.reshape(tiles_here, 1, cells)
    masked_flat = masked.reshape(tiles_here, channels, cells)
    out_field = (wet_flat * (masked_flat.astype(jnp.float32) + update)).astype(jnp.bfloat16)
    out_grad = cotangent[0] * wet_mask.reshape(tiles_here, 1, cells)
    act_grad = jnp.einsum("tcn,hc->thn", out_grad, out_weight, preferred_element_type=jnp.float32)
    hid_grad = (act_grad * derivative).astype(jnp.bfloat16)
    norm_grad = jnp.einsum(
        "thn,ch->tcn", hid_grad, in_weight, preferred_element_type=jnp.float32
    ).reshape(tile_shape)
    grad_in_weight = jnp.einsum(
        "tcn,thn->ch", flattened, hid_grad, preferred_element_type=jnp.float32
    )
    grad_in_bias = jnp.sum(hid_grad.astype(jnp.float32), axis=(0, 2))
    grad_out_weight = jnp.einsum(
        "thn,tcn->hc", active_b, out_grad, preferred_element_type=jnp.float32
    )
    grad_out_bias = jnp.sum(out_grad.astype(jnp.float32), axis=(0, 2))
    scaled_grad = norm_grad * ln_gain[None, :, None, None]
    conv_grad = (
        inv_std
        * (
            scaled_grad
            - jnp.mean(scaled_grad, axis=1, keepdims=True)
            - normed * jnp.mean(scaled_grad * normed, axis=1, keepdims=True)
        )
    ).astype(jnp.bfloat16)
    grad_gain = jnp.sum(norm_grad * normed, axis=(0, 2, 3))
    grad_shift = jnp.sum(norm_grad, axis=(0, 2, 3))
    grad_conv_bias = jnp.sum(conv_grad.astype(jnp.float32), axis=(0, 2, 3))
    kernel_cols = []
    for first_operand in range(7):
        for second_operand in range(7):
            kernel_window = padded_field[
                :,
                :,
                KERNEL_DILATION * first_operand : KERNEL_DILATION * first_operand + tile_row_count,
                KERNEL_DILATION * second_operand : KERNEL_DILATION * second_operand
                + tile_column_count,
            ]
            kernel_cols.append(
                jnp.einsum(
                    "tcrw,tcrw->c", conv_grad, kernel_window, preferred_element_type=jnp.float32
                )
            )
    grad_kernel = jnp.stack(kernel_cols, axis=1)
    _, pullback = jax.vjp(
        lambda grid_in: taps_sum(grid_in, kernel, tile_row_count, tile_column_count),
        jnp.zeros(padded_field.shape, jnp.float32),
    )
    (grid_grad,) = pullback(conv_grad.astype(jnp.float32))
    upper_part = grid_grad[:, :, :margin, :]
    lower_part = grid_grad[:, :, margin + tile_row_count :, :]
    middle = grid_grad[:, :, margin : margin + tile_row_count, :]
    to_north = (
        pad_cols(deliver(4, upper_part[..., :margin]), tile_column_count - margin, 0)
        + deliver(0, upper_part[..., margin : margin + tile_column_count])
        + pad_cols(
            deliver(5, upper_part[..., margin + tile_column_count :]), 0, tile_column_count - margin
        )
    )
    to_south = (
        pad_cols(deliver(6, lower_part[..., :margin]), tile_column_count - margin, 0)
        + deliver(1, lower_part[..., margin : margin + tile_column_count])
        + pad_cols(
            deliver(7, lower_part[..., margin + tile_column_count :]), 0, tile_column_count - margin
        )
    )
    own_part = (
        middle[..., margin : margin + tile_column_count]
        + pad_cols(deliver(2, middle[..., :margin]), tile_column_count - margin, 0)
        + pad_cols(
            deliver(3, middle[..., margin + tile_column_count :]), 0, tile_column_count - margin
        )
    )
    south_sums = shifted(to_north.astype(jnp.bfloat16), "tiles", -1).astype(to_north.dtype)
    north_sums = shifted(to_south.astype(jnp.bfloat16), "tiles", 1).astype(to_south.dtype)
    mask_grad = own_part + south_sums + north_sums
    input_grad = (
        wet_float * (out_grad.reshape(tile_shape).astype(jnp.float32) + mask_grad)
    ).astype(jnp.bfloat16)
    reduced = lax.psum(
        (
            grad_kernel,
            grad_conv_bias,
            grad_gain,
            grad_shift,
            grad_in_weight,
            grad_in_bias,
            grad_out_weight,
            grad_out_bias,
        ),
        ("tiles", "rep"),
    )
    norm_factor = float(lax.axis_size("tiles") * lax.axis_size("rep") * tiles_here * cells) ** (
        -0.5
    )
    return (
        out_field.reshape(1, tiles_here, channels, cells),
        input_grad.reshape(1, tiles_here, channels, cells),
        reduced[0] * norm_factor,
        reduced[1] * norm_factor,
        reduced[2] * norm_factor,
        reduced[3] * norm_factor,
        reduced[4] * norm_factor,
        reduced[5] * norm_factor,
        reduced[6] * norm_factor,
        reduced[7] * norm_factor,
    )


def solution(mesh):
    placed = (
        P("rep", "tiles", None, None),
        P("tiles", None, None),
        P("tiles", None),
        P(),
        P(),
        P(),
        P(),
        P(),
        P(),
        P(),
        P(),
        P("rep", "tiles", None, None),
    )
    return jax.shard_map(
        body,
        mesh=mesh,
        in_specs=placed,
        out_specs=(
            P("rep", "tiles", None, None),
            P("rep", "tiles", None, None),
            P(),
            P(),
            P(),
            P(),
            P(),
            P(),
            P(),
            P(),
        ),
        check_vma=False,
    )
```

profile of v0, /device:TPU:8, one launch (start us, length us, event | category | flops | bytes accessed | tf_op | source)
XLA Modules:
  0.0 557.4 jit_solution(12647164100430089113)
XLA Ops:
  10.2 7.1 %collective-permute-start.1 = (bf16[1,200,6,128]{3,2,1,0:T(8,128)(2,1)S(1)}, bf16[1,200,6,128]{3,2,1,0:T(8,128)(2,1)S(1)}, u32[]{:S(2)}, u32[]{:S(2)}) collective-permute-start(bf16[1,200,6,128]{3,2,1,0:T(8,128)(2,1)S(1)} %broadcast_multiply_fusion.2), channel_id=1, source_target_pairs={{4,0},{8,4},{12,8},{16,12},{20,16},{24,20},{28,24},{32,28},{36,32}... | collective-permute-start | bytes 921608 | tf_op jit(solution)/shard_map/ppermute | solution.py:16
  27.0 2.1 reshape_squeeze.9
  29.1 2.1 squeeze.6
  37.4 4.5 maximum_maximum_fusion
  42.3 26.2 %fusion.134 = (f32[6,128]{1,0:T(8,128)S(1)}, f32[1,200,6,128]{3,2,1,0:T(8,128)S(1)}) fusion(f32[200]{0:T(256)S(1)} %bitcast.403, bf16[1,200,6,6]{3,2,1,0:T(8,128)(2,1)S(1)} %get-tuple-element.150, bf16[1,200,6,128]{3,2,1,0:T(8,128)(2,1)S(1)} %multiply_convert_fusion.3, f32[200]{0:T(256)S(1)} %bitcast.405, f32[200]{0:T(256)S(1)} %bitcast.407, ...), kind=kLoop, calls=%fused_computation.315 | loop fusion | flops 31026432 | bytes 10267072 | tf_op jit(solution)/shard_map/reduce_sum | solution.py:139
  69.3 2.2 multiply_convert_fusion
  71.5 2.7 convert_reduce_fusion.1
  79.1 2.7 multiply_reduce_fusion
  81.8 3.2 convert_reduce_fusion
  85.1 16.3 %fusion.83 = (f32[200]{0:T(256)S(1)}, f32[200]{0:T(256)S(1)}, f32[200]{0:T(256)S(1)}, f32[200]{0:T(256)S(1)}, f32[200]{0:T(256)S(1)}, /*index=5*/f32[200]{0:T(25...) fusion(bf16[1,200,6,128]{3,2,1,0:T(8,128)(2,1)S(1)} %get-tuple-, ...), kind=kLoop, calls=%fused_computation.217 | loop fusion | flops 6602000 | bytes 4619200 | tf_op jit(solution)/shard_map/tcrw,tcrw->c/dot_general | solution.py:196
  101.5 10.2 %fusion.62 = (f32[200]{0:T(256)S(1)}, f32[200]{0:T(256)S(1)}, f32[200]{0:T(256)S(1)}, f32[200]{0:T(256)S(1)}, f32[200]{0:T(256)S(1)}, /*index=5*/f32[200]{0:T(25...) fusion(bf16[1,200,6,128]{3,2,1,0:T(8,128)(2,1)S(1)} %get-tuple-, ...), kind=kLoop, calls=%fused_computation.196 | loop fusion | flops 6602000 | bytes 4619200 | tf_op jit(solution)/shard_map/tcrw,tcrw->c/dot_general | solution.py:196
  111.8 4.9 fusion.69
  116.7 5.5 fusion.48
  122.3 6.5 %convert_multiply_fusion.12 = (f32[1,200,6,128]{3,2,1,0:T(8,128)S(1)}, f32[1,200,6,128]{3,2,1,0:T(8,128)}, f32[1,200,6,128]{3,2,1,0:T(8,128)}, f32[1,200,6,128]{...) fusion(bf16[1,200,6,128]{3,2,1,0:T(8,128)(2,1)S(1)} %get-tuple-, ...), kind=kLoop, calls=%fused_computation.13 | loop fusion | flops 2150400 | bytes 8304800 | tf_op jit(solution)/shard_map/transpose(jvp())/mul | solution.py:48
  128.9 9.4 %convert_multiply_fusion.30 = (f32[1,200,6,128]{3,2,1,0:T(8,128)}, f32[1,200,6,128]{3,2,1,0:T(8,128)}, f32[1,200,6,128]{3,2,1,0:T(8,128)}, f32[1,200,6,128]{3,2,...) fusion(bf16[1,200,6,128]{3,2,1,0:T(8,128)(2,1)S(1)} %get-tuple-, ...), kind=kLoop, calls=%fused_computation.31 | loop fusion | flops 2918400 | bytes 11380800 | tf_op jit(solution)/shard_map/transpose(jvp())/mul | solution.py:48
  138.5 8.7 %convert_multiply_fusion.48 = (f32[1,200,6,128]{3,2,1,0:T(8,128)}, f32[1,200,6,128]{3,2,1,0:T(8,128)}, f32[1,200,6,128]{3,2,1,0:T(8,128)}, f32[1,200,6,128]{3,2,...) fusion(bf16[1,200,6,128]{3,2,1,0:T(8,128)(2,1)S(1)} %get-tuple-, ...), kind=kLoop, calls=%fused_computation.49 | loop fusion | flops 2918400 | bytes 11380800 | tf_op jit(solution)/shard_map/transpose(jvp())/mul | solution.py:48
  150.0 5.8 %fusion.90 = (f32[200]{0:T(256)S(1)}, f32[200]{0:T(256)S(1)}, f32[200]{0:T(256)S(1)}, f32[200]{0:T(256)S(1)}, f32[200]{0:T(256)S(1)}, /*index=5*/f32[200]{0:T(256)S(1)}, f32[200]{0:T(256)S(1)}, f32[200]{0:T(256)S(1)}) fusion(bf16[1,200,6,128]{3,2,1,0:T(8,128)(2,1)S(1)} %get-tuple-element.79, bf16[1,200,6,6]{3,2,1,0:T(8,128)(2,1)S(1)} %copy-done.9, ...), kind=kLoop, calls=%fused_computation.224 | loop fusion | flops 7985600 | bytes 958336 | tf_op jit(solution)/shard_map/tcrw,tcrw->c/dot_general | solution.py:196
  156.0 77.8 %all-reduce.55 = (f32[200,49]{0,1:T(8,128)S(1)}, f32[200]{0:T(256)S(1)}, f32[200]{0:T(256)S(1)}, f32[200]{0:T(256)S(1)}, f32[800]{0:T(1024)S(1)}, /*index=5*/f32[200]{0:T(256)S(1)}) all-reduce(f32[200,49]{0,1:T(8,128)S(1)} %stack.199, f32[200]{0:T(256)S(1)} %get-tuple-element.78, ...), channel_id=1, replica_groups=mesh['tiles'=64,'rep'=4] {'tiles','rep'}, use_global_device_ids=true, to_apply=%region_4.5 | all-reduce | flops 11400 | bytes 91200 | tf_op jit(solution)/shard_map/psum | solution.py:236
  235.0 43.8 %pad_add_fusion = f32[1,200,18,140]{3,2,1,0:T(8,128)S(1)} fusion(f32[1,200,6,128]{3,2,1,0:T(8,128)} %get-tuple-element.144, f32[1,200,6,128]{3,2,1,0:T(8,128)} %get-tuple-element.143, f32[1,200,6,128]{3,2,1,0:T(8,128)} %get-tuple-element.142, f32[1,200,6,128]{3,2,1,0:T(8,128)} %get-tuple-element.141, f32[1,200,6,128]{3,2,1,0:T(8,128)} %get-tuple-element.140, ...), kind=kLoop, calls=%fused_computation.99 | loop fusion | flops 24192000 | bytes 32121600 | tf_op jit(solution)/shard_map/transpose(jvp())/add_any | solution.py:39
  284.8 2.4 collective-permute-start.3
  288.4 2.6 fusion.11
  290.9 5.4 collective-permute-done.3
  296.3 2.6 fusion.102
  300.1 246.2 %all-reduce.59.cloned.1.call-done = (f32[200,800]{1,0:T(8,128)}, f32[800,200]{0,1:T(8,128)}) async-done(((f32[200,800]{1,0:T(8,128)}, f32[800,200]{0,1:T(8,128)}), (f32[200,800]{1,0:T(8,128)}, f32[800,200]{0,1:T(8,128)})) %all-reduce.59.cloned.1.call-update) | async-done | bytes 1280016 | tf_op jit(solution)/shard_map/psum | solution.py:236
  (235 shorter events, 35.5 us)
Async XLA Ops:
  7.2 62.1 %copy-start = (bf16[200,800]{1,0:T(8,128)(2,1)S(1)}, bf16[200,800]{1,0:T(8,128)(2,1)}, u32[]{:S(2)}) copy-start(bf16[200,800]{1,0:T(8,128)(2,1)} %param.19) | copy-start | bytes 960004
  7.2 539.1 %all-reduce.59.cloned.1.call-start = ((), (), s32[]{:S(2)}) async-start(), calls=%async_computation | async-start | bytes 2867200 | tf_op jit(solution)/shard_map/psum | solution.py:236
  10.2 31.7 %copy-start.4 = (bf16[1,200,6,128]{3,2,1,0:T(8,128)(2,1)}, bf16[1,200,6,128]{3,2,1,0:T(8,128)(2,1)S(1)}, u32[]{:S(2)}) copy-start(bf16[1,200,6,128]{3,2,1,0:T(8,128)(2,1)S(1)} %broadcast_multiply_fusion.2) | copy-start | bytes 921604
  10.2 26.4 %collective-permute-start.1 = (bf16[1,200,6,128]{3,2,1,0:T(8,128)(2,1)S(1)}, bf16[1,200,6,128]{3,2,1,0:T(8,128)(2,1)S(1)}, u32[]{:S(2)}, u32[]{:S(2)}) collective-permute-start(bf16[1,200,6,128]{3,2,1,0:T(8,128)(2,1)S(1)} %broadcast_multiply_fusion.2), channel_id=1, source_target_pairs={{4,0},{8,4},{12,8},{16,12},{20,16},{24,20},{28,24},{32,28},{36,32}... | collective-permute-start | bytes 921608 | tf_op jit(solution)/shard_map/ppermute | solution.py:16
  17.3 19.7 %collective-permute-start = (bf16[1,200,6,128]{3,2,1,0:T(8,128)(2,1)S(1)}, bf16[1,200,6,128]{3,2,1,0:T(8,128)(2,1)S(1)}, u32[]{:S(2)}, u32[]{:S(2)}) collective-permute-start(bf16[1,200,6,128]{3,2,1,0:T(8,128)(2,1)S(1)} %broadcast_multiply_fusion.2), channel_id=1, source_target_pairs={{0,4},{4,8},{8,12},{12,16},{16,20},{20,24},{24,28},{28,32},{32,36}... | collective-permute-start | bytes 921608 | tf_op jit(solution)/shard_map/ppermute | solution.py:16
  20.1 21.8 %copy-start.29 = (f32[200,1]{0,1:T(1,128)}, f32[200,1]{0,1:T(1,128)S(1)}, u32[]{:S(2)}) copy-start(f32[200,1]{0,1:T(1,128)S(1)} %get-tuple-element.198) | copy-start | bytes 2404
  20.2 21.8 %copy-start.31 = (f32[200,1]{0,1:T(1,128)}, f32[200,1]{0,1:T(1,128)S(1)}, u32[]{:S(2)}) copy-start(f32[200,1]{0,1:T(1,128)S(1)} %get-tuple-element.199) | copy-start | bytes 2404
  20.2 21.8 %copy-start.69 = (f32[200,1]{0,1:T(1,128)}, f32[200,1]{0,1:T(1,128)S(1)}, u32[]{:S(2)}) copy-start(f32[200,1]{0,1:T(1,128)S(1)} %get-tuple-element.189) | copy-start | bytes 2404
  20.2 21.8 %copy-start.71 = (f32[200,1]{0,1:T(1,128)}, f32[200,1]{0,1:T(1,128)S(1)}, u32[]{:S(2)}) copy-start(f32[200,1]{0,1:T(1,128)S(1)} %get-tuple-element.190) | copy-start | bytes 2404
  20.2 21.8 %copy-start.73 = (f32[200,1]{0,1:T(1,128)}, f32[200,1]{0,1:T(1,128)S(1)}, u32[]{:S(2)}) copy-start(f32[200,1]{0,1:T(1,128)S(1)} %get-tuple-element.191) | copy-start | bytes 2404
  20.2 21.8 %copy-start.75 = (f32[200,1]{0,1:T(1,128)}, f32[200,1]{0,1:T(1,128)S(1)}, u32[]{:S(2)}) copy-start(f32[200,1]{0,1:T(1,128)S(1)} %get-tuple-element.192) | copy-start | bytes 2404
  20.2 21.8 %copy-start.77 = (f32[200,1]{0,1:T(1,128)}, f32[200,1]{0,1:T(1,128)S(1)}, u32[]{:S(2)}) copy-start(f32[200,1]{0,1:T(1,128)S(1)} %get-tuple-element.193) | copy-start | bytes 2404
  20.2 21.8 %copy-start.79 = (f32[200,1]{0,1:T(1,128)}, f32[200,1]{0,1:T(1,128)S(1)}, u32[]{:S(2)}) copy-start(f32[200,1]{0,1:T(1,128)S(1)} %get-tuple-element.194) | copy-start | bytes 2404
  20.2 21.8 %copy-start.81 = (f32[200,1]{0,1:T(1,128)}, f32[200,1]{0,1:T(1,128)S(1)}, u32[]{:S(2)}) copy-start(f32[200,1]{0,1:T(1,128)S(1)} %get-tuple-element.195) | copy-start | bytes 2404
  20.2 21.8 %copy-start.83 = (f32[200,1]{0,1:T(1,128)}, f32[200,1]{0,1:T(1,128)S(1)}, u32[]{:S(2)}) copy-start(f32[200,1]{0,1:T(1,128)S(1)} %get-tuple-element.196) | copy-start | bytes 2404
  20.2 21.8 %copy-start.85 = (f32[200,1]{0,1:T(1,128)}, f32[200,1]{0,1:T(1,128)S(1)}, u32[]{:S(2)}) copy-start(f32[200,1]{0,1:T(1,128)S(1)} %get-tuple-element.197) | copy-start | bytes 2404
  41.9 26.6 %copy-start.2 = (bf16[1,200,12,140]{3,2,1,0:T(8,128)(2,1)}, bf16[1,200,12,140]{3,2,1,0:T(8,128)(2,1)S(1)}, u32[]{:S(2)}) copy-start(bf16[1,200,12,140]{3,2,1,0:T(8,128)(2,1)S(1)} %get-tuple-element.95) | copy-start | bytes 2016004
  42.3 26.5 %copy-start.27 = (f32[200]{0:T(256)S(1)}, f32[200]{0:T(256)}, u32[]{:S(2)}) copy-start(f32[200]{0:T(256)} %param.17) | copy-start | bytes 2404
  42.3 26.5 %copy-start.91 = (f32[200]{0:T(256)S(1)}, f32[200]{0:T(256)}, u32[]{:S(2)}) copy-start(f32[200]{0:T(256)} %param.18) | copy-start | bytes 2404
  42.3 27.0 %copy-start.93 = (f32[800]{0:T(1024)S(1)}, f32[800]{0:T(1024)}, u32[]{:S(2)}) copy-start(f32[800]{0:T(1024)} %param.20) | copy-start | bytes 9604
  101.4 20.8 %copy-start.70 = (f32[200,1]{0,1:T(1,128)S(1)}, f32[200,1]{0,1:T(1,128)}, u32[]{:S(2)}) copy-start(f32[200,1]{0,1:T(1,128)} %copy-done.69) | copy-start | bytes 2404
  282.7 8.2 %collective-permute-start.2 = (bf16[1,200,6,128]{3,2,1,0:T(8,128)(2,1)}, bf16[1,200,6,128]{3,2,1,0:T(8,128)(2,1)S(1)}, u32[]{:S(2)}, u32[]{:S(2)}) collective-permute-start(bf16[1,200,6,128]{3,2,1,0:T(8,128)(2,1)} %get-tuple-element.92), channel_id=1, source_target_pairs={{4,0},{8,4},{12,8},{16,12},{20,16},{24,20},{28,24},{32,28},{36,32}... | collective-permute-start | bytes 921608 | tf_op jit(solution)/shard_map/ppermute | solution.py:16
  284.8 11.6 %collective-permute-start.3 = (bf16[1,200,6,128]{3,2,1,0:T(8,128)(2,1)S(1)}, bf16[1,200,6,128]{3,2,1,0:T(8,128)(2,1)}, u32[]{:S(2)}, u32[]{:S(2)}) collective-permute-start(bf16[1,200,6,128]{3,2,1,0:T(8,128)(2,1)S(1)} %get-tuple-element.93), channel_id=1, source_target_pairs={{0,4},{4,8},{8,12},{12,16},{16,20},{20,24},{24,28},{28,32},{32,36}... | collective-permute-start | bytes 921608 | tf_op jit(solution)/shard_map/ppermute | solution.py:16
  296.3 254.0 %copy-start.1 = (bf16[200,800]{1,0:T(8,128)(2,1)S(1)}, bf16[200,800]{1,0:T(8,128)(2,1)}, u32[]{:S(2)}) copy-start(bf16[200,800]{1,0:T(8,128)(2,1)} %param.19) | copy-start | bytes 960004
  (76 other events, 956.7 us)
Sparse Core Ops, SparseCore 0:
  287.3 258.9 all-reduce.58
where the time goes:
time: 561 us; the launch traced here: 557 us
  waiting for transfers between devices  252 us (45%)
  other arithmetic  164 us (29%)
  blocking collectives  77.8 us (14%)
  between operations  21 us (4%)
  local copies, waits for them, and re-layouts  17.4 us (3%)
  starting transfers between devices  13.5 us (2%)
  matrix products  11.7 us (2%)
    psum x1, waiting for transfers between devices, body(): lax.psum((grad_kernel, grad_conv_bias, grad_gain, grad_shift, grad_in_wei...  246 us
    psum x1, blocking collectives, body(): lax.psum((grad_kernel, grad_conv_bias, grad_gain, grad_shift, grad_in_wei...  77.8 us
    add_any x1, other arithmetic, taps_sum(): padded_field[:, :, KERNEL_DILATION * first_operand:KERNEL_DILATION * firs...  43.8 us
    dot_general x5, other arithmetic, body(): jnp.einsum('tcrw,tcrw->c', conv_grad, kernel_window, preferred_element_ty...  42.7 us
    reduce_sum x1, other arithmetic, body(): centred = convolved - jnp.mean(convolved, axis=1, keepdims=True)  26.2 us
    mul x3, other arithmetic, taps_sum(): kernel_window * kernel[:, 7 * first_operand + second_operand][None, :, No...  24.5 us
    ppermute x4, starting transfers between devices, shifted(): lax.ppermute(value, axis, [(source, source + steps) for source in range(i...  13.5 us
  transfers between devices with their start and end apart: 5, of which 2 were waited for; matrix products, arithmetic and copies ran while one was open for 4% of the time, Pallas kernels for 0%

commit v1 on v0

v1 whole, which is shorter than its diff:
```python
import jax
import jax.numpy as jnp
from jax import lax
from jax.experimental import pallas as pl
from jax.experimental.pallas import tpu as pltpu
from jax.sharding import Mesh, PartitionSpec as P

C = 200
CX = 208
HID = 800
ROWS = 6
COLS = 128
CELLS = 768
WORDS = 5
BITS = 30
GROUPS = C // 8
IN_BLOCKS = 7
OUT_BASE = IN_BLOCKS * CX
PACK = 3072
SMALL = C - 128
BIAS_LANES = 49

bf16 = jnp.bfloat16
f32 = jnp.float32
gelu_scale = 0.7978845608028654
VMEM = pl.BlockSpec(memory_space=pltpu.VMEM)
SMEM = pl.BlockSpec(memory_space=pltpu.SMEM)
NT_DIMS = (((1,), (1,)), ((), ()))


def row_class(row):
    return row // ROWS


def lanes(r):
    return slice(r * COLS, (r + 1) * COLS)


def wet_row(bits_ref, r):
    col = lax.broadcasted_iota(jnp.int32, (8, COLS), 1)
    word = jnp.zeros((8, COLS), jnp.int32)
    shift = col
    for w in range(WORDS):
        word = jnp.where(col >= BITS * w, bits_ref[r, w], word)
        shift = jnp.where(col >= BITS * w, col - BITS * w, shift)
    return jnp.bitwise_and(jnp.right_shift(word, shift), 1).astype(f32)


def mask_kernel(bits_ref, fields_ref, masked_ref, wet_ref):
    for r in range(ROWS):
        wet = wet_row(bits_ref, r)
        wet_ref[:, lanes(r)] = wet
        masked_ref[:, lanes(r)] = (fields_ref[:, lanes(r)].astype(f32) * wet[0:1]).astype(bf16)


def fill_masks(slot_ref, near_ref, masks_ref):
    slot = slot_ref[0]

    def flag(k, step):
        return jnp.where(near_ref[0, k] == slot + step, 1.0, 0.0).astype(f32)

    lane = lax.broadcasted_iota(jnp.int32, (8, COLS), 1)
    triples = (
        (flag(0, -1), flag(4, -1), flag(5, -1)),
        (jnp.float32(1.0), flag(2, 0), flag(3, 0)),
        (flag(1, 1), flag(6, 1), flag(7, 1)),
    )
    for cls, (centre, west, east) in enumerate(triples):
        for b in range(7):
            off = 2 * b - 6
            mask = jnp.full((8, COLS), centre, f32)
            if off > 0:
                mask = jnp.where(lane < off, jnp.full((8, COLS), east, f32), mask)
            if off < 0:
                mask = jnp.where(lane >= COLS + off, jnp.full((8, COLS), west, f32), mask)
            masks_ref[7 * cls + b] = mask


def fill_rows(north_ref, own_ref, south_ref, rows_ref):
    for part, ref in enumerate((north_ref, own_ref, south_ref)):
        for r in range(ROWS):
            rows_ref[ROWS * part + r] = ref[:, lanes(r)].astype(f32)


def conv_group(rows, taps, masks_ref, flip):
    total = [None] * ROWS
    for b in range(7):
        off = 2 * b - 6
        masked = [rows[r] * masks_ref[7 * row_class(r) + b] for r in range(3 * ROWS)]
        coef = []
        for a in range(7):
            t = 7 * (6 - a) + (6 - b) if flip else 7 * a + b
            coef.append(jnp.broadcast_to(taps[:, t : t + 1], (8, COLS)))
        for i in range(ROWS):
            acc = coef[0] * masked[i]
            for a in range(1, 7):
                acc = acc + coef[a] * masked[i + 2 * a]
            if off != 0:
                acc = pltpu.roll(acc, (-off) % COLS, 1)
            total[i] = acc if total[i] is None else total[i] + acc
    return total


def main_kernel(
    slot_ref,
    near_ref,
    own_ref,
    north_ref,
    south_ref,
    wet_ref,
    cot_ref,
    kern_ref,
    chan_ref,
    inw_ref,
    inwt_ref,
    outw_ref,
    outwt_ref,
    field_ref,
    cgrad_ref,
    norm_ref,
    act_ref,
    hgrad_ref,
    ograd_ref,
    sums_ref,
    rows_ref,
    masks_ref,
    conv_ref,
    istd_ref,
    hid_ref,
    agrad_ref,
):
    fill_masks(slot_ref, near_ref, masks_ref)
    fill_rows(north_ref, own_ref, south_ref, rows_ref)

    osum = jnp.zeros((C, COLS), f32)
    for r in range(ROWS):
        og = cot_ref[:, lanes(r)].astype(f32) * wet_ref[0:1, lanes(r)]
        osum = osum + og
        ograd_ref[:, lanes(r)] = jnp.concatenate([og, jnp.zeros((256 - C, COLS), f32)], axis=0).astype(bf16)
    sums_ref[3] = osum
    agrad_ref[...] = jnp.dot(outw_ref[...], ograd_ref[0:C, :], preferred_element_type=f32)

    def conv_step(g, carry):
        start = pl.multiple_of(g * 8, 8)
        rows = [rows_ref[r, pl.ds(start, 8), :] for r in range(3 * ROWS)]
        taps = kern_ref[pl.ds(start, 8), :]
        total = conv_group(rows, taps, masks_ref, False)
        bias = jnp.broadcast_to(chan_ref[pl.ds(start, 8), 0:1], (8, COLS))
        for i in range(ROWS):
            conv_ref[pl.ds(start, 8), lanes(i)] = total[i] + bias
        return carry

    lax.fori_loop(0, GROUPS, conv_step, 0)

    gain = chan_ref[:, 1:2]
    shift = chan_ref[:, 2:3]
    obias = chan_ref[:, 3:4]
    extra = lax.broadcasted_iota(jnp.int32, (8, COLS), 0)
    extra = jnp.where(extra < 2, 1.0, 0.0).astype(f32)
    for r in range(ROWS):
        x = conv_ref[:, lanes(r)]
        mean = jnp.sum(x, axis=0, keepdims=True) * (1.0 / C)
        x = x - mean
        var = jnp.sum(x * x, axis=0, keepdims=True) * (1.0 / C)
        istd = lax.rsqrt(var + 1e-06)
        normed = x * istd
        conv_ref[:, lanes(r)] = normed
        istd_ref[:, lanes(r)] = jnp.broadcast_to(istd, (8, COLS))
        no = jnp.concatenate([normed * gain + shift, extra], axis=0)
        norm_ref[:, lanes(r)] = no.astype(bf16)

    hid_ref[...] = jnp.dot(inwt_ref[...], norm_ref[...], preferred_element_type=f32)

    def gelu_step(i, carry):
        at = pl.ds(pl.multiple_of(i * 16, 16), 16)
        h = hid_ref[at, :]
        h2 = h * h
        t = jnp.tanh(h * (gelu_scale + (gelu_scale * 0.044715) * h2))
        half = 0.5 + 0.5 * t
        act_ref[at, :] = (h * half).astype(bf16)
        slope = (0.5 * gelu_scale) + (0.5 * gelu_scale * 3.0 * 0.044715) * h2
        deriv = half + h * (1.0 - t * t) * slope
        hgrad_ref[at, :] = (agrad_ref[at, :] * deriv).astype(bf16)
        return carry

    lax.fori_loop(0, HID // 16, gelu_step, 0)

    hid_ref[0:C, :] = jnp.dot(outwt_ref[...], act_ref[...], preferred_element_type=f32)
    agrad_ref[0:C, :] = jnp.dot(inw_ref[...], hgrad_ref[...], preferred_element_type=f32)

    gsum = jnp.zeros((C, COLS), f32)
    ssum = jnp.zeros((C, COLS), f32)
    bsum = jnp.zeros((C, COLS), f32)
    for r in range(ROWS):
        wet = wet_ref[0:1, lanes(r)]
        update = hid_ref[0:C, lanes(r)] + obias
        field_ref[:, lanes(r)] = (wet * (own_ref[:, lanes(r)].astype(f32) + update)).astype(bf16)
        ng = agrad_ref[0:C, lanes(r)]
        normed = conv_ref[:, lanes(r)]
        ssum = ssum + ng
        gsum = gsum + ng * normed
        scaled = ng * gain
        m1 = jnp.sum(scaled, axis=0, keepdims=True) * (1.0 / C)
        m2 = jnp.sum(scaled * normed, axis=0, keepdims=True) * (1.0 / C)
        cg = (istd_ref[0:1, lanes(r)] * (scaled - m1 - normed * m2)).astype(bf16)
        cgrad_ref[:, lanes(r)] = cg
        bsum = bsum + cg.astype(f32)
    sums_ref[0] = bsum
    sums_ref[1] = gsum
    sums_ref[2] = ssum


def grads_kernel(
    slot_ref,
    near_ref,
    own_ref,
    north_ref,
    south_ref,
    cgrad_ref,
    norm_ref,
    act_ref,
    hgrad_ref,
    ograd_ref,
    sums_ref,
    pack_ref,
    rows_ref,
    masks_ref,
    small_ref,
):
    fill_masks(slot_ref, near_ref, masks_ref)
    fill_rows(north_ref, own_ref, south_ref, rows_ref)
    cg_base = 3 * ROWS
    for r in range(ROWS):
        rows_ref[cg_base + r] = cgrad_ref[:, lanes(r)].astype(f32)

    def tap_step(g, carry):
        start = pl.multiple_of(g * 8, 8)
        at = pl.ds(start, 8)
        lane = lax.broadcasted_iota(jnp.int32, (8, COLS), 1)
        small = jnp.zeros((8, COLS), f32)
        for b in range(7):
            off = 2 * b - 6
            acc = [None] * 7
            for i in range(ROWS):
                turned = rows_ref[cg_base + i, at, :]
                if off != 0:
                    turned = pltpu.roll(turned, off % COLS, 1)
                parts = [turned * masks_ref[7 * cls + b] for cls in range(3)]
                for a in range(7):
                    r = i + 2 * a
                    term = parts[row_class(r)] * rows_ref[r, at, :]
                    acc[a] = term if acc[a] is None else acc[a] + term
            for a in range(7):
                value = jnp.sum(acc[a], axis=1, keepdims=True)
                small = jnp.where(lane == SMALL + 7 * a + b, value, small)
        for s in range(4):
            value = jnp.sum(sums_ref[s, at, :], axis=1, keepdims=True)
            small = jnp.where(lane == SMALL + BIAS_LANES + s, value, small)
        small_ref[at, :] = small
        return carry

    lax.fori_loop(0, GROUPS, tap_step, 0)

    for blk in range(IN_BLOCKS):
        first, last = blk * COLS, min((blk + 1) * COLS, HID)
        part = lax.dot_general(norm_ref[...], hgrad_ref[first:last, :], NT_DIMS, preferred_element_type=f32)
        if last - first < COLS:
            part = jnp.concatenate([part, jnp.zeros((CX, COLS - (last - first)), f32)], axis=1)
        pack_ref[blk * CX : (blk + 1) * CX, :] = part.astype(bf16)
    whole = lax.dot_general(act_ref[...], ograd_ref[...], NT_DIMS, preferred_element_type=f32)
    pack_ref[OUT_BASE : OUT_BASE + HID, :] = whole[:, 0:COLS].astype(bf16)
    second = OUT_BASE + HID
    small = jnp.concatenate([small_ref[...], jnp.zeros((8, COLS), f32)], axis=0)
    pack_ref[second : second + CX, :] = (whole[0:CX, COLS:] + small).astype(bf16)
    pack_ref[second + CX : second + HID, :] = whole[CX:, COLS:].astype(bf16)
    pack_ref[second + HID :, :] = jnp.zeros((PACK - second - HID, COLS), bf16)


def back_kernel(
    slot_ref,
    near_ref,
    own_ref,
    north_ref,
    south_ref,
    wet_ref,
    cot_ref,
    kern_ref,
    igrad_ref,
    rows_ref,
    masks_ref,
    conv_ref,
):
    fill_masks(slot_ref, near_ref, masks_ref)
    fill_rows(north_ref, own_ref, south_ref, rows_ref)

    def conv_step(g, carry):
        start = pl.multiple_of(g * 8, 8)
        rows = [rows_ref[r, pl.ds(start, 8), :] for r in range(3 * ROWS)]
        taps = kern_ref[pl.ds(start, 8), :]
        total = conv_group(rows, taps, masks_ref, True)
        for i in range(ROWS):
            conv_ref[pl.ds(start, 8), lanes(i)] = total[i]
        return carry

    lax.fori_loop(0, GROUPS, conv_step, 0)
    for r in range(ROWS):
        wet = wet_ref[0:1, lanes(r)]
        og = cot_ref[:, lanes(r)].astype(f32) * wet
        igrad_ref[:, lanes(r)] = (wet * (og + conv_ref[:, lanes(r)])).astype(bf16)


def unpack_kernel(factor, core_ref, mine_ref, other_ref, gin_ref, gout_ref, gsmall_ref, gvec_ref, full_ref):
    half = PACK // 2
    first = core_ref[0] == 0

    @pl.when(first)
    def _():
        full_ref[0:half, :] = mine_ref[...].astype(f32) * factor
        full_ref[half:, :] = other_ref[...].astype(f32) * factor

    @pl.when(jnp.logical_not(first))
    def _():
        full_ref[0:half, :] = other_ref[...].astype(f32) * factor
        full_ref[half:, :] = mine_ref[...].astype(f32) * factor

    for blk in range(IN_BLOCKS):
        begin, end = blk * COLS, min((blk + 1) * COLS, HID)
        gin_ref[:, begin:end] = full_ref[blk * CX : blk * CX + C, 0 : end - begin]
        gvec_ref[4:5, begin:end] = full_ref[blk * CX + C : blk * CX + C + 1, 0 : end - begin]
    second = OUT_BASE + HID
    gout_ref[:, 0:COLS] = full_ref[OUT_BASE:second, :]
    gout_ref[:, COLS:C] = full_ref[second : second + HID, 0:SMALL]
    gsmall_ref[...] = full_ref[second : second + C, SMALL : SMALL + 49]
    columns = full_ref[second : second + C, :].T
    gvec_ref[0:4, 0:C] = columns[SMALL + BIAS_LANES : SMALL + BIAS_LANES + 4, :]


def call(kernel, outs, n_smem, n_in, scratch=(), flops=0, name=None):
    return pl.pallas_call(
        kernel,
        out_shape=[jax.ShapeDtypeStruct(s, d) for s, d in outs],
        in_specs=[SMEM] * n_smem + [VMEM] * (n_in - n_smem),
        out_specs=[VMEM] * len(outs),
        scratch_shapes=[pltpu.VMEM(s, d) for s, d in scratch],
        cost_estimate=pl.CostEstimate(flops=flops, bytes_accessed=4000000, transcendentals=0),
        name=name,
    )


TILE_AXES = ("y", "z", "core")
PLANE = ("y", "rep")


def shifted(value, steps):
    count = lax.axis_size(TILE_AXES)
    first, last = max(0, -steps), min(count, count - steps)
    return lax.ppermute(value, TILE_AXES, [(s, s + steps) for s in range(first, last)])


def exchange(value, axes):
    return lax.all_to_all(value, axes, 0, 0, tiled=True)


def spread(value, axes):
    count = lax.axis_size(axes)
    rows = value.shape[0]
    return exchange(jnp.broadcast_to(value[None], (count, rows, COLS)).reshape(count * rows, COLS), axes)


def summed(value, count):
    rows = value.shape[0] // count
    return jnp.sum(value.reshape(count, rows, COLS).astype(f32), axis=0).astype(bf16)


def reduce_pack(pack, core):
    half = PACK // 2
    swap = [(0, 1), (1, 0)]
    mine = lax.dynamic_slice_in_dim(pack, core * half, half, 0)
    other = lax.dynamic_slice_in_dim(pack, (1 - core) * half, half, 0)
    got = lax.ppermute(other, "core", swap)
    pair = (mine.astype(f32) + got.astype(f32)).astype(bf16)
    count = lax.axis_size(PLANE)
    part = summed(exchange(pair, PLANE), count)
    part = summed(spread(part, "z"), lax.axis_size("z"))
    mine = spread(part, PLANE)
    return mine, lax.ppermute(mine, "core", swap)


def body(
    fields,
    wet_bits,
    neighbours,
    kernel,
    conv_bias,
    ln_gain,
    ln_shift,
    in_weight,
    in_bias,
    out_weight,
    out_bias,
    cotangent,
):
    act2 = (C, CELLS)
    slot = lax.axis_index(TILE_AXES).astype(jnp.int32).reshape(1)
    core = lax.axis_index("core").astype(jnp.int32)
    cot = cotangent.reshape(act2)
    masked, wet = call(mask_kernel, [(act2, bf16), ((8, CELLS), f32)], 1, 2, name="mask")(
        wet_bits.reshape(ROWS, WORDS), fields.reshape(act2)
    )
    from_north = shifted(masked, 1)
    from_south = shifted(masked, -1)
    chan = jnp.stack([conv_bias, ln_gain, ln_shift, out_bias], axis=1)
    high = lax.reduce_precision(in_bias, 8, 7)
    bias_rows = jnp.stack([high, in_bias - high]).astype(bf16)
    inwt = jnp.concatenate([in_weight, bias_rows, jnp.zeros((CX - C - 2, HID), bf16)], axis=0).T
    field, cgrad, norm, act, hgrad, ograd, sums = call(
        main_kernel,
        [
            (act2, bf16),
            (act2, bf16),
            ((CX, CELLS), bf16),
            ((HID, CELLS), bf16),
            ((HID, CELLS), bf16),
            ((256, CELLS), bf16),
            ((4, C, COLS), f32),
        ],
        2,
        13,
        [
            ((3 * ROWS, C, COLS), f32),
            ((21, 8, COLS), f32),
            (act2, f32),
            ((8, CELLS), f32),
            ((HID, CELLS), f32),
            ((HID, CELLS), f32),
        ],
        flops=10**10,
        name="main",
    )(
        slot,
        neighbours,
        masked,
        from_north,
        from_south,
        wet,
        cot,
        kernel,
        chan,
        in_weight,
        inwt,
        out_weight,
        out_weight.T,
    )
    cg_north = shifted(cgrad, 1)
    cg_south = shifted(cgrad, -1)
    (pack,) = call(
        grads_kernel,
        [((PACK, COLS), bf16)],
        2,
        11,
        [((4 * ROWS, C, COLS), f32), ((21, 8, COLS), f32), ((C, COLS), f32)],
        flops=5 * 10**9,
        name="grads",
    )(slot, neighbours, masked, from_north, from_south, cgrad, norm, act, hgrad, ograd, sums)
    (input_grad,) = call(
        back_kernel,
        [(act2, bf16)],
        2,
        8,
        [((3 * ROWS, C, COLS), f32), ((21, 8, COLS), f32), (act2, f32)],
        flops=3 * 10**9,
        name="back",
    )(slot, neighbours, cgrad, cg_north, cg_south, wet, cot, kernel)
    mine, other = reduce_pack(pack, core)
    total_cells = lax.axis_size(TILE_AXES) * lax.axis_size("rep") * CELLS
    factor = float(total_cells) ** -0.5
    gin, gout, gsmall, gvec = call(
        lambda *refs: unpack_kernel(factor, *refs),
        [((C, HID), f32), ((HID, C), f32), ((C, 49), f32), ((8, HID), f32)],
        1,
        3,
        [((PACK, COLS), f32)],
        flops=10**8,
        name="unpack",
    )(core.reshape(1), mine, other)
    return (
        field.reshape(1, 1, C, CELLS),
        input_grad.reshape(1, 1, C, CELLS),
        gsmall,
        gvec[0, 0:C],
        gvec[1, 0:C],
        gvec[2, 0:C],
        gin,
        gvec[4],
        gout,
        gvec[3, 0:C],
    )


def solution(mesh):
    rep = mesh.shape["rep"]
    fine = Mesh(mesh.devices.reshape(4, -1, 2, rep), ("y", "z", "core", "rep"))
    tile = P("rep", TILE_AXES, None, None)
    placed = (tile, P(TILE_AXES, None, None), P(TILE_AXES, None)) + (P(),) * 8 + (tile,)
    return jax.shard_map(
        body,
        mesh=fine,
        in_specs=placed,
        out_specs=(tile, tile) + (P(),) * 8,
        check_vma=False,
    )
```

time: 561 us -> 118 us (0.21)
  waiting for transfers between devices: 252 us -> 5.94 us
  other arithmetic: 164 us -> 2.88 us
  blocking collectives: 77.8 us -> 31 us
  Pallas kernels: 0 us -> 38.9 us
  between operations: 21 us -> 0.84 us
  matrix products: 11.7 us -> 0 us
  starting transfers between devices: 13.5 us -> 22.7 us
    psum x1 -> x0, waiting for transfers between devices: 246 us -> none  [body(): lax.psum((grad_kernel, grad_conv_bias, grad_gain, grad_shift, grad_in_wei...]
    psum x1 -> x0, blocking collectives: 77.8 us -> none  [body(): lax.psum((grad_kernel, grad_conv_bias, grad_gain, grad_shift, grad_in_wei...]
    add_any x1 -> x0, other arithmetic: 43.8 us -> none  [taps_sum(): padded_field[:, :, KERNEL_DILATION * first_operand:KERNEL_DILATION * firs...]
    dot_general x6 -> x0, other arithmetic: 43.6 us -> none  [the longest x5 42.7 us: body(): jnp.einsum('tcrw,tcrw->c', conv_grad, kernel_window, preferred_element_ty...]
    pallas_call x0 -> x5, Pallas kernels: none -> 38.9 us  [the longest x1 14.1 us: body(): call(grads_kernel, [((PACK, COLS), bf16)], 2, 11, [((4 * ROWS, C, COLS),...]
    reduce_sum x6 -> x2, other arithmetic: 35.2 us -> 0.09 us  [summed(): jnp.sum(value.reshape(count, rows, COLS).astype(f32), axis=0).astype(bf16)]
    all_to_all x0 -> x2, blocking collectives: none -> 31 us  [exchange(): return lax.all_to_all(value, axes, 0, 0, tiled=True)]
    mul x10 -> x0, other arithmetic: 30.9 us -> none  [the longest x3 24.5 us: taps_sum(): kernel_window * kernel[:, 7 * first_operand + second_operand][None, :, No...]
  transfers between devices with their start and end apart: 5 -> 7, of which waited for: 2 -> 3; matrix products, arithmetic and copies ran while one was open for 4% -> 5% of each run, Pallas kernels for 0% -> 7%
where the time goes in v1:
time: 118 us
  Pallas kernels  38.9 us (33%)
  blocking collectives  31 us (26%)
  starting transfers between devices  22.7 us (19%)
  local copies, waits for them, and re-layouts  15.4 us (13%)
  waiting for transfers between devices  5.94 us (5%)
  other arithmetic  2.88 us (2%)
    all_to_all x2, blocking collectives, exchange(): return lax.all_to_all(value, axes, 0, 0, tiled=True)  31 us
    ppermute x4, starting transfers between devices, shifted(): lax.ppermute(value, TILE_AXES, [(s, s + steps) for s in range(first, last)])  16.7 us
    pallas_call x1, Pallas kernels, body(): call(grads_kernel, [((PACK, COLS), bf16)], 2, 11, [((4 * ROWS, C, COLS),...  14.1 us
    pallas_call x1, Pallas kernels, body(): call(main_kernel, [(act2, bf16), (act2, bf16), ((CX, CELLS), bf16), ((HID...  12.8 us
    unnamed x34, local copies, waits for them, and re-layouts  9.61 us
    pallas_call x1, Pallas kernels, body(): call(back_kernel, [(act2, bf16)], 2, 8, [((3 * ROWS, C, COLS), f32), ((21...  7.71 us
    all_to_all x1, starting transfers between devices, exchange(): return lax.all_to_all(value, axes, 0, 0, tiled=True)  5.81 us
    ppermute x4, waiting for transfers between devices, shifted(): lax.ppermute(value, TILE_AXES, [(s, s + steps) for s in range(first, last)])  4.23 us
  transfers between devices with their start and end apart: 7, of which 3 were waited for; matrix products, arithmetic and copies ran while one was open for 5% of the time, Pallas kernels for 7%

profile of v1, /device:TPU:8, one launch (start us, length us, event | category | flops | bytes accessed | tf_op | source)
XLA Modules:
  0.0 117.7 jit_solution(18294523114088856571)
XLA Ops:
  0.7 1.4 %copy.52 = s32[1,6,5]{2,1,0:T(8,128)} copy(s32[1,6,5]{1,0,2:T(1,128)} %param.13) | data formatting | bytes 240 | tf_op args[1]
  2.1 1.8 %mask.1 = (bf16[200,768]{1,0:T(8,128)(2,1)}, f32[8,768]{1,0:T(8,128)}) custom-call(s32[6,5]{1,0:T(8,128)} %bitcast.25, bf16[200,768]{1,0:T(8,128)(2,1)} %bitcast.24), custom_call_target="tpu_custom_call" | custom-call | bytes 4000000 | tf_op jit(solution)/shard_map/mask/pallas_call | solution.py:407
  3.9 1.9 %collective-permute-start = (bf16[200,768]{1,0:T(8,128)(2,1)}, bf16[200,768]{1,0:T(8,128)(2,1)S(1)}, u32[]{:S(2)}, u32[]{:S(2)}) collective-permute-start(bf16[200,768]{1,0:T(8,128)(2,1)} %get-tuple-element.23.own_ref), channel_id=1, source_target_pairs={{0,4},{4,8},{8,12},{12,16},{16,20},{20,24},{24,28},{28,32},{32,36}... | collective-permute-start | bytes 921608 | tf_op jit(solution)/shard_map/ppermute | solution.py:357
  5.8 7.1 %collective-permute-start.1 = (bf16[200,768]{1,0:T(8,128)(2,1)}, bf16[200,768]{1,0:T(8,128)(2,1)S(1)}, u32[]{:S(2)}, u32[]{:S(2)}) collective-permute-start(bf16[200,768]{1,0:T(8,128)(2,1)} %get-tuple-element.23.own_ref), channel_id=1, source_target_pairs={{4,0},{8,4},{12,8},{16,12},{20,16},{24,20},{28,24},{32,28},{36,32}... | collective-permute-start | bytes 921608 | tf_op jit(solution)/shard_map/ppermute | solution.py:357
  14.0 1.2 copy.53
  15.9 0.9 copy.58.outw_ref
  17.7 1.0 maximum_bitcast_fusion.inwt_ref
  19.6 12.8 %main.1 = (bf16[200,768]{1,0:T(8,128)(2,1)}, bf16[200,768]{1,0:T(8,128)(2,1)}, bf16[208,768]{1,0:T(8,128)(2,1)}, bf16[800,768]{1,0:T(8,128)(2,1)}, bf16[800,768]...) custom-call(s32[1]{0:T(128)} %bitcast.slot_ref, s32[1,8]{1,0:T(1,128)} %near_ref.5, ...), custom_call_target="tpu_custom_call" | custom-call | flops 10000000000 | bytes 4000000 | tf_op jit(solution)/shard_map/main/pallas_call | solution.py:416
  32.4 14.1 %grads.1 = bf16[3072,128]{1,0:T(8,128)(2,1)} custom-call(s32[1]{0:T(128)} %bitcast.slot_ref, s32[1,8]{1,0:T(1,128)} %near_ref.5, bf16[200,768]{1,0:T(8,128)(2,1)} %get-tuple-element.23.own_ref, bf16[200,768]{1,0:T(8,128)(2,1)} %copy-done.9, bf16[200,768]{1,0:T(8,128)(2,1)} %copy-done.10, bf16[200,768]{1,0:T(8,128)(2,1)} %get-tuple-element.26.own_ref.cgrad_ref, ...), custom_call_target="tpu_custom_call" | custom-call | flops 5000000000 | bytes 4000000 | tf_op jit(solution)/shard_map/grads/pallas_call | solution.py:456
  46.5 1.0 constant_dynamic-slice_fusion
  47.6 1.7 %collective-permute-done.4 = bf16[1536,128]{1,0:T(8,128)(2,1)S(1)} collective-permute-done((bf16[1536,128]{1,0:T(8,128)(2,1)S(1)}, bf16[1536,128]{1,0:T(8,128)(2,1)S(1)}, u32[]{:S(2)}, u32[]{:S(2)}) %collective-permute-start.4) | collective-permute-done | bytes 393248 | tf_op jit(solution)/shard_map/ppermute | solution.py:380
  49.3 1.1 add_convert_fusion
  50.4 15.3 %all_to_all.23 = bf16[16,96,128]{2,1,0:T(8,128)(2,1)S(1)} all-to-all(bf16[16,96,128]{2,1,0:T(8,128)(2,1)S(1)} %bitcast.22), channel_id=1, replica_groups=mesh['y'=4,'z'=8,'core'=2,'rep'=4] {'y','rep'}, dimensions={0} | all-to-all | bytes 786432 | tf_op jit(solution)/shard_map/all_to_all | solution.py:361
  65.9 15.7 %all_to_all.24 = bf16[8,96,128]{2,1,0:T(8,128)(2,1)S(1)} all-to-all(bf16[8,96,128]{2,1,0:T(8,128)(2,1)S(1)} %broadcast_in_dim.7), channel_id=1, replica_groups=mesh['y'=4,'z'=8,'core'=2,'rep'=4] {'z'}, dimensions={0} | all-to-all | bytes 393216 | tf_op jit(solution)/shard_map/all_to_all | solution.py:361
  82.4 5.8 %all-to-all-start.2 = ((bf16[16,96,128]{2,1,0:T(8,128)(2,1)}), bf16[16,96,128]{2,1,0:T(8,128)(2,1)S(1)}, u32[]{:S(2)}, u32[]{:S(2)}) async-start(bf16[16,96,128]{2,1,0:T(8,128)(2,1)} %broadcast_in_dim.8), calls=%async_computation.2 | async-start | bytes 786432 | tf_op jit(solution)/shard_map/all_to_all | solution.py:361
  88.2 1.9 %collective-permute-start.2 = (bf16[200,768]{1,0:T(8,128)(2,1)S(1)}, bf16[200,768]{1,0:T(8,128)(2,1)S(1)}, u32[]{:S(2)}, u32[]{:S(2)}) collective-permute-start(bf16[200,768]{1,0:T(8,128)(2,1)S(1)} %copy-done.11), channel_id=1, source_target_pairs={{0,4},{4,8},{8,12},{12,16},{16,20},{20,24},{24,28},{28,32},{32,36}... | collective-permute-start | bytes 921608 | tf_op jit(solution)/shard_map/ppermute | solution.py:357
  90.1 5.8 %collective-permute-start.3 = (bf16[200,768]{1,0:T(8,128)(2,1)S(1)}, bf16[200,768]{1,0:T(8,128)(2,1)S(1)}, u32[]{:S(2)}, u32[]{:S(2)}) collective-permute-start(bf16[200,768]{1,0:T(8,128)(2,1)S(1)} %copy-done.11), channel_id=1, source_target_pairs={{4,0},{8,4},{12,8},{16,12},{20,16},{24,20},{28,24},{32,28},{36,32}... | collective-permute-start | bytes 921608 | tf_op jit(solution)/shard_map/ppermute | solution.py:357
  96.0 2.5 %collective-permute-done.2.north_ref = bf16[200,768]{1,0:T(8,128)(2,1)S(1)} collective-permute-done((bf16[200,768]{1,0:T(8,128)(2,1)S(1)}, bf16[200,768]{1,0:T(8,128)(2,1)S(1)}, u32[]{:S(2)}, u32[]{:S(2)}) %collective-permute-start.2) | collective-permute-done | bytes 307232 | tf_op jit(solution)/shard_map/ppermute | solution.py:357
  98.5 1.8 %collective-permute-done.3.south_ref = bf16[200,768]{1,0:T(8,128)(2,1)S(1)} collective-permute-done((bf16[200,768]{1,0:T(8,128)(2,1)S(1)}, bf16[200,768]{1,0:T(8,128)(2,1)S(1)}, u32[]{:S(2)}, u32[]{:S(2)}) %collective-permute-start.3) | collective-permute-done | bytes 307232 | tf_op jit(solution)/shard_map/ppermute | solution.py:357
  101.0 7.7 %back.1 = bf16[200,768]{1,0:T(8,128)(2,1)} custom-call(s32[1]{0:T(128)} %bitcast.slot_ref, s32[1,8]{1,0:T(1,128)} %near_ref.5, bf16[200,768]{1,0:T(8,128)(2,1)} %get-tuple-element.26.own_ref.cgrad_ref, bf16[200,768]{1,0:T(8,128)(2,1)} %copy-done.12, bf16[200,768]{1,0:T(8,128)(2,1)} %copy-done.13, f32[8,768]{1,0:T(8,128)} %get-tuple-element.24.wet_ref, ...), custom_call_target="tpu_custom_call" | custom-call | flops 3000000000 | bytes 4000000 | tf_op jit(solution)/shard_map/back/pallas_call | solution.py:465
  109.5 2.5 %unpack.1 = (f32[200,800]{1,0:T(8,128)}, f32[800,200]{1,0:T(8,128)}, f32[200,49]{1,0:T(8,128)}, f32[8,800]{1,0:T(8,128)}) custom-call(s32[1]{0:T(128)} %bitcast.12.refs_0_, bf16[1536,128]{1,0:T(8,128)(2,1)} %bitcast.21, bf16[1536,128]{1,0:T(8,128)(2,1)} %copy-done.1), custom_call_target="tpu_custom_call" | custom-call | flops 100000000 | bytes 4000000 | tf_op jit(solution)/shard_map/unpack/pallas_call | solution.py:477
  111.9 1.4 %fusion.1 = (f32[1,200]{1,0:T(1,128)}, f32[1,200]{1,0:T(1,128)}, f32[1,200]{1,0:T(1,128)}, f32[1,200]{1,0:T(1,128)}) fusion(f32[8,800]{1,0:T(8,128)} %get-tuple-element.33), kind=kLoop, calls=%fused_computation.8 | loop fusion | bytes 6400 | tf_op jit(solution)/shard_map/slice | solution.py:496
  113.4 1.4 %slice_reduce_fusion = f32[800]{0:T(1024)} fusion(f32[8,800]{1,0:T(8,128)} %get-tuple-element.33), kind=kLoop, calls=%fused_computation.6 | loop fusion | bytes 6400 | tf_op jit(solution)/shard_map/slice | solution.py:494
  114.7 2.3 %copy.61 = f32[800,200]{0,1:T(8,128)} copy(f32[800,200]{1,0:T(8,128)} %get-tuple-element.74) | data formatting | bytes 1280000
  (47 shorter events, 6.8 us)
Async XLA Ops:
  0.6 14.5 %copy-start.4 = (f32[200,49]{0,1:T(8,128)S(1)}, f32[200,49]{0,1:T(8,128)}, u32[]{:S(2)}) copy-start(f32[200,49]{0,1:T(8,128)} %param.15) | copy-start | bytes 117604
  0.7 15.3 %copy-start.2 = (bf16[800,200]{0,1:T(8,128)(2,1)S(1)}, bf16[800,200]{0,1:T(8,128)(2,1)}, u32[]{:S(2)}) copy-start(bf16[800,200]{0,1:T(8,128)(2,1)} %param.21) | copy-start | bytes 960004
  2.1 14.8 %copy-start.5 = (f32[200]{0:T(256)S(1)}, f32[200]{0:T(256)}, u32[]{:S(2)}) copy-start(f32[200]{0:T(256)} %param.22) | copy-start | bytes 2404
  2.1 14.8 %copy-start.6 = (f32[200]{0:T(256)S(1)}, f32[200]{0:T(256)}, u32[]{:S(2)}) copy-start(f32[200]{0:T(256)} %param.18) | copy-start | bytes 2404
  2.1 14.8 %copy-start.7 = (f32[200]{0:T(256)S(1)}, f32[200]{0:T(256)}, u32[]{:S(2)}) copy-start(f32[200]{0:T(256)} %param.17) | copy-start | bytes 2404
  2.1 14.8 %copy-start.8 = (f32[200]{0:T(256)S(1)}, f32[200]{0:T(256)}, u32[]{:S(2)}) copy-start(f32[200]{0:T(256)} %param.16) | copy-start | bytes 2404
  3.9 14.8 %collective-permute-start = (bf16[200,768]{1,0:T(8,128)(2,1)}, bf16[200,768]{1,0:T(8,128)(2,1)S(1)}, u32[]{:S(2)}, u32[]{:S(2)}) collective-permute-start(bf16[200,768]{1,0:T(8,128)(2,1)} %get-tuple-element.23.own_ref), channel_id=1, source_target_pairs={{0,4},{4,8},{8,12},{12,16},{16,20},{20,24},{24,28},{28,32},{32,36}... | collective-permute-start | bytes 921608 | tf_op jit(solution)/shard_map/ppermute | solution.py:357
  5.8 12.9 %collective-permute-start.1 = (bf16[200,768]{1,0:T(8,128)(2,1)}, bf16[200,768]{1,0:T(8,128)(2,1)S(1)}, u32[]{:S(2)}, u32[]{:S(2)}) collective-permute-start(bf16[200,768]{1,0:T(8,128)(2,1)} %get-tuple-element.23.own_ref), channel_id=1, source_target_pairs={{4,0},{8,4},{12,8},{16,12},{20,16},{24,20},{28,24},{32,28},{36,32}... | collective-permute-start | bytes 921608 | tf_op jit(solution)/shard_map/ppermute | solution.py:357
  18.7 0.7 copy-start.9
  18.7 0.8 copy-start.10
  47.5 1.8 %collective-permute-start.4 = (bf16[1536,128]{1,0:T(8,128)(2,1)S(1)}, bf16[1536,128]{1,0:T(8,128)(2,1)S(1)}, u32[]{:S(2)}, u32[]{:S(2)}) collective-permute-start(bf16[1536,128]{1,0:T(8,128)(2,1)S(1)} %constant_dynamic-slice_fusion), channel_id=1, source_target_pairs={{0,4},{4,0},{1,5},{5,1},{2,6},{6,2},{3,7},{7,3},{8,12},{12,8},{9,1... | collective-permute-start | bytes 1179656 | tf_op jit(solution)/shard_map/ppermute | solution.py:380
  65.8 22.4 %copy-start.11 = (bf16[200,768]{1,0:T(8,128)(2,1)S(1)}, bf16[200,768]{1,0:T(8,128)(2,1)}, u32[]{:S(2)}) copy-start(bf16[200,768]{1,0:T(8,128)(2,1)} %get-tuple-element.26.own_ref.cgrad_ref) | copy-start | bytes 921604
  82.4 13.5 %all-to-all-start.2 = ((bf16[16,96,128]{2,1,0:T(8,128)(2,1)}), bf16[16,96,128]{2,1,0:T(8,128)(2,1)S(1)}, u32[]{:S(2)}, u32[]{:S(2)}) async-start(bf16[16,96,128]{2,1,0:T(8,128)(2,1)} %broadcast_in_dim.8), calls=%async_computation.2 | async-start | bytes 786432 | tf_op jit(solution)/shard_map/all_to_all | solution.py:361
  88.2 10.3 %collective-permute-start.2 = (bf16[200,768]{1,0:T(8,128)(2,1)S(1)}, bf16[200,768]{1,0:T(8,128)(2,1)S(1)}, u32[]{:S(2)}, u32[]{:S(2)}) collective-permute-start(bf16[200,768]{1,0:T(8,128)(2,1)S(1)} %copy-done.11), channel_id=1, source_target_pairs={{0,4},{4,8},{8,12},{12,16},{16,20},{20,24},{24,28},{28,32},{32,36}... | collective-permute-start | bytes 921608 | tf_op jit(solution)/shard_map/ppermute | solution.py:357
  90.1 10.1 %collective-permute-start.3 = (bf16[200,768]{1,0:T(8,128)(2,1)S(1)}, bf16[200,768]{1,0:T(8,128)(2,1)S(1)}, u32[]{:S(2)}, u32[]{:S(2)}) collective-permute-start(bf16[200,768]{1,0:T(8,128)(2,1)S(1)} %copy-done.11), channel_id=1, source_target_pairs={{4,0},{8,4},{12,8},{16,12},{20,16},{24,20},{28,24},{32,28},{36,32}... | collective-permute-start | bytes 921608 | tf_op jit(solution)/shard_map/ppermute | solution.py:357
  95.9 12.8 %copy-start = (bf16[16,96,128]{2,1,0:T(8,128)(2,1)}, bf16[16,96,128]{2,1,0:T(8,128)(2,1)S(1)}, u32[]{:S(2)}) copy-start(bf16[16,96,128]{2,1,0:T(8,128)(2,1)S(1)} %all-to-all-done.2) | copy-start | bytes 1179652
  95.9 12.8 %collective-permute-start.5 = (bf16[1536,128]{1,0:T(8,128)(2,1)S(1)}, bf16[1536,128]{1,0:T(8,128)(2,1)S(1)}, u32[]{:S(2)}, u32[]{:S(2)}) collective-permute-start(bf16[1536,128]{1,0:T(8,128)(2,1)S(1)} %bitcast.20), channel_id=1, source_target_pairs={{0,4},{4,0},{1,5},{5,1},{2,6},{6,2},{3,7},{7,3},{8,12},{12,8},{9,1... | collective-permute-start | bytes 1179656 | tf_op jit(solution)/shard_map/ppermute | solution.py:386
  98.5 1.8 %copy-start.12 = (bf16[200,768]{1,0:T(8,128)(2,1)}, bf16[200,768]{1,0:T(8,128)(2,1)S(1)}, u32[]{:S(2)}) copy-start(bf16[200,768]{1,0:T(8,128)(2,1)S(1)} %collective-permute-done.2.north_ref) | copy-start | bytes 921604
  100.3 0.7 copy-start.13
  108.7 0.8 copy-start.1
  111.9 5.1 %copy-start.3 = (f32[200,49]{1,0:T(8,128)S(1)}, f32[200,49]{1,0:T(8,128)}, u32[]{:S(2)}) copy-start(f32[200,49]{1,0:T(8,128)} %get-tuple-element.68) | copy-start | bytes 117604

commit v2 on v1

v2 whole, which is shorter than its diff:
```python
import jax
import jax.numpy as jnp
from jax import lax
from jax.experimental import pallas as pl
from jax.experimental.pallas import tpu as pltpu
from jax.sharding import Mesh, PartitionSpec as P


C = 200
CX = 208
HID = 800
ROWS = 6
COLS = 128
CELLS = 768
WORDS = 5
BITS = 30
TAPS = 49
GROUPS = C // 8
BLOCKS = 7
HALF = 1536
SMALL = HID - 6 * COLS
VECTORS = SMALL + TAPS
MIB = 1 << 20

bf16 = jnp.bfloat16
f32 = jnp.float32
gelu_scale = 0.7978845608028654
VMEM = pl.BlockSpec(memory_space=pltpu.VMEM)
SMEM = pl.BlockSpec(memory_space=pltpu.SMEM)
NT_DIMS = (((1,), (1,)), ((), ()))
NORTH, OWN, SOUTH = 0, 1, 2


def row_class(row):
    return row // ROWS


def lanes(r):
    return slice(r * COLS, (r + 1) * COLS)


def wet_row(bits_ref, r):
    col = lax.broadcasted_iota(jnp.int32, (8, COLS), 1)
    word = jnp.zeros((8, COLS), jnp.int32)
    shift = col
    for w in range(WORDS):
        word = jnp.where(col >= BITS * w, bits_ref[w, 0, r], word)
        shift = jnp.where(col >= BITS * w, col - BITS * w, shift)
    return jnp.bitwise_and(jnp.right_shift(word, shift), 1).astype(f32)


def mask_kernel(bits_ref, fields_ref, masked_ref, wet_ref):
    for r in range(ROWS):
        wet = wet_row(bits_ref, r)
        wet_ref[:, lanes(r)] = wet
        masked_ref[:, lanes(r)] = (fields_ref[:, lanes(r)].astype(f32) * wet[0:1]).astype(bf16)


def fill_masks(slot_ref, near_ref, masks_ref):
    slot = slot_ref[0]

    def flag(k, step):
        return jnp.where(near_ref[0, k] == slot + step, 1.0, 0.0).astype(f32)

    lane = lax.broadcasted_iota(jnp.int32, (8, COLS), 1)
    triples = (
        (flag(0, -1), flag(4, -1), flag(5, -1)),
        (jnp.float32(1.0), flag(2, 0), flag(3, 0)),
        (flag(1, 1), flag(6, 1), flag(7, 1)),
    )
    for cls, (centre, west, east) in enumerate(triples):
        for b in range(7):
            off = 2 * b - 6
            mask = jnp.full((8, COLS), centre, f32)
            if off > 0:
                mask = jnp.where(lane < off, jnp.full((8, COLS), east, f32), mask)
            if off < 0:
                mask = jnp.where(lane >= COLS + off, jnp.full((8, COLS), west, f32), mask)
            masks_ref[7 * cls + b] = mask


def fill_rows(ref, part, rows_ref):
    for r in range(ROWS):
        rows_ref[ROWS * part + r] = ref[:, lanes(r)].astype(f32)


def conv_group(rows, coef, masks_ref, classes):
    total = [None] * ROWS
    for b in range(7):
        off = 2 * b - 6
        masked = {}
        for r in rows:
            plain = b == 3 and row_class(r) == OWN
            masked[r] = rows[r] if plain else rows[r] * masks_ref[7 * row_class(r) + b]
        taps = [coef(a, b) for a in range(7)]
        for i in range(ROWS):
            acc = None
            for a in range(7):
                if row_class(i + 2 * a) in classes:
                    term = taps[a] * masked[i + 2 * a]
                    acc = term if acc is None else acc + term
            if off != 0:
                acc = pltpu.roll(acc, (-off) % COLS, 1)
            total[i] = acc if total[i] is None else total[i] + acc
    return total


def pre_kernel(
    slot_ref,
    near_ref,
    own_ref,
    wet_ref,
    cot_ref,
    kern_ref,
    chan_ref,
    outw_ref,
    masks_ref,
    coef_ref,
    chans_ref,
    part_ref,
    ograd_ref,
    agrad_ref,
    osum_ref,
    rows_ref,
):
    fill_masks(slot_ref, near_ref, masks_ref)
    fill_rows(own_ref, 0, rows_ref)
    osum = jnp.zeros((C, COLS), f32)
    for r in range(ROWS):
        og = cot_ref[:, lanes(r)].astype(f32) * wet_ref[0:1, lanes(r)]
        osum = osum + og
        ograd_ref[:, lanes(r)] = jnp.concatenate([og, jnp.zeros((CX - C, COLS), f32)], axis=0).astype(bf16)
    osum_ref[...] = osum
    agrad_ref[...] = jnp.dot(outw_ref[...], ograd_ref[0:C, :], preferred_element_type=f32)

    def step(g, carry):
        at = pl.ds(pl.multiple_of(g * 8, 8), 8)
        kern = kern_ref[at, :]
        chan = chan_ref[at, :]
        for k in range(4):
            chans_ref[k, at, :] = jnp.broadcast_to(chan[:, k : k + 1], (8, COLS))
        rows = {ROWS + r: rows_ref[r, at, :] for r in range(ROWS)}

        def coef(a, b):
            t = 7 * a + b
            tap = jnp.broadcast_to(kern[:, t : t + 1], (8, COLS))
            coef_ref[t, at, :] = tap
            return tap

        total = conv_group(rows, coef, masks_ref, (OWN,))
        for i in range(ROWS):
            part_ref[at, lanes(i)] = total[i] + chans_ref[0, at, :]
        return carry

    lax.fori_loop(0, GROUPS, step, 0)


def main_kernel(
    core_ref,
    own_ref,
    north_ref,
    south_ref,
    wet_ref,
    masks_ref,
    coef_ref,
    chans_ref,
    part_ref,
    ograd_ref,
    agrad_ref,
    osum_ref,
    inw_ref,
    inwt_ref,
    outwt_ref,
    field_ref,
    cgrad_ref,
    keep_ref,
    send_ref,
    rows_ref,
    conv_ref,
    istd_ref,
    hid_ref,
    norm_ref,
    act_ref,
    hgrad_ref,
    sums_ref,
    pack_ref,
):
    fill_rows(north_ref, NORTH, rows_ref)
    fill_rows(own_ref, OWN, rows_ref)
    fill_rows(south_ref, SOUTH, rows_ref)

    def conv_step(g, carry):
        at = pl.ds(pl.multiple_of(g * 8, 8), 8)
        rows = {r: rows_ref[r, at, :] for r in range(3 * ROWS) if row_class(r) != OWN}
        total = conv_group(rows, lambda a, b: coef_ref[7 * a + b, at, :], masks_ref, (NORTH, SOUTH))
        for i in range(ROWS):
            conv_ref[at, lanes(i)] = total[i] + part_ref[at, lanes(i)]
        return carry

    lax.fori_loop(0, GROUPS, conv_step, 0)

    extra = lax.broadcasted_iota(jnp.int32, (8, COLS), 0)
    extra = jnp.where(extra < 2, 1.0, 0.0).astype(f32)
    for r in range(ROWS):
        x = conv_ref[:, lanes(r)]
        mean = jnp.sum(x, axis=0, keepdims=True) * (1.0 / C)
        x = x - mean
        var = jnp.sum(x * x, axis=0, keepdims=True) * (1.0 / C)
        istd = lax.rsqrt(var + 1e-06)
        normed = x * istd
        conv_ref[:, lanes(r)] = normed
        istd_ref[:, lanes(r)] = jnp.broadcast_to(istd, (8, COLS))
        no = jnp.concatenate([normed * chans_ref[1] + chans_ref[2], extra], axis=0)
        norm_ref[:, lanes(r)] = no.astype(bf16)

    hid_ref[...] = jnp.dot(inwt_ref[...], norm_ref[...], preferred_element_type=f32)

    def gelu_step(i, carry):
        at = pl.ds(pl.multiple_of(i * 16, 16), 16)
        h = hid_ref[at, :]
        h2 = h * h
        t = jnp.tanh(h * (gelu_scale + (gelu_scale * 0.044715) * h2))
        half = 0.5 + 0.5 * t
        act_ref[at, :] = (h * half).astype(bf16)
        slope = (0.5 * gelu_scale) + (0.5 * gelu_scale * 3.0 * 0.044715) * h2
        deriv = half + h * (1.0 - t * t) * slope
        hgrad_ref[at, :] = (agrad_ref[at, :] * deriv).astype(bf16)
        return carry

    lax.fori_loop(0, HID // 16, gelu_step, 0, unroll=2)

    hid_ref[0:C, :] = jnp.dot(inw_ref[...], hgrad_ref[...], preferred_element_type=f32)
    gsum = jnp.zeros((C, COLS), f32)
    ssum = jnp.zeros((C, COLS), f32)
    bsum = jnp.zeros((C, COLS), f32)
    cg_base = 3 * ROWS
    for r in range(ROWS):
        ng = hid_ref[0:C, lanes(r)]
        normed = conv_ref[:, lanes(r)]
        ssum = ssum + ng
        gsum = gsum + ng * normed
        scaled = ng * chans_ref[1]
        m1 = jnp.sum(scaled, axis=0, keepdims=True) * (1.0 / C)
        m2 = jnp.sum(scaled * normed, axis=0, keepdims=True) * (1.0 / C)
        cg = (istd_ref[0:1, lanes(r)] * (scaled - m1 - normed * m2)).astype(bf16)
        cgrad_ref[:, lanes(r)] = cg
        rows_ref[cg_base + r] = cg.astype(f32)
        bsum = bsum + cg.astype(f32)
    sums_ref[0] = bsum
    sums_ref[1] = gsum
    sums_ref[2] = ssum
    sums_ref[3] = osum_ref[...]

    hid_ref[0:C, :] = jnp.dot(outwt_ref[...], act_ref[...], preferred_element_type=f32)
    for r in range(ROWS):
        wet = wet_ref[0:1, lanes(r)]
        update = hid_ref[0:C, lanes(r)] + chans_ref[3]
        field_ref[:, lanes(r)] = (wet * (own_ref[:, lanes(r)].astype(f32) + update)).astype(bf16)

    def tap_step(g, carry):
        at = pl.ds(pl.multiple_of(g * 8, 8), 8)
        lane = lax.broadcasted_iota(jnp.int32, (8, COLS), 1)
        small = jnp.zeros((8, COLS), f32)
        for b in range(7):
            off = 2 * b - 6
            acc = [None] * 7
            for i in range(ROWS):
                turned = rows_ref[cg_base + i, at, :]
                if off != 0:
                    turned = pltpu.roll(turned, off % COLS, 1)
                parts = [turned if b == 3 and cls == OWN else turned * masks_ref[7 * cls + b] for cls in range(3)]
                for a in range(7):
                    r = i + 2 * a
                    term = parts[row_class(r)] * rows_ref[r, at, :]
                    acc[a] = term if acc[a] is None else acc[a] + term
            for a in range(7):
                value = jnp.sum(acc[a], axis=1, keepdims=True)
                small = jnp.where(lane == SMALL + 7 * a + b, value, small)
        for s in range(4):
            value = jnp.sum(sums_ref[s, at, :], axis=1, keepdims=True)
            small = jnp.where(lane == VECTORS + s, value, small)
        conv_ref[at, 0:COLS] = small
        return carry

    lax.fori_loop(0, GROUPS, tap_step, 0)

    for half, (left_ref, right_ref) in enumerate(((norm_ref, hgrad_ref), (ograd_ref, act_ref))):
        for blk in range(BLOCKS):
            first, last = blk * COLS, min((blk + 1) * COLS, HID)
            part = lax.dot_general(left_ref[...], right_ref[first:last, :], NT_DIMS, preferred_element_type=f32)
            if last - first < COLS:
                part = jnp.concatenate([part, jnp.zeros((CX, COLS - (last - first)), f32)], axis=1)
                if half == 0:
                    part = part + jnp.concatenate([conv_ref[:, 0:COLS], jnp.zeros((CX - C, COLS), f32)], axis=0)
            pack_ref[half, blk * CX : (blk + 1) * CX, :] = part.astype(bf16)
        pack_ref[half, BLOCKS * CX :, :] = jnp.zeros((HALF - BLOCKS * CX, COLS), bf16)
    core = core_ref[0]
    keep_ref[...] = pack_ref[core]
    send_ref[...] = pack_ref[1 - core]


def back_kernel(
    slot_ref,
    near_ref,
    own_ref,
    north_ref,
    south_ref,
    wet_ref,
    cot_ref,
    kern_ref,
    igrad_ref,
    masks_ref,
    rows_ref,
    conv_ref,
):
    fill_masks(slot_ref, near_ref, masks_ref)
    fill_rows(north_ref, NORTH, rows_ref)
    fill_rows(own_ref, OWN, rows_ref)
    fill_rows(south_ref, SOUTH, rows_ref)

    def conv_step(g, carry):
        at = pl.ds(pl.multiple_of(g * 8, 8), 8)
        rows = {r: rows_ref[r, at, :] for r in range(3 * ROWS)}
        kern = kern_ref[at, :]

        def coef(a, b):
            t = TAPS - 1 - 7 * a - b
            return jnp.broadcast_to(kern[:, t : t + 1], (8, COLS))

        total = conv_group(rows, coef, masks_ref, (NORTH, OWN, SOUTH))
        for i in range(ROWS):
            conv_ref[at, lanes(i)] = total[i]
        return carry

    lax.fori_loop(0, GROUPS, conv_step, 0)
    for r in range(ROWS):
        wet = wet_ref[0:1, lanes(r)]
        og = cot_ref[:, lanes(r)].astype(f32) * wet
        igrad_ref[:, lanes(r)] = (wet * (og + conv_ref[:, lanes(r)])).astype(bf16)


def unpack_kernel(factor, core_ref, mine_ref, other_ref, gin_ref, gout_ref, gkern_ref, *rest):
    *vec_refs, gbias_ref, full_ref = rest
    core = core_ref[0]
    full_ref[core] = mine_ref[...].astype(f32) * factor
    full_ref[1 - core] = other_ref[...].astype(f32) * factor
    for blk in range(BLOCKS):
        begin, end = blk * COLS, min((blk + 1) * COLS, HID)
        gin_ref[:, begin:end] = full_ref[0, blk * CX : blk * CX + C, 0 : end - begin]
        gbias_ref[0:1, begin:end] = full_ref[0, blk * CX + C : blk * CX + C + 1, 0 : end - begin]
        gout_ref[:, begin:end] = full_ref[1, blk * CX : blk * CX + C, 0 : end - begin]
    columns = full_ref[0, (BLOCKS - 1) * CX : (BLOCKS - 1) * CX + C, :].T
    gkern_ref[...] = columns[SMALL:VECTORS, :]
    for s, ref in enumerate(vec_refs):
        ref[...] = columns[VECTORS + s : VECTORS + s + 1, :]


def near(x):
    return pltpu.with_memory_space_constraint(x, pltpu.VMEM)


def hbm(shape, dtype):
    return jax.ShapeDtypeStruct(shape, dtype)


def call(kernel, outs, n_smem, args, scratch=(), time=1.0, limit=8):
    args = list(args[:n_smem]) + [near(x) for x in args[n_smem:]]
    return pl.pallas_call(
        kernel,
        out_shape=outs,
        in_specs=[SMEM] * n_smem + [VMEM] * (len(args) - n_smem),
        out_specs=[VMEM] * len(outs),
        scratch_shapes=[pltpu.VMEM(s, d) for s, d in scratch],
        cost_estimate=pl.CostEstimate(flops=int(time * 1.1e9), bytes_accessed=1000000, transcendentals=0),
        compiler_params=pltpu.CompilerParams(vmem_limit_bytes=limit * MIB),
    )(*args)


TILE_AXES = ("y", "z", "core")
PLANE = ("y", "rep")


def shifted(value, steps):
    count = lax.axis_size(TILE_AXES)
    first, last = max(0, -steps), min(count, count - steps)
    return lax.ppermute(value, TILE_AXES, [(s, s + steps) for s in range(first, last)])


def exchange(value, axes):
    return lax.all_to_all(value, axes, 0, 0, tiled=True)


def fold_kernel(value_ref, copies_ref):
    total = value_ref[0].astype(f32)
    for k in range(1, value_ref.shape[0]):
        total = total + value_ref[k].astype(f32)
    total = total.astype(bf16)
    for k in range(copies_ref.shape[0]):
        copies_ref[k] = total


def fold(value, axes, next_axes):
    count, copies = lax.axis_size(axes), lax.axis_size(next_axes)
    rows = value.shape[0] // count
    (out,) = call(
        fold_kernel,
        [pltpu.VMEM((copies, rows, COLS), bf16)],
        0,
        [value.reshape(count, rows, COLS)],
        limit=4,
    )
    return out.reshape(copies * rows, COLS)


def reduce_pack(keep, send):
    swap = [(0, 1), (1, 0)]
    got = lax.ppermute(send, "core", swap)
    pair = (keep.astype(f32) + got.astype(f32)).astype(bf16)
    part = fold(exchange(pair, PLANE), PLANE, "z")
    part = exchange(part, "z")
    mine = exchange(fold(part, "z", PLANE), PLANE)
    return mine, lax.ppermute(mine, "core", swap)


def step(
    fields,
    wet_bits,
    neighbours,
    kernel,
    conv_bias,
    ln_gain,
    ln_shift,
    in_weight,
    in_bias,
    out_weight,
    out_bias,
    cotangent,
):
    act2 = (C, CELLS)
    slot = lax.axis_index(TILE_AXES).astype(jnp.int32).reshape(1)
    core = lax.axis_index("core").astype(jnp.int32).reshape(1)
    cot = cotangent.reshape(act2)
    masked, wet = call(
        mask_kernel,
        [pltpu.VMEM(act2, bf16), pltpu.VMEM((8, CELLS), f32)],
        1,
        [wet_bits.transpose(2, 0, 1), fields.reshape(act2)],
        limit=4,
    )
    from_north = shifted(masked, 1)
    from_south = shifted(masked, -1)
    chan = jnp.stack([conv_bias, ln_gain, ln_shift, out_bias], axis=1)
    high = lax.reduce_precision(in_bias, 8, 7)
    bias_rows = jnp.stack([high, in_bias - high]).astype(bf16)
    inwt = jnp.concatenate([in_weight, bias_rows, jnp.zeros((CX - C - 2, HID), bf16)], axis=0).T
    chan, inwt = lax.optimization_barrier((chan, inwt))
    masks, coef, chans, part, ograd, agrad, osum = call(
        pre_kernel,
        [
            pltpu.VMEM((21, 8, COLS), f32),
            pltpu.VMEM((TAPS, C, COLS), f32),
            pltpu.VMEM((4, C, COLS), f32),
            pltpu.VMEM(act2, f32),
            pltpu.VMEM((CX, CELLS), bf16),
            pltpu.VMEM((HID, CELLS), f32),
            pltpu.VMEM((C, COLS), f32),
        ],
        2,
        [slot, neighbours, masked, wet, cot, kernel, chan, out_weight],
        [((ROWS, C, COLS), f32)],
        time=6.0,
        limit=8,
    )
    field, cgrad, keep, send = call(
        main_kernel,
        [
            hbm(act2, bf16),
            pltpu.VMEM(act2, bf16),
            pltpu.VMEM((HALF, COLS), bf16),
            pltpu.VMEM((HALF, COLS), bf16),
        ],
        1,
        [
            core,
            masked,
            from_north,
            from_south,
            wet,
            masks,
            coef,
            chans,
            part,
            ograd,
            agrad,
            osum,
            in_weight,
            inwt,
            out_weight.T,
        ],
        [
            ((4 * ROWS, C, COLS), f32),
            (act2, f32),
            ((8, CELLS), f32),
            ((HID, CELLS), f32),
            ((CX, CELLS), bf16),
            ((HID, CELLS), bf16),
            ((HID, CELLS), bf16),
            ((4, C, COLS), f32),
            ((2, HALF, COLS), bf16),
        ],
        time=12.0,
        limit=20,
    )
    cg_north = shifted(cgrad, 1)
    cg_south = shifted(cgrad, -1)
    (input_grad,) = call(
        back_kernel,
        [hbm(act2, bf16)],
        2,
        [slot, neighbours, cgrad, cg_north, cg_south, wet, cot, kernel],
        [((21, 8, COLS), f32), ((3 * ROWS, C, COLS), f32), (act2, f32)],
        time=6.0,
        limit=8,
    )
    mine, other = reduce_pack(keep, send)
    total_cells = lax.axis_size(TILE_AXES) * lax.axis_size("rep") * CELLS
    factor = float(total_cells) ** -0.5
    gin, gout, gkern, gbias, ggain, gshift, gobias, gibias = call(
        lambda *refs: unpack_kernel(factor, *refs),
        [hbm((C, HID), f32), hbm((C, HID), f32), hbm((TAPS, C), f32)] + [hbm((1, C), f32)] * 4 + [hbm((1, HID), f32)],
        1,
        [core, mine, other],
        [((2, HALF, COLS), f32)],
        limit=8,
    )
    return (
        field.reshape(1, 1, C, CELLS),
        input_grad.reshape(1, 1, C, CELLS),
        gkern.T,
        gbias.reshape(C),
        ggain.reshape(C),
        gshift.reshape(C),
        gin,
        gibias.reshape(HID),
        gout.T,
        gobias.reshape(C),
    )


def solution(mesh):
    rep = mesh.shape["rep"]
    fine = Mesh(mesh.devices.reshape(4, -1, 2, rep), ("y", "z", "core", "rep"))
    tile = P("rep", TILE_AXES, None, None)
    placed = (tile, P(TILE_AXES, None, None), P(TILE_AXES, None)) + (P(),) * 8 + (tile,)
    return jax.shard_map(
        step,
        mesh=fine,
        in_specs=placed,
        out_specs=(tile, tile) + (P(),) * 8,
        check_vma=False,
    )
```

time: 118 us -> 102 us (0.86)
  local copies, waits for them, and re-layouts: 15.4 us -> 4.52 us
  waiting for transfers between devices: 5.94 us -> 9.59 us
  starting transfers between devices: 22.7 us -> 19.2 us
  Pallas kernels: 38.9 us -> 35.7 us
  other arithmetic: 2.88 us -> 1.65 us
    unnamed x34 -> x23, local copies, waits for them, and re-layouts: 9.61 us -> 3.99 us
    ppermute x4, starting transfers between devices: 16.7 us -> 13.3 us  [shifted(): lax.ppermute(value, TILE_AXES, [(s, s + steps) for s in range(first, last)])]
    pallas_call x5 -> x7, Pallas kernels: 38.9 us -> 35.7 us  [call(): pl.pallas_call(kernel, out_shape=outs, in_specs=[SMEM] * n_smem + [VMEM]...]
    all_to_all x1, waiting for transfers between devices: 0.01 us -> 2.97 us  [exchange(): return lax.all_to_all(value, axes, 0, 0, tiled=True)]
    slice x2 -> x0, local copies, waits for them, and re-layouts: 2.78 us -> none  [the longest x1 1.42 us: body(): gvec[3, 0:C]]
  transfers between devices with their start and end apart: 7 -> 7, of which waited for: 3 -> 3; matrix products, arithmetic and copies ran while one was open for 5% -> 4% of each run, Pallas kernels for 7% -> 15%
where the time goes in v2:
time: 102 us
  Pallas kernels  35.7 us (35%)
  blocking collectives  30.3 us (30%)
  starting transfers between devices  19.2 us (19%)
  waiting for transfers between devices  9.59 us (9%)
  local copies, waits for them, and re-layouts  4.52 us (4%)
  other arithmetic  1.65 us (2%)
    pallas_call x7, Pallas kernels, call(): pl.pallas_call(kernel, out_shape=outs, in_specs=[SMEM] * n_smem + [VMEM]...  35.7 us
    all_to_all x2, blocking collectives, exchange(): return lax.all_to_all(value, axes, 0, 0, tiled=True)  30.3 us
    ppermute x4, starting transfers between devices, shifted(): lax.ppermute(value, TILE_AXES, [(s, s + steps) for s in range(first, last)])  13.3 us
    all_to_all x1, starting transfers between devices, exchange(): return lax.all_to_all(value, axes, 0, 0, tiled=True)  5.84 us
    ppermute x4, waiting for transfers between devices, shifted(): lax.ppermute(value, TILE_AXES, [(s, s + steps) for s in range(first, last)])  4.9 us
    unnamed x23, local copies, waits for them, and re-layouts  3.99 us
    all_to_all x1, waiting for transfers between devices, exchange(): return lax.all_to_all(value, axes, 0, 0, tiled=True)  2.97 us
  transfers between devices with their start and end apart: 7, of which 3 were waited for; matrix products, arithmetic and copies ran while one was open for 4% of the time, Pallas kernels for 15%

profile of v2, /device:TPU:8, one launch (start us, length us, event | category | flops | bytes accessed | tf_op | source)
XLA Modules:
  0.0 101.8 jit_solution(2813535324816153136)
XLA Ops:
  0.7 1.0 copy-done.2
  1.7 0.7 copy-done.4
  2.4 0.7 shard_map.195
  3.0 7.1 %collective-permute-start.1 = (bf16[200,768]{1,0:T(8,128)(2,1)S(1)}, bf16[200,768]{1,0:T(8,128)(2,1)S(1)}, u32[]{:S(2)}, u32[]{:S(2)}) collective-permute-start(bf16[200,768]{1,0:T(8,128)(2,1)S(1)} %get-tuple-element.33.own_ref), channel_id=1, source_target_pairs={{4,0},{8,4},{12,8},{16,12},{20,16},{24,20},{28,24},{32,28},{36,32}... | collective-permute-start | bytes 921608 | tf_op jit(solution)/shard_map/ppermute | solution.py:386
  10.1 1.9 %collective-permute-start = (bf16[200,768]{1,0:T(8,128)(2,1)S(1)}, bf16[200,768]{1,0:T(8,128)(2,1)S(1)}, u32[]{:S(2)}, u32[]{:S(2)}) collective-permute-start(bf16[200,768]{1,0:T(8,128)(2,1)S(1)} %get-tuple-element.33.own_ref), channel_id=1, source_target_pairs={{0,4},{4,8},{8,12},{12,16},{16,20},{20,24},{24,28},{28,32},{32,36}... | collective-permute-start | bytes 921608 | tf_op jit(solution)/shard_map/ppermute | solution.py:386
  12.1 0.7 reduce-precision_convert_fusion
  12.8 0.9 copy.39.kern_ref
  14.0 1.2 %copy.36 = bf16[200,800]{0,1:T(8,128)(2,1)S(1)} copy(bf16[200,800]{1,0:T(8,128)(2,1)} %inw_ref.1) | data formatting | bytes 640000 | tf_op args[7]
  15.3 0.2 maximum_bitcast_fusion.inwt_ref
  15.7 0.2 copy.41.outw_ref
  15.9 7.9 %shard_map.196 = (f32[21,8,128]{2,1,0:T(8,128)S(1)}, f32[49,200,128]{2,1,0:T(8,128)S(1)}, f32[4,200,128]{2,1,0:T(8,128)S(1)}, f32[200,768]{1,0:T(8,128)S(1)}, bf...) custom-call(s32[1]{0:T(128)} %bitcast.3.slot_ref, s32[1,8]{1,0:T(1,128)S(1)} %copy-done.5, ...), custom_call_target="tpu_custom_call" | custom-call | flops 6600000000 | bytes 1000000 | tf_op jit(solution)/shard_map/pallas_call | solution.py:368
  23.9 18.0 %shard_map.197 = (bf16[200,768]{1,0:T(8,128)(2,1)}, bf16[200,768]{1,0:T(8,128)(2,1)S(1)}, bf16[1536,128]{1,0:T(8,128)(2,1)S(1)}, bf16[1536,128]{1,0:T(8,128)(2,1)S(1)}) custom-call(s32[1]{0:T(128)} %bitcast.core_ref.refs_0_, bf16[200,768]{1,0:T(8,128)(2,1)S(1)} %get-tuple-element.33.own_ref, bf16[200,768]{1,0:T(8,128)(2,1)S(1)} %collective-permute-done.north_ref, ...), custom_call_target="tpu_custom_call" | custom-call | flops 13200000000 | bytes 1000000 | tf_op jit(solution)/shard_map/pallas_call | solution.py:368
  42.0 1.7 %collective-permute-done.4 = bf16[1536,128]{1,0:T(8,128)(2,1)S(1)} collective-permute-done((bf16[1536,128]{1,0:T(8,128)(2,1)S(1)}, bf16[1536,128]{1,0:T(8,128)(2,1)S(1)}, u32[]{:S(2)}, u32[]{:S(2)}) %collective-permute-start.4) | collective-permute-done | bytes 393248 | tf_op jit(solution)/shard_map/ppermute | solution.py:417
  43.8 15.3 %all_to_all.23.value_ref = bf16[16,96,128]{2,1,0:T(8,128)(2,1)S(1)} all-to-all(bf16[16,96,128]{2,1,0:T(8,128)(2,1)S(1)} %bitcast.29), channel_id=1, replica_groups=mesh['y'=4,'z'=8,'core'=2,'rep'=4] {'y','rep'}, dimensions={0} | all-to-all | bytes 786432 | tf_op jit(solution)/shard_map/all_to_all | solution.py:390
  59.2 14.9 %all_to_all.24.value_ref = bf16[8,96,128]{2,1,0:T(8,128)(2,1)S(1)} all-to-all(bf16[8,96,128]{2,1,0:T(8,128)(2,1)S(1)} %shard_map.199), channel_id=1, replica_groups=mesh['y'=4,'z'=8,'core'=2,'rep'=4] {'z'}, dimensions={0} | all-to-all | bytes 393216 | tf_op jit(solution)/shard_map/all_to_all | solution.py:390
  74.1 0.8 shard_map.200
  74.9 5.8 %all-to-all-start.2 = ((bf16[16,96,128]{2,1,0:T(8,128)(2,1)}), bf16[16,96,128]{2,1,0:T(8,128)(2,1)S(1)}, u32[]{:S(2)}, u32[]{:S(2)}) async-start(bf16[16,96,128]{2,1,0:T(8,128)(2,1)} %shard_map.200), calls=%async_computation.2 | async-start | bytes 786432 | tf_op jit(solution)/shard_map/all_to_all | solution.py:390
  80.7 1.9 %collective-permute-start.3 = (bf16[200,768]{1,0:T(8,128)(2,1)S(1)}, bf16[200,768]{1,0:T(8,128)(2,1)S(1)}, u32[]{:S(2)}, u32[]{:S(2)}) collective-permute-start(bf16[200,768]{1,0:T(8,128)(2,1)S(1)} %get-tuple-element.45.own_ref), channel_id=1, source_target_pairs={{4,0},{8,4},{12,8},{16,12},{20,16},{24,20},{28,24},{32,28},{36,32}... | collective-permute-start | bytes 921608 | tf_op jit(solution)/shard_map/ppermute | solution.py:386
  82.7 2.4 %collective-permute-start.2 = (bf16[200,768]{1,0:T(8,128)(2,1)S(1)}, bf16[200,768]{1,0:T(8,128)(2,1)S(1)}, u32[]{:S(2)}, u32[]{:S(2)}) collective-permute-start(bf16[200,768]{1,0:T(8,128)(2,1)S(1)} %get-tuple-element.45.own_ref), channel_id=1, source_target_pairs={{0,4},{4,8},{8,12},{12,16},{16,20},{20,24},{24,28},{28,32},{32,36}... | collective-permute-start | bytes 921608 | tf_op jit(solution)/shard_map/ppermute | solution.py:386
  85.1 3.0 %all-to-all-done.2 = bf16[16,96,128]{2,1,0:T(8,128)(2,1)S(1)} async-done(((bf16[16,96,128]{2,1,0:T(8,128)(2,1)}), bf16[16,96,128]{2,1,0:T(8,128)(2,1)S(1)}, u32[]{:S(2)}, u32[]{:S(2)}) %all-to-all-start.2) | async-done | bytes 393248 | tf_op jit(solution)/shard_map/all_to_all | solution.py:390
  88.1 4.9 %collective-permute-done.2.north_ref = bf16[200,768]{1,0:T(8,128)(2,1)S(1)} collective-permute-done((bf16[200,768]{1,0:T(8,128)(2,1)S(1)}, bf16[200,768]{1,0:T(8,128)(2,1)S(1)}, u32[]{:S(2)}, u32[]{:S(2)}) %collective-permute-start.2) | collective-permute-done | bytes 307232 | tf_op jit(solution)/shard_map/ppermute | solution.py:386
  93.0 7.0 %shard_map.198 = bf16[200,768]{1,0:T(8,128)(2,1)} custom-call(s32[1]{0:T(128)} %bitcast.3.slot_ref, s32[1,8]{1,0:T(1,128)S(1)} %copy-done.5, bf16[200,768]{1,0:T(8,128)(2,1)S(1)} %get-tuple-element.45.own_ref, bf16[200,768]{1,0:T(8,128)(2,1)S(1)} %collective-permute-done.2.north_ref, bf16[200,768]{1,0:T(8,128)(2,1)S(1)} %collective-permute-done.3.south_ref, ...), custom_call_target="tpu_custom_call" | custom-call | flops 6600000000 | bytes 1000000 | tf_op jit(solution)/shard_map/pallas_call | solution.py:368
  99.9 1.3 %shard_map.201 = (f32[200,800]{1,0:T(8,128)}, f32[200,800]{1,0:T(8,128)}, f32[49,200]{1,0:T(8,128)}, f32[1,200]{1,0:T(1,128)}, f32[1,200]{1,0:T(1,128)}, /*index...) custom-call(s32[1]{0:T(128)} %bitcast.core_ref.refs_0_, bf16[1536,128]{1,0:T(8,128)(2,1)S(1)} %bitcast.23, ...), custom_call_target="tpu_custom_call" | custom-call | flops 1100000000 | bytes 1000000 | tf_op jit(solution)/shard_map/pallas_call | solution.py:368
  101.2 0.6 reduce
  (32 shorter events, 0.8 us)
Async XLA Ops:
  0.6 15.1 %copy-start = (bf16[800,200]{0,1:T(8,128)(2,1)S(1)}, bf16[800,200]{0,1:T(8,128)(2,1)}, u32[]{:S(2)}) copy-start(bf16[800,200]{0,1:T(8,128)(2,1)} %param.21) | copy-start | bytes 960004
  0.7 1.0 copy-start.2
  1.7 0.7 copy-start.4
  2.4 13.0 %copy-start.6 = (f32[200]{0:T(256)S(1)}, f32[200]{0:T(256)}, u32[]{:S(2)}) copy-start(f32[200]{0:T(256)} %param.22) | copy-start | bytes 2404
  2.4 13.0 %copy-start.7 = (f32[200]{0:T(256)S(1)}, f32[200]{0:T(256)}, u32[]{:S(2)}) copy-start(f32[200]{0:T(256)} %param.18) | copy-start | bytes 2404
  2.4 13.0 %copy-start.8 = (f32[200]{0:T(256)S(1)}, f32[200]{0:T(256)}, u32[]{:S(2)}) copy-start(f32[200]{0:T(256)} %param.17) | copy-start | bytes 2404
  2.4 13.0 %copy-start.9 = (f32[200]{0:T(256)S(1)}, f32[200]{0:T(256)}, u32[]{:S(2)}) copy-start(f32[200]{0:T(256)} %param.16) | copy-start | bytes 2404
  2.4 13.6 %copy-start.3 = (bf16[1,1,200,768]{3,2,1,0:T(8,128)(2,1)S(1)}, bf16[1,1,200,768]{3,2,1,0:T(8,128)(2,1)}, u32[]{:S(2)}) copy-start(bf16[1,1,200,768]{3,2,1,0:T(8,128)(2,1)} %param.23) | copy-start | bytes 921604
  2.4 13.6 %copy-start.5 = (s32[1,8]{1,0:T(1,128)S(1)}, s32[1,8]{1,0:T(1,128)}, u32[]{:S(2)}) copy-start(s32[1,8]{1,0:T(1,128)} %near_ref.3) | copy-start | bytes 100
  3.0 20.8 %collective-permute-start.1 = (bf16[200,768]{1,0:T(8,128)(2,1)S(1)}, bf16[200,768]{1,0:T(8,128)(2,1)S(1)}, u32[]{:S(2)}, u32[]{:S(2)}) collective-permute-start(bf16[200,768]{1,0:T(8,128)(2,1)S(1)} %get-tuple-element.33.own_ref), channel_id=1, source_target_pairs={{4,0},{8,4},{12,8},{16,12},{20,16},{24,20},{28,24},{32,28},{36,32}... | collective-permute-start | bytes 921608 | tf_op jit(solution)/shard_map/ppermute | solution.py:386
  10.1 13.8 %collective-permute-start = (bf16[200,768]{1,0:T(8,128)(2,1)S(1)}, bf16[200,768]{1,0:T(8,128)(2,1)S(1)}, u32[]{:S(2)}, u32[]{:S(2)}) collective-permute-start(bf16[200,768]{1,0:T(8,128)(2,1)S(1)} %get-tuple-element.33.own_ref), channel_id=1, source_target_pairs={{0,4},{4,8},{8,12},{12,16},{16,20},{20,24},{24,28},{28,32},{32,36}... | collective-permute-start | bytes 921608 | tf_op jit(solution)/shard_map/ppermute | solution.py:386
  15.9 8.0 %copy-start.1 = (bf16[200,800]{1,0:T(8,128)(2,1)S(1)}, bf16[200,800]{1,0:T(8,128)(2,1)}, u32[]{:S(2)}) copy-start(bf16[200,800]{1,0:T(8,128)(2,1)} %inw_ref.1) | copy-start | bytes 960004
  42.0 1.7 %collective-permute-start.4 = (bf16[1536,128]{1,0:T(8,128)(2,1)S(1)}, bf16[1536,128]{1,0:T(8,128)(2,1)S(1)}, u32[]{:S(2)}, u32[]{:S(2)}) collective-permute-start(bf16[1536,128]{1,0:T(8,128)(2,1)S(1)} %get-tuple-element.47), channel_id=1, source_target_pairs={{0,4},{4,0},{1,5},{5,1},{2,6},{6,2},{3,7},{7,3},{8,12},{12,8},{9,1... | collective-permute-start | bytes 1179656 | tf_op jit(solution)/shard_map/ppermute | solution.py:417
  74.9 13.1 %all-to-all-start.2 = ((bf16[16,96,128]{2,1,0:T(8,128)(2,1)}), bf16[16,96,128]{2,1,0:T(8,128)(2,1)S(1)}, u32[]{:S(2)}, u32[]{:S(2)}) async-start(bf16[16,96,128]{2,1,0:T(8,128)(2,1)} %shard_map.200), calls=%async_computation.2 | async-start | bytes 786432 | tf_op jit(solution)/shard_map/all_to_all | solution.py:390
  80.7 7.3 %collective-permute-start.3 = (bf16[200,768]{1,0:T(8,128)(2,1)S(1)}, bf16[200,768]{1,0:T(8,128)(2,1)S(1)}, u32[]{:S(2)}, u32[]{:S(2)}) collective-permute-start(bf16[200,768]{1,0:T(8,128)(2,1)S(1)} %get-tuple-element.45.own_ref), channel_id=1, source_target_pairs={{4,0},{8,4},{12,8},{16,12},{20,16},{24,20},{28,24},{32,28},{36,32}... | collective-permute-start | bytes 921608 | tf_op jit(solution)/shard_map/ppermute | solution.py:386
  82.7 10.3 %collective-permute-start.2 = (bf16[200,768]{1,0:T(8,128)(2,1)S(1)}, bf16[200,768]{1,0:T(8,128)(2,1)S(1)}, u32[]{:S(2)}, u32[]{:S(2)}) collective-permute-start(bf16[200,768]{1,0:T(8,128)(2,1)S(1)} %get-tuple-element.45.own_ref), channel_id=1, source_target_pairs={{0,4},{4,8},{8,12},{12,16},{16,20},{20,24},{24,28},{28,32},{32,36}... | collective-permute-start | bytes 921608 | tf_op jit(solution)/shard_map/ppermute | solution.py:386
  88.1 11.9 %collective-permute-start.5 = (bf16[1536,128]{1,0:T(8,128)(2,1)S(1)}, bf16[1536,128]{1,0:T(8,128)(2,1)S(1)}, u32[]{:S(2)}, u32[]{:S(2)}) collective-permute-start(bf16[1536,128]{1,0:T(8,128)(2,1)S(1)} %bitcast.22), channel_id=1, source_target_pairs={{0,4},{4,0},{1,5},{5,1},{2,6},{6,2},{3,7},{7,3},{8,12},{12,8},{9,1... | collective-permute-start | bytes 1179656 | tf_op jit(solution)/shard_map/ppermute | solution.py:422

commit v3 on v2

--- a/solution.py
+++ b/solution.py
@@ -18,9 +18,10 @@
 GROUPS = C // 8
 BLOCKS = 7
 HALF = 1536
-SMALL = HID - 6 * COLS
-VECTORS = SMALL + TAPS
+SMALL = BLOCKS * CX
+PAIRS = 27
 MIB = 1 << 20
+UNROLL = 5
 
 bf16 = jnp.bfloat16
 f32 = jnp.float32
@@ -105,14 +106,18 @@
     return total
 
 
+def fill_coef(table_ref, coef_ref):
+    for t in range(TAPS):
+        coef_ref[t] = jnp.broadcast_to(table_ref[:, t : t + 1], (C, COLS))
+
+
 def pre_kernel(
     slot_ref,
     near_ref,
     own_ref,
     wet_ref,
     cot_ref,
-    kern_ref,
-    chan_ref,
+    table_ref,
     outw_ref,
     masks_ref,
     coef_ref,
@@ -132,27 +137,19 @@
         ograd_ref[:, lanes(r)] = jnp.concatenate([og, jnp.zeros((CX - C, COLS), f32)], axis=0).astype(bf16)
     osum_ref[...] = osum
     agrad_ref[...] = jnp.dot(outw_ref[...], ograd_ref[0:C, :], preferred_element_type=f32)
+    fill_coef(table_ref, coef_ref)
+    for k in range(4):
+        chans_ref[k] = jnp.broadcast_to(table_ref[:, TAPS + k : TAPS + k + 1], (C, COLS))
 
     def step(g, carry):
         at = pl.ds(pl.multiple_of(g * 8, 8), 8)
-        kern = kern_ref[at, :]
-        chan = chan_ref[at, :]
-        for k in range(4):
-            chans_ref[k, at, :] = jnp.broadcast_to(chan[:, k : k + 1], (8, COLS))
         rows = {ROWS + r: rows_ref[r, at, :] for r in range(ROWS)}
-
-        def coef(a, b):
-            t = 7 * a + b
-            tap = jnp.broadcast_to(kern[:, t : t + 1], (8, COLS))
-            coef_ref[t, at, :] = tap
-            return tap
-
-        total = conv_group(rows, coef, masks_ref, (OWN,))
+        total = conv_group(rows, lambda a, b: coef_ref[7 * a + b, at, :], masks_ref, (OWN,))
         for i in range(ROWS):
             part_ref[at, lanes(i)] = total[i] + chans_ref[0, at, :]
         return carry
 
-    lax.fori_loop(0, GROUPS, step, 0)
+    lax.fori_loop(0, GROUPS, step, 0, unroll=UNROLL)
 
 
 def main_kernel(
@@ -160,7 +157,6 @@
     own_ref,
     north_ref,
     south_ref,
-    wet_ref,
     masks_ref,
     coef_ref,
     chans_ref,
@@ -170,9 +166,8 @@
     osum_ref,
     inw_ref,
     inwt_ref,
-    outwt_ref,
-    field_ref,
     cgrad_ref,
+    act_ref,
     keep_ref,
     send_ref,
     rows_ref,
@@ -180,9 +175,9 @@
     istd_ref,
     hid_ref,
     norm_ref,
-    act_ref,
     hgrad_ref,
     sums_ref,
+    small_ref,
     pack_ref,
 ):
     fill_rows(north_ref, NORTH, rows_ref)
@@ -197,7 +192,7 @@
             conv_ref[at, lanes(i)] = total[i] + part_ref[at, lanes(i)]
         return carry
 
-    lax.fori_loop(0, GROUPS, conv_step, 0)
+    lax.fori_loop(0, GROUPS, conv_step, 0, unroll=UNROLL)
 
     extra = lax.broadcasted_iota(jnp.int32, (8, COLS), 0)
     extra = jnp.where(extra < 2, 1.0, 0.0).astype(f32)
@@ -246,21 +241,11 @@
         cgrad_ref[:, lanes(r)] = cg
         rows_ref[cg_base + r] = cg.astype(f32)
         bsum = bsum + cg.astype(f32)
-    sums_ref[0] = bsum
-    sums_ref[1] = gsum
-    sums_ref[2] = ssum
-    sums_ref[3] = osum_ref[...]
-
-    hid_ref[0:C, :] = jnp.dot(outwt_ref[...], act_ref[...], preferred_element_type=f32)
-    for r in range(ROWS):
-        wet = wet_ref[0:1, lanes(r)]
-        update = hid_ref[0:C, lanes(r)] + chans_ref[3]
-        field_ref[:, lanes(r)] = (wet * (own_ref[:, lanes(r)].astype(f32) + update)).astype(bf16)
+    for s, vec in enumerate((bsum, gsum, ssum, osum_ref[...], jnp.zeros((C, COLS), f32))):
+        sums_ref[(TAPS + s) // 2, :, lanes((TAPS + s) % 2)] = vec.astype(bf16)
 
     def tap_step(g, carry):
         at = pl.ds(pl.multiple_of(g * 8, 8), 8)
-        lane = lax.broadcasted_iota(jnp.int32, (8, COLS), 1)
-        small = jnp.zeros((8, COLS), f32)
         for b in range(7):
             off = 2 * b - 6
             acc = [None] * 7
@@ -274,29 +259,43 @@
                     term = parts[row_class(r)] * rows_ref[r, at, :]
                     acc[a] = term if acc[a] is None else acc[a] + term
             for a in range(7):
-                value = jnp.sum(acc[a], axis=1, keepdims=True)
-                small = jnp.where(lane == SMALL + 7 * a + b, value, small)
-        for s in range(4):
-            value = jnp.sum(sums_ref[s, at, :], axis=1, keepdims=True)
-            small = jnp.where(lane == VECTORS + s, value, small)
-        conv_ref[at, 0:COLS] = small
+                t = 7 * a + b
+                sums_ref[t // 2, at, lanes(t % 2)] = acc[a].astype(bf16)
         return carry
 
-    lax.fori_loop(0, GROUPS, tap_step, 0)
+    lax.fori_loop(0, GROUPS, tap_step, 0, unroll=UNROLL)
+    lane = lax.broadcasted_iota(jnp.int32, (8, 2 * COLS), 1)
+    line = lax.broadcasted_iota(jnp.int32, (8, 2 * COLS), 0)
+    pick = jnp.where((lane >= COLS) == (line == 1), jnp.where(line < 2, 1.0, 0.0), 0.0).astype(bf16)
+    small_ref[...] = jnp.zeros(small_ref.shape, f32)
+    for k in range(PAIRS):
+        both = lax.dot_general(pick, sums_ref[k], NT_DIMS, preferred_element_type=f32)
+        small_ref[2 * k : 2 * k + 2, 0:C] = both[0:2, :]
 
     for half, (left_ref, right_ref) in enumerate(((norm_ref, hgrad_ref), (ograd_ref, act_ref))):
-        for blk in range(BLOCKS):
-            first, last = blk * COLS, min((blk + 1) * COLS, HID)
+        for first in range(0, HID, 2 * COLS):
+            last = min(first + 2 * COLS, HID)
+            blk = first // COLS
             part = lax.dot_general(left_ref[...], right_ref[first:last, :], NT_DIMS, preferred_element_type=f32)
             if last - first < COLS:
                 part = jnp.concatenate([part, jnp.zeros((CX, COLS - (last - first)), f32)], axis=1)
-                if half == 0:
-                    part = part + jnp.concatenate([conv_ref[:, 0:COLS], jnp.zeros((CX - C, COLS), f32)], axis=0)
-            pack_ref[half, blk * CX : (blk + 1) * CX, :] = part.astype(bf16)
-        pack_ref[half, BLOCKS * CX :, :] = jnp.zeros((HALF - BLOCKS * CX, COLS), bf16)
+            pack_ref[half, blk * CX : (blk + 1) * CX, :] = part[:, 0:COLS].astype(bf16)
+            if last - first > COLS:
+                pack_ref[half, (blk + 1) * CX : (blk + 2) * CX, :] = part[:, COLS:].astype(bf16)
+        pack_ref[half, SMALL : SMALL + 2 * PAIRS + 2, :] = small_ref[:, lanes(half)].astype(bf16)
+        pack_ref[half, SMALL + 2 * PAIRS + 2 :, :] = jnp.zeros((HALF - SMALL - 2 * PAIRS - 2, COLS), bf16)
     core = core_ref[0]
     keep_ref[...] = pack_ref[core]
     send_ref[...] = pack_ref[1 - core]
+
+
+def field_kernel(own_ref, wet_ref, table_ref, act_ref, outwt_ref, field_ref, hid_ref):
+    hid_ref[...] = jnp.dot(outwt_ref[...], act_ref[...], preferred_element_type=f32)
+    bias = jnp.broadcast_to(table_ref[:, TAPS + 3 : TAPS + 4], (C, COLS))
+    for r in range(ROWS):
+        update = hid_ref[:, lanes(r)] + bias
+        own = own_ref[:, lanes(r)].astype(f32)
+        field_ref[:, lanes(r)] = (wet_ref[0:1, lanes(r)] * (own + update)).astype(bf16)
 
 
 def back_kernel(
@@ -307,13 +306,15 @@
     south_ref,
     wet_ref,
     cot_ref,
-    kern_ref,
+    table_ref,
     igrad_ref,
     masks_ref,
     rows_ref,
     conv_ref,
+    coef_ref,
 ):
     fill_masks(slot_ref, near_ref, masks_ref)
+    fill_coef(table_ref, coef_ref)
     fill_rows(north_ref, NORTH, rows_ref)
     fill_rows(own_ref, OWN, rows_ref)
     fill_rows(south_ref, SOUTH, rows_ref)
@@ -321,18 +322,14 @@
     def conv_step(g, carry):
         at = pl.ds(pl.multiple_of(g * 8, 8), 8)
         rows = {r: rows_ref[r, at, :] for r in range(3 * ROWS)}
-        kern = kern_ref[at, :]
-
-        def coef(a, b):
-            t = TAPS - 1 - 7 * a - b
-            return jnp.broadcast_to(kern[:, t : t + 1], (8, COLS))
-
-        total = conv_group(rows, coef, masks_ref, (NORTH, OWN, SOUTH))
+        total = conv_group(
+            rows, lambda a, b: coef_ref[TAPS - 1 - 7 * a - b, at, :], masks_ref, (NORTH, OWN, SOUTH)
+        )
         for i in range(ROWS):
             conv_ref[at, lanes(i)] = total[i]
         return carry
 
-    lax.fori_loop(0, GROUPS, conv_step, 0)
+    lax.fori_loop(0, GROUPS, conv_step, 0, unroll=UNROLL)
     for r in range(ROWS):
         wet = wet_ref[0:1, lanes(r)]
         og = cot_ref[:, lanes(r)].astype(f32) * wet
@@ -349,10 +346,11 @@
         gin_ref[:, begin:end] = full_ref[0, blk * CX : blk * CX + C, 0 : end - begin]
         gbias_ref[0:1, begin:end] = full_ref[0, blk * CX + C : blk * CX + C + 1, 0 : end - begin]
         gout_ref[:, begin:end] = full_ref[1, blk * CX : blk * CX + C, 0 : end - begin]
-    columns = full_ref[0, (BLOCKS - 1) * CX : (BLOCKS - 1) * CX + C, :].T
-    gkern_ref[...] = columns[SMALL:VECTORS, :]
-    for s, ref in enumerate(vec_refs):
-        ref[...] = columns[VECTORS + s : VECTORS + s + 1, :]
+    for half, begin, end in ((0, 0, COLS), (1, COLS, C)):
+        small = full_ref[half, SMALL : SMALL + 2 * PAIRS + 2, 0 : end - begin]
+        gkern_ref[:, begin:end] = small[0:TAPS]
+        for s, ref in enumerate(vec_refs):
+            ref[:, begin:end] = small[TAPS + s : TAPS + s + 1]
 
 
 def near(x):
@@ -390,6 +388,10 @@
     return lax.all_to_all(value, axes, 0, 0, tiled=True)
 
 
+def add_kernel(keep_ref, got_ref, pair_ref):
+    pair_ref[...] = (keep_ref[...].astype(f32) + got_ref[...].astype(f32)).astype(bf16)
+
+
 def fold_kernel(value_ref, copies_ref):
     total = value_ref[0].astype(f32)
     for k in range(1, value_ref.shape[0]):
@@ -415,8 +417,9 @@
 def reduce_pack(keep, send):
     swap = [(0, 1), (1, 0)]
     got = lax.ppermute(send, "core", swap)
-    pair = (keep.astype(f32) + got.astype(f32)).astype(bf16)
-    part = fold(exchange(pair, PLANE), PLANE, "z")
+    (pair,) = call(add_kernel, [pltpu.VMEM((HALF, COLS), bf16)], 0, [keep, got], limit=4)
+    part = exchange(pair, PLANE)
+    part = fold(part, PLANE, "z")
     part = exchange(part, "z")
     mine = exchange(fold(part, "z", PLANE), PLANE)
     return mine, lax.ppermute(mine, "core", swap)
@@ -449,11 +452,12 @@
     )
     from_north = shifted(masked, 1)
     from_south = shifted(masked, -1)
-    chan = jnp.stack([conv_bias, ln_gain, ln_shift, out_bias], axis=1)
+    vectors = jnp.stack([conv_bias, ln_gain, ln_shift, out_bias])
+    table = jnp.concatenate([kernel.T, vectors], axis=0).T
     high = lax.reduce_precision(in_bias, 8, 7)
     bias_rows = jnp.stack([high, in_bias - high]).astype(bf16)
     inwt = jnp.concatenate([in_weight, bias_rows, jnp.zeros((CX - C - 2, HID), bf16)], axis=0).T
-    chan, inwt = lax.optimization_barrier((chan, inwt))
+    table, inwt = lax.optimization_barrier((table, inwt))
     masks, coef, chans, part, ograd, agrad, osum = call(
         pre_kernel,
         [
@@ -466,16 +470,16 @@
             pltpu.VMEM((C, COLS), f32),
         ],
         2,
-        [slot, neighbours, masked, wet, cot, kernel, chan, out_weight],
+        [slot, neighbours, masked, wet, cot, table, out_weight],
         [((ROWS, C, COLS), f32)],
         time=6.0,
         limit=8,
     )
-    field, cgrad, keep, send = call(
+    cgrad, act, keep, send = call(
         main_kernel,
         [
-            hbm(act2, bf16),
             pltpu.VMEM(act2, bf16),
+            pltpu.VMEM((HID, CELLS), bf16),
             pltpu.VMEM((HALF, COLS), bf16),
             pltpu.VMEM((HALF, COLS), bf16),
         ],
@@ -485,7 +489,6 @@
             masked,
             from_north,
             from_south,
-            wet,
             masks,
             coef,
             chans,
@@ -495,7 +498,6 @@
             osum,
             in_weight,
             inwt,
-            out_weight.T,
         ],
         [
             ((4 * ROWS, C, COLS), f32),
@@ -504,23 +506,32 @@
             ((HID, CELLS), f32),
             ((CX, CELLS), bf16),
             ((HID, CELLS), bf16),
-            ((HID, CELLS), bf16),
-            ((4, C, COLS), f32),
+            ((PAIRS, C, 2 * COLS), bf16),
+            ((2 * PAIRS + 2, 2 * COLS), f32),
             ((2, HALF, COLS), bf16),
         ],
         time=12.0,
-        limit=20,
+        limit=24,
     )
     cg_north = shifted(cgrad, 1)
     cg_south = shifted(cgrad, -1)
+    (field,) = call(
+        field_kernel,
+        [hbm(act2, bf16)],
+        0,
+        [masked, wet, table, act, out_weight.T],
+        [(act2, f32)],
+        time=1.5,
+        limit=4,
+    )
     (input_grad,) = call(
         back_kernel,
         [hbm(act2, bf16)],
         2,
-        [slot, neighbours, cgrad, cg_north, cg_south, wet, cot, kernel],
-        [((21, 8, COLS), f32), ((3 * ROWS, C, COLS), f32), (act2, f32)],
+        [slot, neighbours, cgrad, cg_north, cg_south, wet, cot, table],
+        [((21, 8, COLS), f32), ((3 * ROWS, C, COLS), f32), (act2, f32), ((TAPS, C, COLS), f32)],
         time=6.0,
-        limit=8,
+        limit=14,
     )
     mine, other = reduce_pack(keep, send)
     total_cells = lax.axis_size(TILE_AXES) * lax.axis_size("rep") * CELLS

time: 102 us -> 89 us (0.87)
  Pallas kernels: 35.7 us -> 22.5 us
  local copies, waits for them, and re-layouts: 4.52 us -> 7.49 us
  waiting for transfers between devices: 9.59 us -> 7.05 us
    pallas_call x7 -> x9, Pallas kernels: 35.7 us -> 22.5 us  [call(): pl.pallas_call(kernel, out_shape=outs, in_specs=[SMEM] * n_smem + [VMEM]...]
    all_to_all x1, waiting for transfers between devices: 2.97 us -> 0.43 us  [exchange(): return lax.all_to_all(value, axes, 0, 0, tiled=True)]
    another operation x0 -> x4, local copies, waits for them, and re-layouts: none -> 2.44 us  [step(): vectors = jnp.stack([conv_bias, ln_gain, ln_shift, out_bias])]
    concatenate x0 -> x1, local copies, waits for them, and re-layouts: none -> 1.17 us  [step(): table = jnp.concatenate([kernel.T, vectors], axis=0).T]
    unnamed x23 -> x31, local copies, waits for them, and re-layouts: 3.99 us -> 3.46 us
  transfers between devices with their start and end apart: 7 -> 7, of which waited for: 3 -> 3; matrix products, arithmetic and copies ran while one was open for 4% -> 5% of each run, Pallas kernels for 15% -> 12%
where the time goes in v3:
time: 89 us; the launch traced here: 88.5 us
  blocking collectives  30.3 us (34%)
  Pallas kernels  22.5 us (25%)
  starting transfers between devices  19.4 us (22%)
  local copies, waits for them, and re-layouts  7.49 us (8%)
  waiting for transfers between devices  7.05 us (8%)
  between operations  0.96 us (1%)
    all_to_all x2, blocking collectives, exchange(): return lax.all_to_all(value, axes, 0, 0, tiled=True)  30.3 us
    pallas_call x9, Pallas kernels, call(): pl.pallas_call(kernel, out_shape=outs, in_specs=[SMEM] * n_smem + [VMEM]...  22.5 us
    ppermute x4, starting transfers between devices, shifted(): lax.ppermute(value, TILE_AXES, [(s, s + steps) for s in range(first, last)])  13.5 us
    all_to_all x1, starting transfers between devices, exchange(): return lax.all_to_all(value, axes, 0, 0, tiled=True)  5.84 us
    ppermute x4, waiting for transfers between devices, shifted(): lax.ppermute(value, TILE_AXES, [(s, s + steps) for s in range(first, last)])  4.9 us
    unnamed x31, local copies, waits for them, and re-layouts  3.46 us
    another operation x4, local copies, waits for them, and re-layouts, step(): vectors = jnp.stack([conv_bias, ln_gain, ln_shift, out_bias])  2.44 us
  transfers between devices with their start and end apart: 7, of which 3 were waited for; matrix products, arithmetic and copies ran while one was open for 5% of the time, Pallas kernels for 12%

profile of v3, /device:TPU:8, one launch (start us, length us, event | category | flops | bytes accessed | tf_op | source)
XLA Modules:
  0.0 88.5 jit_solution(7293527333351898793)
XLA Ops:
  0.7 1.0 %copy-done.2 = bf16[1,1,200,768]{3,2,1,0:T(8,128)(2,1)S(1)} copy-done((bf16[1,1,200,768]{3,2,1,0:T(8,128)(2,1)S(1)}, bf16[1,1,200,768]{3,2,1,0:T(8,128)(2,1)}, u32[]{:S(2)}) %copy-start.2) | copy-done | bytes 307224
  1.7 0.7 copy-done.4
  2.4 0.7 shard_map.195
  3.1 7.2 %collective-permute-start.1 = (bf16[200,768]{1,0:T(8,128)(2,1)S(1)}, bf16[200,768]{1,0:T(8,128)(2,1)S(1)}, u32[]{:S(2)}, u32[]{:S(2)}) collective-permute-start(bf16[200,768]{1,0:T(8,128)(2,1)S(1)} %get-tuple-element.33.own_ref), channel_id=1, source_target_pairs={{4,0},{8,4},{12,8},{16,12},{20,16},{24,20},{28,24},{32,28},{36,32}... | collective-permute-start | bytes 921608 | tf_op jit(solution)/shard_map/ppermute | solution.py:384
  10.3 1.9 %collective-permute-start = (bf16[200,768]{1,0:T(8,128)(2,1)S(1)}, bf16[200,768]{1,0:T(8,128)(2,1)S(1)}, u32[]{:S(2)}, u32[]{:S(2)}) collective-permute-start(bf16[200,768]{1,0:T(8,128)(2,1)S(1)} %get-tuple-element.33.own_ref), channel_id=1, source_target_pairs={{0,4},{4,8},{8,12},{12,16},{16,20},{20,24},{24,28},{28,32},{32,36}... | collective-permute-start | bytes 921608 | tf_op jit(solution)/shard_map/ppermute | solution.py:384
  12.5 0.8 copy.27
  13.3 0.8 copy.28
  14.1 0.8 copy.29
  15.7 1.2 %concatenate.7 = f32[53,200]{0,1:T(8,128)S(1)} concatenate(f32[49,200]{0,1:T(8,128)S(1)} %bitcast.35, f32[1,200]{0,1:T(8,128)S(1)} %copy.26, f32[1,200]{0,1:T(8,128)} %copy.27, f32[1,200]{0,1:T(8,128)} %copy.28, f32[1,200]{0,1:T(8,128)} %copy.29), dimensions={0} | concatenate | bytes 84800 | tf_op jit(solution)/shard_map/concatenate | solution.py:456
  17.1 3.5 %shard_map.196 = (f32[21,8,128]{2,1,0:T(8,128)S(1)}, f32[49,200,128]{2,1,0:T(8,128)S(1)}, f32[4,200,128]{2,1,0:T(8,128)S(1)}, f32[200,768]{1,0:T(8,128)S(1)}, bf...) custom-call(s32[1]{0:T(128)} %bitcast.10.slot_ref, s32[1,8]{1,0:T(1,128)S(1)} %copy-done.5, ...), custom_call_target="tpu_custom_call" | custom-call | flops 6600000000 | bytes 1000000 | tf_op jit(solution)/shard_map/pallas_call | solution.py:366
  20.7 9.4 %shard_map.197 = (bf16[200,768]{1,0:T(8,128)(2,1)S(1)}, bf16[800,768]{1,0:T(8,128)(2,1)S(1)}, bf16[1536,128]{1,0:T(8,128)(2,1)S(1)}, bf16[1536,128]{1,0:T(8,128)(2,1)S(1)}) custom-call(s32[1]{0:T(128)} %bitcast.9.core_ref.refs_0_, bf16[200,768]{1,0:T(8,128)(2,1)S(1)} %get-tuple-element.33.own_ref, bf16[200,768]{1,0:T(8,128)(2,1)S(1)} %collective-permute-done.north_ref, ...), custom_call_target="tpu_custom_call" | custom-call | flops 13200000000 | bytes 1000000 | tf_op jit(solution)/shard_map/pallas_call | solution.py:366
  30.2 1.7 %collective-permute-done.4.got_ref = bf16[1536,128]{1,0:T(8,128)(2,1)S(1)} collective-permute-done((bf16[1536,128]{1,0:T(8,128)(2,1)S(1)}, bf16[1536,128]{1,0:T(8,128)(2,1)S(1)}, u32[]{:S(2)}, u32[]{:S(2)}) %collective-permute-start.4) | collective-permute-done | bytes 393248 | tf_op jit(solution)/shard_map/ppermute | solution.py:419
  32.0 15.3 %all_to_all.23.value_ref = bf16[16,96,128]{2,1,0:T(8,128)(2,1)S(1)} all-to-all(bf16[16,96,128]{2,1,0:T(8,128)(2,1)S(1)} %bitcast.26), channel_id=1, replica_groups=mesh['y'=4,'z'=8,'core'=2,'rep'=4] {'y','rep'}, dimensions={0} | all-to-all | bytes 786432 | tf_op jit(solution)/shard_map/all_to_all | solution.py:388
  47.4 14.9 %all_to_all.24.value_ref = bf16[8,96,128]{2,1,0:T(8,128)(2,1)S(1)} all-to-all(bf16[8,96,128]{2,1,0:T(8,128)(2,1)S(1)} %shard_map.201), channel_id=1, replica_groups=mesh['y'=4,'z'=8,'core'=2,'rep'=4] {'z'}, dimensions={0} | all-to-all | bytes 393216 | tf_op jit(solution)/shard_map/all_to_all | solution.py:388
  62.3 0.8 shard_map.202
  63.1 5.8 %all-to-all-start.2 = ((bf16[16,96,128]{2,1,0:T(8,128)(2,1)}), bf16[16,96,128]{2,1,0:T(8,128)(2,1)S(1)}, u32[]{:S(2)}, u32[]{:S(2)}) async-start(bf16[16,96,128]{2,1,0:T(8,128)(2,1)} %shard_map.202), calls=%async_computation.2 | async-start | bytes 786432 | tf_op jit(solution)/shard_map/all_to_all | solution.py:388
  69.0 1.9 %collective-permute-start.3 = (bf16[200,768]{1,0:T(8,128)(2,1)S(1)}, bf16[200,768]{1,0:T(8,128)(2,1)S(1)}, u32[]{:S(2)}, u32[]{:S(2)}) collective-permute-start(bf16[200,768]{1,0:T(8,128)(2,1)S(1)} %get-tuple-element.45.own_ref), channel_id=1, source_target_pairs={{4,0},{8,4},{12,8},{16,12},{20,16},{24,20},{28,24},{32,28},{36,32}... | collective-permute-start | bytes 921608 | tf_op jit(solution)/shard_map/ppermute | solution.py:384
  70.9 2.4 %collective-permute-start.2 = (bf16[200,768]{1,0:T(8,128)(2,1)S(1)}, bf16[200,768]{1,0:T(8,128)(2,1)S(1)}, u32[]{:S(2)}, u32[]{:S(2)}) collective-permute-start(bf16[200,768]{1,0:T(8,128)(2,1)S(1)} %get-tuple-element.45.own_ref), channel_id=1, source_target_pairs={{0,4},{4,8},{8,12},{12,16},{16,20},{20,24},{24,28},{28,32},{32,36}... | collective-permute-start | bytes 921608 | tf_op jit(solution)/shard_map/ppermute | solution.py:384
  73.3 1.3 %copy-done.7 = bf16[800,768]{1,0:T(8,128)(2,1)S(1)} copy-done((bf16[800,768]{1,0:T(8,128)(2,1)S(1)}, bf16[800,768]{1,0:T(8,128)(2,1)}, u32[]{:S(2)}) %copy-start.7) | copy-done | bytes 1228824
  74.6 1.2 %shard_map.198 = bf16[200,768]{1,0:T(8,128)(2,1)} custom-call(bf16[200,768]{1,0:T(8,128)(2,1)S(1)} %get-tuple-element.33.own_ref, f32[8,768]{1,0:T(8,128)S(1)} %get-tuple-element.34.wet_ref, f32[200,53]{1,0:T(8,128)S(1)} %bitcast.29, bf16[800,768]{1,0:T(8,128)(2,1)S(1)} %copy-done.7, bf16[200,800]{1,0:T(8,128)(2,1)S(1)} %bitcast.27), custom_call_target="tpu_custom_call" | custom-call | flops 1650000000 | bytes 1000000 | tf_op jit(solution)/shard_map/pallas_call | solution.py:366
  76.3 4.9 %collective-permute-done.2.north_ref = bf16[200,768]{1,0:T(8,128)(2,1)S(1)} collective-permute-done((bf16[200,768]{1,0:T(8,128)(2,1)S(1)}, bf16[200,768]{1,0:T(8,128)(2,1)S(1)}, u32[]{:S(2)}, u32[]{:S(2)}) %collective-permute-start.2) | collective-permute-done | bytes 307232 | tf_op jit(solution)/shard_map/ppermute | solution.py:384
  81.2 5.5 %shard_map.199 = bf16[200,768]{1,0:T(8,128)(2,1)} custom-call(s32[1]{0:T(128)} %bitcast.10.slot_ref, s32[1,8]{1,0:T(1,128)S(1)} %copy-done.5, bf16[200,768]{1,0:T(8,128)(2,1)S(1)} %get-tuple-element.45.own_ref, bf16[200,768]{1,0:T(8,128)(2,1)S(1)} %collective-permute-done.2.north_ref, bf16[200,768]{1,0:T(8,128)(2,1)S(1)} %collective-permute-done.3.south_ref, ...), custom_call_target="tpu_custom_call" | custom-call | flops 6600000000 | bytes 1000000 | tf_op jit(solution)/shard_map/pallas_call | solution.py:366
  86.6 1.3 %shard_map.203 = (f32[200,800]{1,0:T(8,128)}, f32[200,800]{1,0:T(8,128)}, f32[49,200]{1,0:T(8,128)}, f32[1,200]{1,0:T(1,128)}, f32[1,200]{1,0:T(1,128)}, /*index...) custom-call(s32[1]{0:T(128)} %bitcast.9.core_ref.refs_0_, bf16[1536,128]{1,0:T(8,128)(2,1)S(1)} %bitcast.25, ...), custom_call_target="tpu_custom_call" | custom-call | flops 1100000000 | bytes 1000000 | tf_op jit(solution)/shard_map/pallas_call | solution.py:366
  87.9 0.6 reduce
  (44 shorter events, 2.0 us)
Async XLA Ops:
  0.6 11.7 %copy-start.10 = (f32[200]{0:T(256)S(1)}, f32[200]{0:T(256)}, u32[]{:S(2)}) copy-start(f32[200]{0:T(256)} %param.16) | copy-start | bytes 2404
  0.7 11.8 %copy-start.11 = (f32[200]{0:T(256)S(1)}, f32[200]{0:T(256)}, u32[]{:S(2)}) copy-start(f32[200]{0:T(256)} %param.17) | copy-start | bytes 2404
  0.7 12.6 %copy-start.12 = (f32[200]{0:T(256)S(1)}, f32[200]{0:T(256)}, u32[]{:S(2)}) copy-start(f32[200]{0:T(256)} %param.18) | copy-start | bytes 2404
  0.7 1.0 %copy-start.2 = (bf16[1,1,200,768]{3,2,1,0:T(8,128)(2,1)S(1)}, bf16[1,1,200,768]{3,2,1,0:T(8,128)(2,1)}, u32[]{:S(2)}) copy-start(bf16[1,1,200,768]{3,2,1,0:T(8,128)(2,1)} %param.12) | copy-start | bytes 921604
  1.7 0.7 copy-start.4
  2.3 9.9 %copy-start.9 = (f32[800]{0:T(1024)S(1)}, f32[800]{0:T(1024)}, u32[]{:S(2)}) copy-start(f32[800]{0:T(1024)} %param.20) | copy-start | bytes 9604
  2.3 9.9 %copy-start.8 = (f32[200,49]{0,1:T(8,128)S(1)}, f32[200,49]{0,1:T(8,128)}, u32[]{:S(2)}) copy-start(f32[200,49]{0,1:T(8,128)} %param.15) | copy-start | bytes 117604
  2.3 11.7 %copy-start.13 = (f32[200]{0:T(256)S(1)}, f32[200]{0:T(256)}, u32[]{:S(2)}) copy-start(f32[200]{0:T(256)} %param.22) | copy-start | bytes 2404
  2.4 12.8 %copy-start = (bf16[200,800]{1,0:T(8,128)(2,1)S(1)}, bf16[200,800]{1,0:T(8,128)(2,1)}, u32[]{:S(2)}) copy-start(bf16[200,800]{1,0:T(8,128)(2,1)} %inw_ref.1) | copy-start | bytes 960004
  3.0 13.9 %copy-start.1 = (bf16[800,200]{0,1:T(8,128)(2,1)S(1)}, bf16[800,200]{0,1:T(8,128)(2,1)}, u32[]{:S(2)}) copy-start(bf16[800,200]{0,1:T(8,128)(2,1)} %param.21) | copy-start | bytes 960004
  3.0 14.1 %copy-start.3 = (bf16[1,1,200,768]{3,2,1,0:T(8,128)(2,1)S(1)}, bf16[1,1,200,768]{3,2,1,0:T(8,128)(2,1)}, u32[]{:S(2)}) copy-start(bf16[1,1,200,768]{3,2,1,0:T(8,128)(2,1)} %param.23) | copy-start | bytes 921604
  3.0 14.1 %copy-start.5 = (s32[1,8]{1,0:T(1,128)S(1)}, s32[1,8]{1,0:T(1,128)}, u32[]{:S(2)}) copy-start(s32[1,8]{1,0:T(1,128)} %near_ref.3) | copy-start | bytes 100
  3.1 17.6 %collective-permute-start.1 = (bf16[200,768]{1,0:T(8,128)(2,1)S(1)}, bf16[200,768]{1,0:T(8,128)(2,1)S(1)}, u32[]{:S(2)}, u32[]{:S(2)}) collective-permute-start(bf16[200,768]{1,0:T(8,128)(2,1)S(1)} %get-tuple-element.33.own_ref), channel_id=1, source_target_pairs={{4,0},{8,4},{12,8},{16,12},{20,16},{24,20},{28,24},{32,28},{36,32}... | collective-permute-start | bytes 921608 | tf_op jit(solution)/shard_map/ppermute | solution.py:384
  10.3 10.4 %collective-permute-start = (bf16[200,768]{1,0:T(8,128)(2,1)S(1)}, bf16[200,768]{1,0:T(8,128)(2,1)S(1)}, u32[]{:S(2)}, u32[]{:S(2)}) collective-permute-start(bf16[200,768]{1,0:T(8,128)(2,1)S(1)} %get-tuple-element.33.own_ref), channel_id=1, source_target_pairs={{0,4},{4,8},{8,12},{12,16},{16,20},{20,24},{24,28},{28,32},{32,36}... | collective-permute-start | bytes 921608 | tf_op jit(solution)/shard_map/ppermute | solution.py:384
  30.1 17.3 %copy-start.6 = (bf16[800,768]{1,0:T(8,128)(2,1)}, bf16[800,768]{1,0:T(8,128)(2,1)S(1)}, u32[]{:S(2)}) copy-start(bf16[800,768]{1,0:T(8,128)(2,1)S(1)} %get-tuple-element.44.act_ref) | copy-start | bytes 3686404
  30.1 1.8 %collective-permute-start.4 = (bf16[1536,128]{1,0:T(8,128)(2,1)S(1)}, bf16[1536,128]{1,0:T(8,128)(2,1)S(1)}, u32[]{:S(2)}, u32[]{:S(2)}) collective-permute-start(bf16[1536,128]{1,0:T(8,128)(2,1)S(1)} %get-tuple-element.47), channel_id=1, source_target_pairs={{0,4},{4,0},{1,5},{5,1},{2,6},{6,2},{3,7},{7,3},{8,12},{12,8},{9,1... | collective-permute-start | bytes 1179656 | tf_op jit(solution)/shard_map/ppermute | solution.py:419
  63.1 13.1 %all-to-all-start.2 = ((bf16[16,96,128]{2,1,0:T(8,128)(2,1)}), bf16[16,96,128]{2,1,0:T(8,128)(2,1)S(1)}, u32[]{:S(2)}, u32[]{:S(2)}) async-start(bf16[16,96,128]{2,1,0:T(8,128)(2,1)} %shard_map.202), calls=%async_computation.2 | async-start | bytes 786432 | tf_op jit(solution)/shard_map/all_to_all | solution.py:388
  69.0 7.3 %collective-permute-start.3 = (bf16[200,768]{1,0:T(8,128)(2,1)S(1)}, bf16[200,768]{1,0:T(8,128)(2,1)S(1)}, u32[]{:S(2)}, u32[]{:S(2)}) collective-permute-start(bf16[200,768]{1,0:T(8,128)(2,1)S(1)} %get-tuple-element.45.own_ref), channel_id=1, source_target_pairs={{4,0},{8,4},{12,8},{16,12},{20,16},{24,20},{28,24},{32,28},{36,32}... | collective-permute-start | bytes 921608 | tf_op jit(solution)/shard_map/ppermute | solution.py:384
  70.9 10.3 %collective-permute-start.2 = (bf16[200,768]{1,0:T(8,128)(2,1)S(1)}, bf16[200,768]{1,0:T(8,128)(2,1)S(1)}, u32[]{:S(2)}, u32[]{:S(2)}) collective-permute-start(bf16[200,768]{1,0:T(8,128)(2,1)S(1)} %get-tuple-element.45.own_ref), channel_id=1, source_target_pairs={{0,4},{4,8},{8,12},{12,16},{16,20},{20,24},{24,28},{28,32},{32,36}... | collective-permute-start | bytes 921608 | tf_op jit(solution)/shard_map/ppermute | solution.py:384
  73.3 1.3 %copy-start.7 = (bf16[800,768]{1,0:T(8,128)(2,1)S(1)}, bf16[800,768]{1,0:T(8,128)(2,1)}, u32[]{:S(2)}) copy-start(bf16[800,768]{1,0:T(8,128)(2,1)} %copy-done.6) | copy-start | bytes 3686404
  76.3 10.4 %collective-permute-start.5 = (bf16[1536,128]{1,0:T(8,128)(2,1)S(1)}, bf16[1536,128]{1,0:T(8,128)(2,1)S(1)}, u32[]{:S(2)}, u32[]{:S(2)}) collective-permute-start(bf16[1536,128]{1,0:T(8,128)(2,1)S(1)} %bitcast.24), channel_id=1, source_target_pairs={{0,4},{4,0},{1,5},{5,1},{2,6},{6,2},{3,7},{7,3},{8,12},{12,8},{9,1... | collective-permute-start | bytes 1179656 | tf_op jit(solution)/shard_map/ppermute | solution.py:425

commit v4 on v3

--- a/solution.py
+++ b/solution.py
@@ -117,8 +117,13 @@
     own_ref,
     wet_ref,
     cot_ref,
+    kern_ref,
+    vec0_ref,
+    vec1_ref,
+    vec2_ref,
+    vec3_ref,
+    outw_ref,
     table_ref,
-    outw_ref,
     masks_ref,
     coef_ref,
     chans_ref,
@@ -127,7 +132,14 @@
     agrad_ref,
     osum_ref,
     rows_ref,
+    flat_ref,
 ):
+    flat_ref[...] = jnp.zeros(flat_ref.shape, f32)
+    flat_ref[0:TAPS, 0:C] = kern_ref[...]
+    for k, vec_ref in enumerate((vec0_ref, vec1_ref, vec2_ref, vec3_ref)):
+        flat_ref[TAPS + k : TAPS + k + 1, 0:C] = vec_ref[...]
+    table_ref[0:COLS, :] = flat_ref[:, 0:COLS].T
+    table_ref[COLS:C, :] = flat_ref[:, COLS:].T[0 : C - COLS, :]
     fill_masks(slot_ref, near_ref, masks_ref)
     fill_rows(own_ref, 0, rows_ref)
     osum = jnp.zeros((C, COLS), f32)
@@ -344,7 +356,7 @@
     for blk in range(BLOCKS):
         begin, end = blk * COLS, min((blk + 1) * COLS, HID)
         gin_ref[:, begin:end] = full_ref[0, blk * CX : blk * CX + C, 0 : end - begin]
-        gbias_ref[0:1, begin:end] = full_ref[0, blk * CX + C : blk * CX + C + 1, 0 : end - begin]
+        gbias_ref[begin:end] = full_ref[0, blk * CX + C, 0 : end - begin]
         gout_ref[:, begin:end] = full_ref[1, blk * CX : blk * CX + C, 0 : end - begin]
     for half, begin, end in ((0, 0, COLS), (1, COLS, C)):
         small = full_ref[half, SMALL : SMALL + 2 * PAIRS + 2, 0 : end - begin]
@@ -361,8 +373,10 @@
     return jax.ShapeDtypeStruct(shape, dtype)
 
 
-def call(kernel, outs, n_smem, args, scratch=(), time=1.0, limit=8):
-    args = list(args[:n_smem]) + [near(x) for x in args[n_smem:]]
+def call(kernel, outs, n_smem, args, scratch=(), time=1.0, limit=8, n_far=None):
+    n_far = n_smem if n_far is None else n_far
+    far = [pltpu.with_memory_space_constraint(x, pltpu.HBM) for x in args[:n_far]]
+    args = far + [near(x) for x in args[n_far:]]
     return pl.pallas_call(
         kernel,
         out_shape=outs,
@@ -421,7 +435,8 @@
     part = exchange(pair, PLANE)
     part = fold(part, PLANE, "z")
     part = exchange(part, "z")
-    mine = exchange(fold(part, "z", PLANE), PLANE)
+    part = fold(part, "z", PLANE)
+    mine = exchange(part, PLANE)
     return mine, lax.ppermute(mine, "core", swap)
 
 
@@ -449,18 +464,19 @@
         1,
         [wet_bits.transpose(2, 0, 1), fields.reshape(act2)],
         limit=4,
+        n_far=2,
     )
     from_north = shifted(masked, 1)
     from_south = shifted(masked, -1)
-    vectors = jnp.stack([conv_bias, ln_gain, ln_shift, out_bias])
-    table = jnp.concatenate([kernel.T, vectors], axis=0).T
+    vectors = [v[None, :] for v in (conv_bias, ln_gain, ln_shift, out_bias)]
     high = lax.reduce_precision(in_bias, 8, 7)
     bias_rows = jnp.stack([high, in_bias - high]).astype(bf16)
     inwt = jnp.concatenate([in_weight, bias_rows, jnp.zeros((CX - C - 2, HID), bf16)], axis=0).T
-    table, inwt = lax.optimization_barrier((table, inwt))
-    masks, coef, chans, part, ograd, agrad, osum = call(
+    cot, inwt = lax.optimization_barrier((cot, inwt))
+    table, masks, coef, chans, part, ograd, agrad, osum = call(
         pre_kernel,
         [
+            pltpu.VMEM((C, COLS), f32),
             pltpu.VMEM((21, 8, COLS), f32),
             pltpu.VMEM((TAPS, C, COLS), f32),
             pltpu.VMEM((4, C, COLS), f32),
@@ -470,8 +486,8 @@
             pltpu.VMEM((C, COLS), f32),
         ],
         2,
-        [slot, neighbours, masked, wet, cot, table, out_weight],
-        [((ROWS, C, COLS), f32)],
+        [slot, neighbours, masked, wet, cot, kernel.T] + vectors + [out_weight],
+        [((ROWS, C, COLS), f32), ((COLS, 2 * COLS), f32)],
         time=6.0,
         limit=8,
     )
@@ -538,7 +554,7 @@
     factor = float(total_cells) ** -0.5
     gin, gout, gkern, gbias, ggain, gshift, gobias, gibias = call(
         lambda *refs: unpack_kernel(factor, *refs),
-        [hbm((C, HID), f32), hbm((C, HID), f32), hbm((TAPS, C), f32)] + [hbm((1, C), f32)] * 4 + [hbm((1, HID), f32)],
+        [hbm((C, HID), f32), hbm((C, HID), f32), hbm((TAPS, C), f32)] + [hbm((1, C), f32)] * 4 + [hbm((HID,), f32)],
         1,
         [core, mine, other],
         [((2, HALF, COLS), f32)],
@@ -552,7 +568,7 @@
         ggain.reshape(C),
         gshift.reshape(C),
         gin,
-        gibias.reshape(HID),
+        gibias,
         gout.T,
         gobias.reshape(C),
     )

time: 89 us -> 84.5 us (0.949)
  local copies, waits for them, and re-layouts: 7.49 us -> 2.12 us
  waiting for transfers between devices: 7.05 us -> 10.4 us
  blocking collectives: 30.3 us -> 27.6 us
    ppermute x4, waiting for transfers between devices: 4.9 us -> 8.3 us  [shifted(): lax.ppermute(value, TILE_AXES, [(s, s + steps) for s in range(first, last)])]
    all_to_all x2, blocking collectives: 30.3 us -> 27.6 us  [exchange(): return lax.all_to_all(value, axes, 0, 0, tiled=True)]
    another operation x4 -> x0, local copies, waits for them, and re-layouts: 2.44 us -> none  [step(): vectors = jnp.stack([conv_bias, ln_gain, ln_shift, out_bias])]
    unnamed x31 -> x24, local copies, waits for them, and re-layouts: 3.46 us -> 1.7 us
    concatenate x1 -> x0, local copies, waits for them, and re-layouts: 1.17 us -> none  [step(): table = jnp.concatenate([kernel.T, vectors], axis=0).T]
  transfers between devices with their start and end apart: 7 -> 7, of which waited for: 3 -> 4; matrix products, arithmetic and copies ran while one was open for 5% -> 1% of each run, Pallas kernels for 12% -> 13%
where the time goes in v4:
time: 84.5 us; the launch traced here: 84.1 us
  blocking collectives  27.6 us (33%)
  Pallas kernels  23.3 us (28%)
  starting transfers between devices  19.4 us (23%)
  waiting for transfers between devices  10.4 us (12%)
  local copies, waits for them, and re-layouts  2.12 us (3%)
  between operations  0.95 us (1%)
    all_to_all x2, blocking collectives, exchange(): return lax.all_to_all(value, axes, 0, 0, tiled=True)  27.6 us
    pallas_call x9, Pallas kernels, call(): pl.pallas_call(kernel, out_shape=outs, in_specs=[SMEM] * n_smem + [VMEM]...  23.3 us
    ppermute x4, starting transfers between devices, shifted(): lax.ppermute(value, TILE_AXES, [(s, s + steps) for s in range(first, last)])  13.5 us
    ppermute x4, waiting for transfers between devices, shifted(): lax.ppermute(value, TILE_AXES, [(s, s + steps) for s in range(first, last)])  8.3 us
    all_to_all x1, starting transfers between devices, exchange(): return lax.all_to_all(value, axes, 0, 0, tiled=True)  5.86 us
    ppermute x1, waiting for transfers between devices, reduce_pack(): got = lax.ppermute(send, 'core', swap)  1.71 us
    unnamed x24, local copies, waits for them, and re-layouts  1.7 us
  transfers between devices with their start and end apart: 7, of which 4 were waited for; matrix products, arithmetic and copies ran while one was open for 1% of the time, Pallas kernels for 13%

profile of v4, /device:TPU:8, one launch (start us, length us, event | category | flops | bytes accessed | tf_op | source)
XLA Modules:
  0.0 84.1 jit_solution(11955607556305264834)
XLA Ops:
  0.7 1.1 %shard_map.195 = (bf16[200,768]{1,0:T(8,128)(2,1)S(1)}, f32[8,768]{1,0:T(8,128)S(1)}) custom-call(s32[5,1,6]{2,1,0:T(1,128)} %bitcast.35, bf16[200,768]{1,0:T(8,128)(2,1)} %bitcast.34), custom_call_target="tpu_custom_call" | custom-call | flops 1100000000 | bytes 1000000 | tf_op jit(solution)/shard_map/pallas_call | solution.py:380
  1.9 7.2 %collective-permute-start.1 = (bf16[200,768]{1,0:T(8,128)(2,1)S(1)}, bf16[200,768]{1,0:T(8,128)(2,1)S(1)}, u32[]{:S(2)}, u32[]{:S(2)}) collective-permute-start(bf16[200,768]{1,0:T(8,128)(2,1)S(1)} %get-tuple-element.34.own_ref), channel_id=1, source_target_pairs={{4,0},{8,4},{12,8},{16,12},{20,16},{24,20},{28,24},{32,28},{36,32}... | collective-permute-start | bytes 921608 | tf_op jit(solution)/shard_map/ppermute | solution.py:398
  9.1 1.9 %collective-permute-start = (bf16[200,768]{1,0:T(8,128)(2,1)S(1)}, bf16[200,768]{1,0:T(8,128)(2,1)S(1)}, u32[]{:S(2)}, u32[]{:S(2)}) collective-permute-start(bf16[200,768]{1,0:T(8,128)(2,1)S(1)} %get-tuple-element.34.own_ref), channel_id=1, source_target_pairs={{0,4},{4,8},{8,12},{12,16},{16,20},{20,24},{24,28},{28,32},{32,36}... | collective-permute-start | bytes 921608 | tf_op jit(solution)/shard_map/ppermute | solution.py:398
  11.1 0.2 stack.12
  11.2 0.2 stack.13
  11.4 0.2 copy.24
  11.7 0.2 maximum_bitcast_fusion.inwt_ref
  11.9 0.2 copy.27.outw_ref
  12.2 3.7 %shard_map.196 = (f32[200,128]{1,0:T(8,128)S(1)}, f32[21,8,128]{2,1,0:T(8,128)S(1)}, f32[49,200,128]{2,1,0:T(8,128)S(1)}, f32[4,200,128]{2,1,0:T(8,128)S(1)}, f3...) custom-call(s32[1]{0:T(128)} %bitcast.2.slot_ref, ...), custom_call_target="tpu_custom_call" | custom-call | flops 6600000000 | bytes 1000000 | tf_op jit(solution)/shard_map/pallas_call | solution.py:380
  16.0 3.4 %collective-permute-done.north_ref = bf16[200,768]{1,0:T(8,128)(2,1)S(1)} collective-permute-done((bf16[200,768]{1,0:T(8,128)(2,1)S(1)}, bf16[200,768]{1,0:T(8,128)(2,1)S(1)}, u32[]{:S(2)}, u32[]{:S(2)}) %collective-permute-start) | collective-permute-done | bytes 307232 | tf_op jit(solution)/shard_map/ppermute | solution.py:398
  19.4 9.4 %shard_map.197 = (bf16[200,768]{1,0:T(8,128)(2,1)S(1)}, bf16[800,768]{1,0:T(8,128)(2,1)S(1)}, bf16[1536,128]{1,0:T(8,128)(2,1)S(1)}, bf16[1536,128]{1,0:T(8,128)(2,1)S(1)}) custom-call(s32[1]{0:T(128)} %bitcast.10.core_ref.refs_0_, bf16[200,768]{1,0:T(8,128)(2,1)S(1)} %get-tuple-element.34.own_ref, bf16[200,768]{1,0:T(8,128)(2,1)S(1)} %collective-permute-done.north_ref, ...), custom_call_target="tpu_custom_call" | custom-call | flops 13200000000 | bytes 1000000 | tf_op jit(solution)/shard_map/pallas_call | solution.py:380
  28.9 1.7 %collective-permute-done.4.got_ref = bf16[1536,128]{1,0:T(8,128)(2,1)S(1)} collective-permute-done((bf16[1536,128]{1,0:T(8,128)(2,1)S(1)}, bf16[1536,128]{1,0:T(8,128)(2,1)S(1)}, u32[]{:S(2)}, u32[]{:S(2)}) %collective-permute-start.4) | collective-permute-done | bytes 393248 | tf_op jit(solution)/shard_map/ppermute | solution.py:433
  30.7 15.3 %all_to_all.23.value_ref = bf16[16,96,128]{2,1,0:T(8,128)(2,1)S(1)} all-to-all(bf16[16,96,128]{2,1,0:T(8,128)(2,1)S(1)} %bitcast.25), channel_id=1, replica_groups=mesh['y'=4,'z'=8,'core'=2,'rep'=4] {'y','rep'}, dimensions={0} | all-to-all | bytes 786432 | tf_op jit(solution)/shard_map/all_to_all | solution.py:402
  46.1 12.3 %all_to_all.24.value_ref = bf16[8,96,128]{2,1,0:T(8,128)(2,1)S(1)} all-to-all(bf16[8,96,128]{2,1,0:T(8,128)(2,1)S(1)} %shard_map.201), channel_id=1, replica_groups=mesh['y'=4,'z'=8,'core'=2,'rep'=4] {'z'}, dimensions={0} | all-to-all | bytes 393216 | tf_op jit(solution)/shard_map/all_to_all | solution.py:402
  58.4 0.8 shard_map.202
  59.2 5.9 %all-to-all-start.2 = ((bf16[16,96,128]{2,1,0:T(8,128)(2,1)}), bf16[16,96,128]{2,1,0:T(8,128)(2,1)S(1)}, u32[]{:S(2)}, u32[]{:S(2)}) async-start(bf16[16,96,128]{2,1,0:T(8,128)(2,1)} %shard_map.202), calls=%async_computation.2 | async-start | bytes 786432 | tf_op jit(solution)/shard_map/all_to_all | solution.py:402
  65.0 1.9 %collective-permute-start.3 = (bf16[200,768]{1,0:T(8,128)(2,1)S(1)}, bf16[200,768]{1,0:T(8,128)(2,1)S(1)}, u32[]{:S(2)}, u32[]{:S(2)}) collective-permute-start(bf16[200,768]{1,0:T(8,128)(2,1)S(1)} %get-tuple-element.47.own_ref), channel_id=1, source_target_pairs={{4,0},{8,4},{12,8},{16,12},{20,16},{24,20},{28,24},{32,28},{36,32}... | collective-permute-start | bytes 921608 | tf_op jit(solution)/shard_map/ppermute | solution.py:398
  66.9 2.4 %collective-permute-start.2 = (bf16[200,768]{1,0:T(8,128)(2,1)S(1)}, bf16[200,768]{1,0:T(8,128)(2,1)S(1)}, u32[]{:S(2)}, u32[]{:S(2)}) collective-permute-start(bf16[200,768]{1,0:T(8,128)(2,1)S(1)} %get-tuple-element.47.own_ref), channel_id=1, source_target_pairs={{0,4},{4,8},{8,12},{12,16},{16,20},{20,24},{24,28},{28,32},{32,36}... | collective-permute-start | bytes 921608 | tf_op jit(solution)/shard_map/ppermute | solution.py:398
  69.4 1.3 %copy-done.9 = bf16[800,768]{1,0:T(8,128)(2,1)S(1)} copy-done((bf16[800,768]{1,0:T(8,128)(2,1)S(1)}, bf16[800,768]{1,0:T(8,128)(2,1)}, u32[]{:S(2)}) %copy-start.9) | copy-done | bytes 1228824
  70.6 1.3 %shard_map.198 = bf16[200,768]{1,0:T(8,128)(2,1)} custom-call(bf16[200,768]{1,0:T(8,128)(2,1)S(1)} %get-tuple-element.34.own_ref, f32[8,768]{1,0:T(8,128)S(1)} %get-tuple-element.35.wet_ref, f32[200,128]{1,0:T(8,128)S(1)} %get-tuple-element.37.table_ref, bf16[800,768]{1,0:T(8,128)(2,1)S(1)} %copy-done.9, bf16[200,800]{1,0:T(8,128)(2,1)S(1)} %bitcast.26), custom_call_target="tpu_custom_call" | custom-call | flops 1650000000 | bytes 1000000 | tf_op jit(solution)/shard_map/pallas_call | solution.py:380
  71.9 0.4 all-to-all-done.2
  72.3 4.9 %collective-permute-done.2.north_ref = bf16[200,768]{1,0:T(8,128)(2,1)S(1)} collective-permute-done((bf16[200,768]{1,0:T(8,128)(2,1)S(1)}, bf16[200,768]{1,0:T(8,128)(2,1)S(1)}, u32[]{:S(2)}, u32[]{:S(2)}) %collective-permute-start.2) | collective-permute-done | bytes 307232 | tf_op jit(solution)/shard_map/ppermute | solution.py:398
  77.2 5.6 %shard_map.199 = bf16[200,768]{1,0:T(8,128)(2,1)} custom-call(s32[1]{0:T(128)} %bitcast.2.slot_ref, s32[1,8]{1,0:T(1,128)} %near_ref.3, bf16[200,768]{1,0:T(8,128)(2,1)S(1)} %get-tuple-element.47.own_ref, bf16[200,768]{1,0:T(8,128)(2,1)S(1)} %collective-permute-done.2.north_ref, bf16[200,768]{1,0:T(8,128)(2,1)S(1)} %collective-permute-done.3.south_ref, ...), custom_call_target="tpu_custom_call" | custom-call | flops 6600000000 | bytes 1000000 | tf_op jit(solution)/shard_map/pallas_call | solution.py:380
  82.8 1.3 %shard_map.203 = (f32[200,800]{1,0:T(8,128)}, f32[200,800]{1,0:T(8,128)}, f32[49,200]{1,0:T(8,128)}, f32[1,200]{1,0:T(1,128)}, f32[1,200]{1,0:T(1,128)}, /*index...) custom-call(s32[1]{0:T(128)} %bitcast.10.core_ref.refs_0_, bf16[1536,128]{1,0:T(8,128)(2,1)S(1)} %bitcast.24, ...), custom_call_target="tpu_custom_call" | custom-call | flops 1100000000 | bytes 1000000 | tf_op jit(solution)/shard_map/pallas_call | solution.py:380
  (31 shorter events, 0.4 us)
Async XLA Ops:
  0.6 10.4 %copy-start.10 = (f32[800]{0:T(1024)S(1)}, f32[800]{0:T(1024)}, u32[]{:S(2)}) copy-start(f32[800]{0:T(1024)} %param.20) | copy-start | bytes 9604
  0.7 10.8 %copy-start = (bf16[200,800]{1,0:T(8,128)(2,1)S(1)}, bf16[200,800]{1,0:T(8,128)(2,1)}, u32[]{:S(2)}) copy-start(bf16[200,800]{1,0:T(8,128)(2,1)} %inw_ref.1) | copy-start | bytes 960004
  0.7 11.3 %copy-start.1 = (bf16[800,200]{0,1:T(8,128)(2,1)S(1)}, bf16[800,200]{0,1:T(8,128)(2,1)}, u32[]{:S(2)}) copy-start(bf16[800,200]{0,1:T(8,128)(2,1)} %param.21) | copy-start | bytes 960004
  1.8 10.3 %copy-start.2 = (bf16[1,1,200,768]{3,2,1,0:T(8,128)(2,1)S(1)}, bf16[1,1,200,768]{3,2,1,0:T(8,128)(2,1)}, u32[]{:S(2)}) copy-start(bf16[1,1,200,768]{3,2,1,0:T(8,128)(2,1)} %param.23) | copy-start | bytes 921604
  1.8 10.3 %copy-start.3 = (f32[200,49]{0,1:T(8,128)S(1)}, f32[200,49]{0,1:T(8,128)}, u32[]{:S(2)}) copy-start(f32[200,49]{0,1:T(8,128)} %param.15) | copy-start | bytes 117604
  1.8 10.3 %copy-start.4 = (f32[200]{0:T(256)S(1)}, f32[200]{0:T(256)}, u32[]{:S(2)}) copy-start(f32[200]{0:T(256)} %param.16) | copy-start | bytes 2404
  1.8 10.3 %copy-start.5 = (f32[200]{0:T(256)S(1)}, f32[200]{0:T(256)}, u32[]{:S(2)}) copy-start(f32[200]{0:T(256)} %param.17) | copy-start | bytes 2404
  1.9 10.3 %copy-start.6 = (f32[200]{0:T(256)S(1)}, f32[200]{0:T(256)}, u32[]{:S(2)}) copy-start(f32[200]{0:T(256)} %param.18) | copy-start | bytes 2404
  1.9 10.3 %copy-start.7 = (f32[200]{0:T(256)S(1)}, f32[200]{0:T(256)}, u32[]{:S(2)}) copy-start(f32[200]{0:T(256)} %param.22) | copy-start | bytes 2404
  1.9 14.1 %collective-permute-start.1 = (bf16[200,768]{1,0:T(8,128)(2,1)S(1)}, bf16[200,768]{1,0:T(8,128)(2,1)S(1)}, u32[]{:S(2)}, u32[]{:S(2)}) collective-permute-start(bf16[200,768]{1,0:T(8,128)(2,1)S(1)} %get-tuple-element.34.own_ref), channel_id=1, source_target_pairs={{4,0},{8,4},{12,8},{16,12},{20,16},{24,20},{28,24},{32,28},{36,32}... | collective-permute-start | bytes 921608 | tf_op jit(solution)/shard_map/ppermute | solution.py:398
  9.1 10.3 %collective-permute-start = (bf16[200,768]{1,0:T(8,128)(2,1)S(1)}, bf16[200,768]{1,0:T(8,128)(2,1)S(1)}, u32[]{:S(2)}, u32[]{:S(2)}) collective-permute-start(bf16[200,768]{1,0:T(8,128)(2,1)S(1)} %get-tuple-element.34.own_ref), channel_id=1, source_target_pairs={{0,4},{4,8},{8,12},{12,16},{16,20},{20,24},{24,28},{28,32},{32,36}... | collective-permute-start | bytes 921608 | tf_op jit(solution)/shard_map/ppermute | solution.py:398
  28.8 17.3 %copy-start.8 = (bf16[800,768]{1,0:T(8,128)(2,1)}, bf16[800,768]{1,0:T(8,128)(2,1)S(1)}, u32[]{:S(2)}) copy-start(bf16[800,768]{1,0:T(8,128)(2,1)S(1)} %get-tuple-element.46.act_ref) | copy-start | bytes 3686404
  28.8 1.8 %collective-permute-start.4 = (bf16[1536,128]{1,0:T(8,128)(2,1)S(1)}, bf16[1536,128]{1,0:T(8,128)(2,1)S(1)}, u32[]{:S(2)}, u32[]{:S(2)}) collective-permute-start(bf16[1536,128]{1,0:T(8,128)(2,1)S(1)} %get-tuple-element.49), channel_id=1, source_target_pairs={{0,4},{4,0},{1,5},{5,1},{2,6},{6,2},{3,7},{7,3},{8,12},{12,8},{9,1... | collective-permute-start | bytes 1179656 | tf_op jit(solution)/shard_map/ppermute | solution.py:433
  59.2 13.2 %all-to-all-start.2 = ((bf16[16,96,128]{2,1,0:T(8,128)(2,1)}), bf16[16,96,128]{2,1,0:T(8,128)(2,1)S(1)}, u32[]{:S(2)}, u32[]{:S(2)}) async-start(bf16[16,96,128]{2,1,0:T(8,128)(2,1)} %shard_map.202), calls=%async_computation.2 | async-start | bytes 786432 | tf_op jit(solution)/shard_map/all_to_all | solution.py:402
  65.0 7.3 %collective-permute-start.3 = (bf16[200,768]{1,0:T(8,128)(2,1)S(1)}, bf16[200,768]{1,0:T(8,128)(2,1)S(1)}, u32[]{:S(2)}, u32[]{:S(2)}) collective-permute-start(bf16[200,768]{1,0:T(8,128)(2,1)S(1)} %get-tuple-element.47.own_ref), channel_id=1, source_target_pairs={{4,0},{8,4},{12,8},{16,12},{20,16},{24,20},{28,24},{32,28},{36,32}... | collective-permute-start | bytes 921608 | tf_op jit(solution)/shard_map/ppermute | solution.py:398
  66.9 10.3 %collective-permute-start.2 = (bf16[200,768]{1,0:T(8,128)(2,1)S(1)}, bf16[200,768]{1,0:T(8,128)(2,1)S(1)}, u32[]{:S(2)}, u32[]{:S(2)}) collective-permute-start(bf16[200,768]{1,0:T(8,128)(2,1)S(1)} %get-tuple-element.47.own_ref), channel_id=1, source_target_pairs={{0,4},{4,8},{8,12},{12,16},{16,20},{20,24},{24,28},{28,32},{32,36}... | collective-permute-start | bytes 921608 | tf_op jit(solution)/shard_map/ppermute | solution.py:398
  69.3 1.3 %copy-start.9 = (bf16[800,768]{1,0:T(8,128)(2,1)S(1)}, bf16[800,768]{1,0:T(8,128)(2,1)}, u32[]{:S(2)}) copy-start(bf16[800,768]{1,0:T(8,128)(2,1)} %copy-done.8) | copy-start | bytes 3686404
  72.3 10.5 %collective-permute-start.5 = (bf16[1536,128]{1,0:T(8,128)(2,1)S(1)}, bf16[1536,128]{1,0:T(8,128)(2,1)S(1)}, u32[]{:S(2)}, u32[]{:S(2)}) collective-permute-start(bf16[1536,128]{1,0:T(8,128)(2,1)S(1)} %bitcast.23), channel_id=1, source_target_pairs={{0,4},{4,0},{1,5},{5,1},{2,6},{6,2},{3,7},{7,3},{8,12},{12,8},{9,1... | collective-permute-start | bytes 1179656 | tf_op jit(solution)/shard_map/ppermute | solution.py:440

commit v5 on v4

--- a/solution.py
+++ b/solution.py
@@ -17,8 +17,9 @@
 TAPS = 49
 GROUPS = C // 8
 BLOCKS = 7
-HALF = 1536
-SMALL = BLOCKS * CX
+HALF = 1408
+SMALL = HID - 6 * COLS
+VECTORS = SMALL + TAPS
 PAIRS = 27
 MIB = 1 << 20
 UNROLL = 5
@@ -183,13 +184,13 @@
     keep_ref,
     send_ref,
     rows_ref,
+    vecs_ref,
     conv_ref,
     istd_ref,
     hid_ref,
     norm_ref,
     hgrad_ref,
-    sums_ref,
-    small_ref,
+    bias_ref,
     pack_ref,
 ):
     fill_rows(north_ref, NORTH, rows_ref)
@@ -253,7 +254,35 @@
         cgrad_ref[:, lanes(r)] = cg
         rows_ref[cg_base + r] = cg.astype(f32)
         bsum = bsum + cg.astype(f32)
-    for s, vec in enumerate((bsum, gsum, ssum, osum_ref[...], jnp.zeros((C, COLS), f32))):
+    for s, vec in enumerate((bsum, gsum, ssum, osum_ref[...])):
+        vecs_ref[s] = vec
+
+    bias_ref[...] = jnp.zeros(bias_ref.shape, f32)
+
+    for half, (left_ref, right_ref) in enumerate(((norm_ref, hgrad_ref), (ograd_ref, act_ref))):
+        for first in range(0, HID, 2 * COLS):
+            last = min(first + 2 * COLS, HID)
+            blk = first // COLS
+            part = lax.dot_general(left_ref[...], right_ref[first:last, :], NT_DIMS, preferred_element_type=f32)
+            if last - first < COLS:
+                part = jnp.concatenate([part, jnp.zeros((CX, COLS - (last - first)), f32)], axis=1)
+            for sub in range(max(1, (last - first) // COLS)):
+                piece = part[:, lanes(sub)]
+                if half == 0:
+                    bias_ref[blk + sub : blk + sub + 1, :] = piece[C : C + 1, :]
+                piece = piece[0:C, :]
+                pack_ref[half, (blk + sub) * C : (blk + sub + 1) * C, :] = piece.astype(bf16)
+    pack_ref[0, BLOCKS * C :, :] = bias_ref[...].astype(bf16)
+    pack_ref[1, BLOCKS * C :, :] = jnp.zeros((8, COLS), bf16)
+    core = core_ref[0]
+    keep_ref[...] = pack_ref[core]
+    send_ref[...] = pack_ref[1 - core]
+
+
+def taps_kernel(rows_ref, masks_ref, vecs_ref, out_ref, sums_ref, small_ref):
+    cg_base = 3 * ROWS
+    for s in range(5):
+        vec = vecs_ref[s] if s < 4 else jnp.zeros((C, COLS), f32)
         sums_ref[(TAPS + s) // 2, :, lanes((TAPS + s) % 2)] = vec.astype(bf16)
 
     def tap_step(g, carry):
@@ -282,23 +311,9 @@
     small_ref[...] = jnp.zeros(small_ref.shape, f32)
     for k in range(PAIRS):
         both = lax.dot_general(pick, sums_ref[k], NT_DIMS, preferred_element_type=f32)
-        small_ref[2 * k : 2 * k + 2, 0:C] = both[0:2, :]
-
-    for half, (left_ref, right_ref) in enumerate(((norm_ref, hgrad_ref), (ograd_ref, act_ref))):
-        for first in range(0, HID, 2 * COLS):
-            last = min(first + 2 * COLS, HID)
-            blk = first // COLS
-            part = lax.dot_general(left_ref[...], right_ref[first:last, :], NT_DIMS, preferred_element_type=f32)
-            if last - first < COLS:
-                part = jnp.concatenate([part, jnp.zeros((CX, COLS - (last - first)), f32)], axis=1)
-            pack_ref[half, blk * CX : (blk + 1) * CX, :] = part[:, 0:COLS].astype(bf16)
-            if last - first > COLS:
-                pack_ref[half, (blk + 1) * CX : (blk + 2) * CX, :] = part[:, COLS:].astype(bf16)
-        pack_ref[half, SMALL : SMALL + 2 * PAIRS + 2, :] = small_ref[:, lanes(half)].astype(bf16)
-        pack_ref[half, SMALL + 2 * PAIRS + 2 :, :] = jnp.zeros((HALF - SMALL - 2 * PAIRS - 2, COLS), bf16)
-    core = core_ref[0]
-    keep_ref[...] = pack_ref[core]
-    send_ref[...] = pack_ref[1 - core]
+        small_ref[SMALL + 2 * k : SMALL + 2 * k + 2, 0:C] = both[0:2, :]
+    out_ref[0:COLS, :] = small_ref[:, 0:COLS].T
+    out_ref[COLS:, :] = small_ref[:, COLS:].T[0 : C - COLS, :]
 
 
 def field_kernel(own_ref, wet_ref, table_ref, act_ref, outwt_ref, field_ref, hid_ref):
@@ -355,14 +370,14 @@
     full_ref[1 - core] = other_ref[...].astype(f32) * factor
     for blk in range(BLOCKS):
         begin, end = blk * COLS, min((blk + 1) * COLS, HID)
-        gin_ref[:, begin:end] = full_ref[0, blk * CX : blk * CX + C, 0 : end - begin]
-        gbias_ref[begin:end] = full_ref[0, blk * CX + C, 0 : end - begin]
-        gout_ref[:, begin:end] = full_ref[1, blk * CX : blk * CX + C, 0 : end - begin]
-    for half, begin, end in ((0, 0, COLS), (1, COLS, C)):
-        small = full_ref[half, SMALL : SMALL + 2 * PAIRS + 2, 0 : end - begin]
-        gkern_ref[:, begin:end] = small[0:TAPS]
-        for s, ref in enumerate(vec_refs):
-            ref[:, begin:end] = small[TAPS + s : TAPS + s + 1]
+        gin_ref[:, begin:end] = full_ref[0, blk * C : (blk + 1) * C, 0 : end - begin]
+        gbias_ref[begin:end] = full_ref[0, BLOCKS * C + blk, 0 : end - begin]
+        gout_ref[:, begin:end] = full_ref[1, blk * C : (blk + 1) * C, 0 : end - begin]
+    last = slice((BLOCKS - 1) * C, BLOCKS * C)
+    columns = (full_ref[0, last, :] + full_ref[1, last, :]).T
+    gkern_ref[...] = columns[SMALL:VECTORS, :]
+    for s, ref in enumerate(vec_refs):
+        ref[...] = columns[VECTORS + s : VECTORS + s + 1, :]
 
 
 def near(x):
@@ -402,8 +417,11 @@
     return lax.all_to_all(value, axes, 0, 0, tiled=True)
 
 
-def add_kernel(keep_ref, got_ref, pair_ref):
-    pair_ref[...] = (keep_ref[...].astype(f32) + got_ref[...].astype(f32)).astype(bf16)
+def add_kernel(keep_ref, got_ref, small_ref, pair_ref):
+    last = (BLOCKS - 1) * C
+    total = keep_ref[...].astype(f32) + got_ref[...].astype(f32)
+    pair_ref[...] = total.astype(bf16)
+    pair_ref[last : last + C, :] = (total[last : last + C, :] + small_ref[...]).astype(bf16)
 
 
 def fold_kernel(value_ref, copies_ref):
@@ -428,10 +446,10 @@
     return out.reshape(copies * rows, COLS)
 
 
-def reduce_pack(keep, send):
+def reduce_pack(keep, send, small):
     swap = [(0, 1), (1, 0)]
     got = lax.ppermute(send, "core", swap)
-    (pair,) = call(add_kernel, [pltpu.VMEM((HALF, COLS), bf16)], 0, [keep, got], limit=4)
+    (pair,) = call(add_kernel, [pltpu.VMEM((HALF, COLS), bf16)], 0, [keep, got, small], limit=4)
     part = exchange(pair, PLANE)
     part = fold(part, PLANE, "z")
     part = exchange(part, "z")
@@ -491,13 +509,15 @@
         time=6.0,
         limit=8,
     )
-    cgrad, act, keep, send = call(
+    cgrad, act, keep, send, rows, vecs = call(
         main_kernel,
         [
             pltpu.VMEM(act2, bf16),
             pltpu.VMEM((HID, CELLS), bf16),
             pltpu.VMEM((HALF, COLS), bf16),
             pltpu.VMEM((HALF, COLS), bf16),
+            pltpu.VMEM((4 * ROWS, C, COLS), f32),
+            pltpu.VMEM((4, C, COLS), f32),
         ],
         1,
         [
@@ -516,21 +536,28 @@
             inwt,
         ],
         [
-            ((4 * ROWS, C, COLS), f32),
             (act2, f32),
             ((8, CELLS), f32),
             ((HID, CELLS), f32),
             ((CX, CELLS), bf16),
             ((HID, CELLS), bf16),
-            ((PAIRS, C, 2 * COLS), bf16),
-            ((2 * PAIRS + 2, 2 * COLS), f32),
+            ((8, COLS), f32),
             ((2, HALF, COLS), bf16),
         ],
         time=12.0,
-        limit=24,
+        limit=20,
     )
     cg_north = shifted(cgrad, 1)
     cg_south = shifted(cgrad, -1)
+    (small,) = call(
+        taps_kernel,
+        [pltpu.VMEM((C, COLS), f32)],
+        0,
+        [rows, masks, vecs],
+        [((PAIRS, C, 2 * COLS), bf16), ((COLS, 2 * COLS), f32)],
+        time=3.0,
+        limit=12,
+    )
     (field,) = call(
         field_kernel,
         [hbm(act2, bf16)],
@@ -549,7 +576,7 @@
         time=6.0,
         limit=14,
     )
-    mine, other = reduce_pack(keep, send)
+    mine, other = reduce_pack(keep, send, small)
     total_cells = lax.axis_size(TILE_AXES) * lax.axis_size("rep") * CELLS
     factor = float(total_cells) ** -0.5
     gin, gout, gkern, gbias, ggain, gshift, gobias, gibias = call(

time: 84.5 us -> 82.8 us (0.980)
  waiting for transfers between devices: 10.4 us -> 8.74 us
    ppermute x1, waiting for transfers between devices: 1.71 us -> 0.01 us  [reduce_pack(): got = lax.ppermute(send, 'core', swap)]
    pallas_call x9 -> x10, Pallas kernels: 23.3 us -> 23.4 us  [call(): pl.pallas_call(kernel, out_shape=outs, in_specs=[SMEM] * n_smem + [VMEM]...]
  transfers between devices with their start and end apart: 7 -> 7, of which waited for: 4 -> 3; matrix products, arithmetic and copies ran while one was open for 1% -> 1% of each run, Pallas kernels for 13% -> 18%
where the time goes in v5:
time: 82.8 us; the launch traced here: 82.3 us
  blocking collectives  27.5 us (33%)
  Pallas kernels  23.4 us (28%)
  starting transfers between devices  19.3 us (23%)
  waiting for transfers between devices  8.74 us (11%)
  local copies, waits for them, and re-layouts  2.12 us (3%)
  between operations  0.97 us (1%)
    all_to_all x2, blocking collectives, exchange(): return lax.all_to_all(value, axes, 0, 0, tiled=True)  27.5 us
    pallas_call x10, Pallas kernels, call(): pl.pallas_call(kernel, out_shape=outs, in_specs=[SMEM] * n_smem + [VMEM]...  23.4 us
    ppermute x4, starting transfers between devices, shifted(): lax.ppermute(value, TILE_AXES, [(s, s + steps) for s in range(first, last)])  13.5 us
    ppermute x4, waiting for transfers between devices, shifted(): lax.ppermute(value, TILE_AXES, [(s, s + steps) for s in range(first, last)])  8.47 us
    all_to_all x1, starting transfers between devices, exchange(): return lax.all_to_all(value, axes, 0, 0, tiled=True)  5.79 us
    unnamed x24, local copies, waits for them, and re-layouts  1.7 us
  transfers between devices with their start and end apart: 7, of which 3 were waited for; matrix products, arithmetic and copies ran while one was open for 1% of the time, Pallas kernels for 18%

profile of v5, /device:TPU:8, one launch (start us, length us, event | category | flops | bytes accessed | tf_op | source)
XLA Modules:
  0.0 82.3 jit_solution(495043465433919821)
XLA Ops:
  0.7 1.1 %shard_map.195 = (bf16[200,768]{1,0:T(8,128)(2,1)S(1)}, f32[8,768]{1,0:T(8,128)S(1)}) custom-call(s32[5,1,6]{2,1,0:T(1,128)} %bitcast.35, bf16[200,768]{1,0:T(8,128)(2,1)} %bitcast.34), custom_call_target="tpu_custom_call" | custom-call | flops 1100000000 | bytes 1000000 | tf_op jit(solution)/shard_map/pallas_call | solution.py:395
  1.9 7.2 %collective-permute-start.1 = (bf16[200,768]{1,0:T(8,128)(2,1)S(1)}, bf16[200,768]{1,0:T(8,128)(2,1)S(1)}, u32[]{:S(2)}, u32[]{:S(2)}) collective-permute-start(bf16[200,768]{1,0:T(8,128)(2,1)S(1)} %get-tuple-element.36.own_ref), channel_id=1, source_target_pairs={{4,0},{8,4},{12,8},{16,12},{20,16},{24,20},{28,24},{32,28},{36,32}... | collective-permute-start | bytes 921608 | tf_op jit(solution)/shard_map/ppermute | solution.py:413
  9.1 1.9 %collective-permute-start = (bf16[200,768]{1,0:T(8,128)(2,1)S(1)}, bf16[200,768]{1,0:T(8,128)(2,1)S(1)}, u32[]{:S(2)}, u32[]{:S(2)}) collective-permute-start(bf16[200,768]{1,0:T(8,128)(2,1)S(1)} %get-tuple-element.36.own_ref), channel_id=1, source_target_pairs={{0,4},{4,8},{8,12},{12,16},{16,20},{20,24},{24,28},{28,32},{32,36}... | collective-permute-start | bytes 921608 | tf_op jit(solution)/shard_map/ppermute | solution.py:413
  11.1 0.2 stack.12
  11.2 0.2 stack.13
  11.4 0.2 copy.24
  11.7 0.2 maximum_bitcast_fusion.inwt_ref
  11.9 0.2 copy.27.outw_ref
  12.2 3.8 %shard_map.196 = (f32[200,128]{1,0:T(8,128)S(1)}, f32[21,8,128]{2,1,0:T(8,128)S(1)}, f32[49,200,128]{2,1,0:T(8,128)S(1)}, f32[4,200,128]{2,1,0:T(8,128)S(1)}, f3...) custom-call(s32[1]{0:T(128)} %bitcast.2.slot_ref, ...), custom_call_target="tpu_custom_call" | custom-call | flops 6600000000 | bytes 1000000 | tf_op jit(solution)/shard_map/pallas_call | solution.py:395
  16.0 3.4 %collective-permute-done.north_ref = bf16[200,768]{1,0:T(8,128)(2,1)S(1)} collective-permute-done((bf16[200,768]{1,0:T(8,128)(2,1)S(1)}, bf16[200,768]{1,0:T(8,128)(2,1)S(1)}, u32[]{:S(2)}, u32[]{:S(2)}) %collective-permute-start) | collective-permute-done | bytes 307232 | tf_op jit(solution)/shard_map/ppermute | solution.py:413
  19.4 5.7 %shard_map.197 = (bf16[200,768]{1,0:T(8,128)(2,1)S(1)}, bf16[800,768]{1,0:T(8,128)(2,1)S(1)}, bf16[1408,128]{1,0:T(8,128)(2,1)S(1)}, bf16[1408,128]{1,0:T(8,128)...) custom-call(s32[1]{0:T(128)} %bitcast.10.core_ref.refs_0_, ...), custom_call_target="tpu_custom_call" | custom-call | flops 13200000000 | bytes 1000000 | tf_op jit(solution)/shard_map/pallas_call | solution.py:395
  25.2 3.8 %shard_map.200.small_ref = f32[200,128]{1,0:T(8,128)S(1)} custom-call(f32[24,200,128]{2,1,0:T(8,128)S(1)} %get-tuple-element.52.rows_ref, f32[21,8,128]{2,1,0:T(8,128)S(1)} %get-tuple-element.40.masks_ref, f32[4,200,128]{2,1,0:T(8,128)S(1)} %get-tuple-element.53.vecs_ref), custom_call_target="tpu_custom_call" | custom-call | flops 3300000000 | bytes 1000000 | tf_op jit(solution)/shard_map/pallas_call | solution.py:395
  29.1 15.3 %all_to_all.23.value_ref = bf16[16,88,128]{2,1,0:T(8,128)(2,1)S(1)} all-to-all(bf16[16,88,128]{2,1,0:T(8,128)(2,1)S(1)} %bitcast.25), channel_id=1, replica_groups=mesh['y'=4,'z'=8,'core'=2,'rep'=4] {'y','rep'}, dimensions={0} | all-to-all | bytes 720896 | tf_op jit(solution)/shard_map/all_to_all | solution.py:417
  44.5 12.2 %all_to_all.24.value_ref = bf16[8,88,128]{2,1,0:T(8,128)(2,1)S(1)} all-to-all(bf16[8,88,128]{2,1,0:T(8,128)(2,1)S(1)} %shard_map.202), channel_id=1, replica_groups=mesh['y'=4,'z'=8,'core'=2,'rep'=4] {'z'}, dimensions={0} | all-to-all | bytes 360448 | tf_op jit(solution)/shard_map/all_to_all | solution.py:417
  56.7 0.8 shard_map.203
  57.5 5.8 %all-to-all-start.2 = ((bf16[16,88,128]{2,1,0:T(8,128)(2,1)}), bf16[16,88,128]{2,1,0:T(8,128)(2,1)S(1)}, u32[]{:S(2)}, u32[]{:S(2)}) async-start(bf16[16,88,128]{2,1,0:T(8,128)(2,1)} %shard_map.203), calls=%async_computation.2 | async-start | bytes 720896 | tf_op jit(solution)/shard_map/all_to_all | solution.py:417
  63.2 1.9 %collective-permute-start.3 = (bf16[200,768]{1,0:T(8,128)(2,1)S(1)}, bf16[200,768]{1,0:T(8,128)(2,1)S(1)}, u32[]{:S(2)}, u32[]{:S(2)}) collective-permute-start(bf16[200,768]{1,0:T(8,128)(2,1)S(1)} %get-tuple-element.49.own_ref), channel_id=1, source_target_pairs={{4,0},{8,4},{12,8},{16,12},{20,16},{24,20},{28,24},{32,28},{36,32}... | collective-permute-start | bytes 921608 | tf_op jit(solution)/shard_map/ppermute | solution.py:413
  65.2 2.4 %collective-permute-start.2 = (bf16[200,768]{1,0:T(8,128)(2,1)S(1)}, bf16[200,768]{1,0:T(8,128)(2,1)S(1)}, u32[]{:S(2)}, u32[]{:S(2)}) collective-permute-start(bf16[200,768]{1,0:T(8,128)(2,1)S(1)} %get-tuple-element.49.own_ref), channel_id=1, source_target_pairs={{0,4},{4,8},{8,12},{12,16},{16,20},{20,24},{24,28},{28,32},{32,36}... | collective-permute-start | bytes 921608 | tf_op jit(solution)/shard_map/ppermute | solution.py:413
  67.6 1.3 %copy-done.9 = bf16[800,768]{1,0:T(8,128)(2,1)S(1)} copy-done((bf16[800,768]{1,0:T(8,128)(2,1)S(1)}, bf16[800,768]{1,0:T(8,128)(2,1)}, u32[]{:S(2)}) %copy-start.9) | copy-done | bytes 1228824
  68.9 1.3 %shard_map.198 = bf16[200,768]{1,0:T(8,128)(2,1)} custom-call(bf16[200,768]{1,0:T(8,128)(2,1)S(1)} %get-tuple-element.36.own_ref, f32[8,768]{1,0:T(8,128)S(1)} %get-tuple-element.37.wet_ref, f32[200,128]{1,0:T(8,128)S(1)} %get-tuple-element.39.table_ref, bf16[800,768]{1,0:T(8,128)(2,1)S(1)} %copy-done.9, bf16[200,800]{1,0:T(8,128)(2,1)S(1)} %bitcast.26), custom_call_target="tpu_custom_call" | custom-call | flops 1650000000 | bytes 1000000 | tf_op jit(solution)/shard_map/pallas_call | solution.py:395
  70.1 0.3 all-to-all-done.2
  70.4 5.1 %collective-permute-done.2.north_ref = bf16[200,768]{1,0:T(8,128)(2,1)S(1)} collective-permute-done((bf16[200,768]{1,0:T(8,128)(2,1)S(1)}, bf16[200,768]{1,0:T(8,128)(2,1)S(1)}, u32[]{:S(2)}, u32[]{:S(2)}) %collective-permute-start.2) | collective-permute-done | bytes 307232 | tf_op jit(solution)/shard_map/ppermute | solution.py:413
  75.4 5.6 %shard_map.199 = bf16[200,768]{1,0:T(8,128)(2,1)} custom-call(s32[1]{0:T(128)} %bitcast.2.slot_ref, s32[1,8]{1,0:T(1,128)} %near_ref.3, bf16[200,768]{1,0:T(8,128)(2,1)S(1)} %get-tuple-element.49.own_ref, bf16[200,768]{1,0:T(8,128)(2,1)S(1)} %collective-permute-done.2.north_ref, bf16[200,768]{1,0:T(8,128)(2,1)S(1)} %collective-permute-done.3.south_ref, ...), custom_call_target="tpu_custom_call" | custom-call | flops 6600000000 | bytes 1000000 | tf_op jit(solution)/shard_map/pallas_call | solution.py:395
  81.0 1.3 %shard_map.204 = (f32[200,800]{1,0:T(8,128)}, f32[200,800]{1,0:T(8,128)}, f32[49,200]{1,0:T(8,128)}, f32[1,200]{1,0:T(1,128)}, f32[1,200]{1,0:T(1,128)}, /*index...) custom-call(s32[1]{0:T(128)} %bitcast.10.core_ref.refs_0_, bf16[1408,128]{1,0:T(8,128)(2,1)S(1)} %bitcast.24, ...), custom_call_target="tpu_custom_call" | custom-call | flops 1100000000 | bytes 1000000 | tf_op jit(solution)/shard_map/pallas_call | solution.py:395
  (32 shorter events, 0.4 us)
Async XLA Ops:
  0.6 10.4 %copy-start.10 = (f32[800]{0:T(1024)S(1)}, f32[800]{0:T(1024)}, u32[]{:S(2)}) copy-start(f32[800]{0:T(1024)} %param.20) | copy-start | bytes 9604
  0.7 10.8 %copy-start = (bf16[200,800]{1,0:T(8,128)(2,1)S(1)}, bf16[200,800]{1,0:T(8,128)(2,1)}, u32[]{:S(2)}) copy-start(bf16[200,800]{1,0:T(8,128)(2,1)} %inw_ref.1) | copy-start | bytes 960004
  0.7 11.3 %copy-start.1 = (bf16[800,200]{0,1:T(8,128)(2,1)S(1)}, bf16[800,200]{0,1:T(8,128)(2,1)}, u32[]{:S(2)}) copy-start(bf16[800,200]{0,1:T(8,128)(2,1)} %param.21) | copy-start | bytes 960004
  1.8 10.3 %copy-start.2 = (bf16[1,1,200,768]{3,2,1,0:T(8,128)(2,1)S(1)}, bf16[1,1,200,768]{3,2,1,0:T(8,128)(2,1)}, u32[]{:S(2)}) copy-start(bf16[1,1,200,768]{3,2,1,0:T(8,128)(2,1)} %param.23) | copy-start | bytes 921604
  1.8 10.3 %copy-start.3 = (f32[200,49]{0,1:T(8,128)S(1)}, f32[200,49]{0,1:T(8,128)}, u32[]{:S(2)}) copy-start(f32[200,49]{0,1:T(8,128)} %param.15) | copy-start | bytes 117604
  1.8 10.3 %copy-start.4 = (f32[200]{0:T(256)S(1)}, f32[200]{0:T(256)}, u32[]{:S(2)}) copy-start(f32[200]{0:T(256)} %param.16) | copy-start | bytes 2404
  1.8 10.3 %copy-start.5 = (f32[200]{0:T(256)S(1)}, f32[200]{0:T(256)}, u32[]{:S(2)}) copy-start(f32[200]{0:T(256)} %param.17) | copy-start | bytes 2404
  1.9 10.3 %copy-start.6 = (f32[200]{0:T(256)S(1)}, f32[200]{0:T(256)}, u32[]{:S(2)}) copy-start(f32[200]{0:T(256)} %param.18) | copy-start | bytes 2404
  1.9 10.3 %copy-start.7 = (f32[200]{0:T(256)S(1)}, f32[200]{0:T(256)}, u32[]{:S(2)}) copy-start(f32[200]{0:T(256)} %param.22) | copy-start | bytes 2404
  1.9 14.1 %collective-permute-start.1 = (bf16[200,768]{1,0:T(8,128)(2,1)S(1)}, bf16[200,768]{1,0:T(8,128)(2,1)S(1)}, u32[]{:S(2)}, u32[]{:S(2)}) collective-permute-start(bf16[200,768]{1,0:T(8,128)(2,1)S(1)} %get-tuple-element.36.own_ref), channel_id=1, source_target_pairs={{4,0},{8,4},{12,8},{16,12},{20,16},{24,20},{28,24},{32,28},{36,32}... | collective-permute-start | bytes 921608 | tf_op jit(solution)/shard_map/ppermute | solution.py:413
  9.1 10.3 %collective-permute-start = (bf16[200,768]{1,0:T(8,128)(2,1)S(1)}, bf16[200,768]{1,0:T(8,128)(2,1)S(1)}, u32[]{:S(2)}, u32[]{:S(2)}) collective-permute-start(bf16[200,768]{1,0:T(8,128)(2,1)S(1)} %get-tuple-element.36.own_ref), channel_id=1, source_target_pairs={{0,4},{4,8},{8,12},{12,16},{16,20},{20,24},{24,28},{28,32},{32,36}... | collective-permute-start | bytes 921608 | tf_op jit(solution)/shard_map/ppermute | solution.py:413
  25.1 3.9 %copy-start.8 = (bf16[800,768]{1,0:T(8,128)(2,1)}, bf16[800,768]{1,0:T(8,128)(2,1)S(1)}, u32[]{:S(2)}) copy-start(bf16[800,768]{1,0:T(8,128)(2,1)S(1)} %get-tuple-element.48.act_ref) | copy-start | bytes 3686404
  25.1 3.9 %collective-permute-start.4 = (bf16[1408,128]{1,0:T(8,128)(2,1)S(1)}, bf16[1408,128]{1,0:T(8,128)(2,1)S(1)}, u32[]{:S(2)}, u32[]{:S(2)}) collective-permute-start(bf16[1408,128]{1,0:T(8,128)(2,1)S(1)} %get-tuple-element.51), channel_id=1, source_target_pairs={{0,4},{4,0},{1,5},{5,1},{2,6},{6,2},{3,7},{7,3},{8,12},{12,8},{9,1... | collective-permute-start | bytes 1081352 | tf_op jit(solution)/shard_map/ppermute | solution.py:451
  57.5 12.9 %all-to-all-start.2 = ((bf16[16,88,128]{2,1,0:T(8,128)(2,1)}), bf16[16,88,128]{2,1,0:T(8,128)(2,1)S(1)}, u32[]{:S(2)}, u32[]{:S(2)}) async-start(bf16[16,88,128]{2,1,0:T(8,128)(2,1)} %shard_map.203), calls=%async_computation.2 | async-start | bytes 720896 | tf_op jit(solution)/shard_map/all_to_all | solution.py:417
  63.2 7.1 %collective-permute-start.3 = (bf16[200,768]{1,0:T(8,128)(2,1)S(1)}, bf16[200,768]{1,0:T(8,128)(2,1)S(1)}, u32[]{:S(2)}, u32[]{:S(2)}) collective-permute-start(bf16[200,768]{1,0:T(8,128)(2,1)S(1)} %get-tuple-element.49.own_ref), channel_id=1, source_target_pairs={{4,0},{8,4},{12,8},{16,12},{20,16},{24,20},{28,24},{32,28},{36,32}... | collective-permute-start | bytes 921608 | tf_op jit(solution)/shard_map/ppermute | solution.py:413
  65.2 10.3 %collective-permute-start.2 = (bf16[200,768]{1,0:T(8,128)(2,1)S(1)}, bf16[200,768]{1,0:T(8,128)(2,1)S(1)}, u32[]{:S(2)}, u32[]{:S(2)}) collective-permute-start(bf16[200,768]{1,0:T(8,128)(2,1)S(1)} %get-tuple-element.49.own_ref), channel_id=1, source_target_pairs={{0,4},{4,8},{8,12},{12,16},{16,20},{20,24},{24,28},{28,32},{32,36}... | collective-permute-start | bytes 921608 | tf_op jit(solution)/shard_map/ppermute | solution.py:413
  67.6 1.3 %copy-start.9 = (bf16[800,768]{1,0:T(8,128)(2,1)S(1)}, bf16[800,768]{1,0:T(8,128)(2,1)}, u32[]{:S(2)}) copy-start(bf16[800,768]{1,0:T(8,128)(2,1)} %copy-done.8) | copy-start | bytes 3686404
  70.4 10.7 %collective-permute-start.5 = (bf16[1408,128]{1,0:T(8,128)(2,1)S(1)}, bf16[1408,128]{1,0:T(8,128)(2,1)S(1)}, u32[]{:S(2)}, u32[]{:S(2)}) collective-permute-start(bf16[1408,128]{1,0:T(8,128)(2,1)S(1)} %bitcast.23), channel_id=1, source_target_pairs={{0,4},{4,0},{1,5},{5,1},{2,6},{6,2},{3,7},{7,3},{8,12},{12,8},{9,1... | collective-permute-start | bytes 1081352 | tf_op jit(solution)/shard_map/ppermute | solution.py:458

commit v6 on v5

--- a/solution.py
+++ b/solution.py
@@ -107,9 +107,20 @@
     return total
 
 
-def fill_coef(table_ref, coef_ref):
-    for t in range(TAPS):
-        coef_ref[t] = jnp.broadcast_to(table_ref[:, t : t + 1], (C, COLS))
+def fill_coef(table_ref, store, count):
+    table = table_ref[...]
+    high = table.astype(bf16)
+    low = (table - high.astype(f32)).astype(bf16)
+    both = jnp.concatenate([high, low], axis=1)
+    ones = jnp.ones((2 * COLS, COLS), bf16)
+    lane = lax.broadcasted_iota(jnp.int32, (16, 2 * COLS), 1)
+    lane = jnp.bitwise_and(lane, COLS - 1)
+    for t in range(count):
+        if t % 2 == 0:
+            store(t, jnp.broadcast_to(table[:, t : t + 1], (C, COLS)))
+            continue
+        pick = jnp.where(lane == t, 1.0, 0.0).astype(bf16)
+        store(t, jnp.dot(both * pick[0:1, :], ones, preferred_element_type=f32))
 
 
 def pre_kernel(
@@ -150,9 +161,14 @@
         ograd_ref[:, lanes(r)] = jnp.concatenate([og, jnp.zeros((CX - C, COLS), f32)], axis=0).astype(bf16)
     osum_ref[...] = osum
     agrad_ref[...] = jnp.dot(outw_ref[...], ograd_ref[0:C, :], preferred_element_type=f32)
-    fill_coef(table_ref, coef_ref)
-    for k in range(4):
-        chans_ref[k] = jnp.broadcast_to(table_ref[:, TAPS + k : TAPS + k + 1], (C, COLS))
+
+    def store_pre(t, column):
+        if t < TAPS:
+            coef_ref[t] = column
+        else:
+            chans_ref[t - TAPS] = column
+
+    fill_coef(table_ref, store_pre, TAPS + 4)
 
     def step(g, carry):
         at = pl.ds(pl.multiple_of(g * 8, 8), 8)
@@ -341,7 +357,11 @@
     coef_ref,
 ):
     fill_masks(slot_ref, near_ref, masks_ref)
-    fill_coef(table_ref, coef_ref)
+
+    def store_back(t, column):
+        coef_ref[t] = column
+
+    fill_coef(table_ref, store_back, TAPS)
     fill_rows(north_ref, NORTH, rows_ref)
     fill_rows(own_ref, OWN, rows_ref)
     fill_rows(south_ref, SOUTH, rows_ref)

time: 82.8 us -> 82.2 us (level)
  Pallas kernels: 23.4 us -> 22.4 us
    pallas_call x10, Pallas kernels: 23.4 us -> 22.4 us  [call(): pl.pallas_call(kernel, out_shape=outs, in_specs=[SMEM] * n_smem + [VMEM]...]
  transfers between devices with their start and end apart: 7 -> 7, of which waited for: 3 -> 3; matrix products, arithmetic and copies ran while one was open for 1% -> 1% of each run, Pallas kernels for 18% -> 16%
where the time goes in v6:
time: 82.2 us; the launch traced here: 81.7 us
  blocking collectives  27.5 us (33%)
  Pallas kernels  22.4 us (27%)
  starting transfers between devices  19.3 us (23%)
  waiting for transfers between devices  9.13 us (11%)
  local copies, waits for them, and re-layouts  2.12 us (3%)
  between operations  0.97 us (1%)
    all_to_all x2, blocking collectives, exchange(): return lax.all_to_all(value, axes, 0, 0, tiled=True)  27.5 us
    pallas_call x10, Pallas kernels, call(): pl.pallas_call(kernel, out_shape=outs, in_specs=[SMEM] * n_smem + [VMEM]...  22.4 us
    ppermute x4, starting transfers between devices, shifted(): lax.ppermute(value, TILE_AXES, [(s, s + steps) for s in range(first, last)])  13.5 us
    ppermute x4, waiting for transfers between devices, shifted(): lax.ppermute(value, TILE_AXES, [(s, s + steps) for s in range(first, last)])  8.87 us
    all_to_all x1, starting transfers between devices, exchange(): return lax.all_to_all(value, axes, 0, 0, tiled=True)  5.79 us
    unnamed x24, local copies, waits for them, and re-layouts  1.7 us
  transfers between devices with their start and end apart: 7, of which 3 were waited for; matrix products, arithmetic and copies ran while one was open for 1% of the time, Pallas kernels for 16%

profile of v6, /device:TPU:8, one launch (start us, length us, event | category | flops | bytes accessed | tf_op | source)
XLA Modules:
  0.0 81.7 jit_solution(13120301198777074408)
XLA Ops:
  0.7 1.1 %shard_map.195 = (bf16[200,768]{1,0:T(8,128)(2,1)S(1)}, f32[8,768]{1,0:T(8,128)S(1)}) custom-call(s32[5,1,6]{2,1,0:T(1,128)} %bitcast.35, bf16[200,768]{1,0:T(8,128)(2,1)} %bitcast.34), custom_call_target="tpu_custom_call" | custom-call | flops 1100000000 | bytes 1000000 | tf_op jit(solution)/shard_map/pallas_call | solution.py:415
  1.9 7.2 %collective-permute-start.1 = (bf16[200,768]{1,0:T(8,128)(2,1)S(1)}, bf16[200,768]{1,0:T(8,128)(2,1)S(1)}, u32[]{:S(2)}, u32[]{:S(2)}) collective-permute-start(bf16[200,768]{1,0:T(8,128)(2,1)S(1)} %get-tuple-element.36.own_ref), channel_id=1, source_target_pairs={{4,0},{8,4},{12,8},{16,12},{20,16},{24,20},{28,24},{32,28},{36,32}... | collective-permute-start | bytes 921608 | tf_op jit(solution)/shard_map/ppermute | solution.py:433
  9.1 1.9 %collective-permute-start = (bf16[200,768]{1,0:T(8,128)(2,1)S(1)}, bf16[200,768]{1,0:T(8,128)(2,1)S(1)}, u32[]{:S(2)}, u32[]{:S(2)}) collective-permute-start(bf16[200,768]{1,0:T(8,128)(2,1)S(1)} %get-tuple-element.36.own_ref), channel_id=1, source_target_pairs={{0,4},{4,8},{8,12},{12,16},{16,20},{20,24},{24,28},{28,32},{32,36}... | collective-permute-start | bytes 921608 | tf_op jit(solution)/shard_map/ppermute | solution.py:433
  11.1 0.2 stack.12
  11.2 0.2 stack.13
  11.4 0.2 copy.24
  11.7 0.2 maximum_bitcast_fusion.inwt_ref
  11.9 0.2 copy.27.outw_ref
  12.2 3.4 %shard_map.196 = (f32[200,128]{1,0:T(8,128)S(1)}, f32[21,8,128]{2,1,0:T(8,128)S(1)}, f32[49,200,128]{2,1,0:T(8,128)S(1)}, f32[4,200,128]{2,1,0:T(8,128)S(1)}, f3...) custom-call(s32[1]{0:T(128)} %bitcast.2.slot_ref, ...), custom_call_target="tpu_custom_call" | custom-call | flops 6600000000 | bytes 1000000 | tf_op jit(solution)/shard_map/pallas_call | solution.py:415
  15.6 3.8 %collective-permute-done.north_ref = bf16[200,768]{1,0:T(8,128)(2,1)S(1)} collective-permute-done((bf16[200,768]{1,0:T(8,128)(2,1)S(1)}, bf16[200,768]{1,0:T(8,128)(2,1)S(1)}, u32[]{:S(2)}, u32[]{:S(2)}) %collective-permute-start) | collective-permute-done | bytes 307232 | tf_op jit(solution)/shard_map/ppermute | solution.py:433
  19.4 5.7 %shard_map.197 = (bf16[200,768]{1,0:T(8,128)(2,1)S(1)}, bf16[800,768]{1,0:T(8,128)(2,1)S(1)}, bf16[1408,128]{1,0:T(8,128)(2,1)S(1)}, bf16[1408,128]{1,0:T(8,128)...) custom-call(s32[1]{0:T(128)} %bitcast.10.core_ref.refs_0_, ...), custom_call_target="tpu_custom_call" | custom-call | flops 13200000000 | bytes 1000000 | tf_op jit(solution)/shard_map/pallas_call | solution.py:415
  25.2 3.8 %shard_map.200.small_ref = f32[200,128]{1,0:T(8,128)S(1)} custom-call(f32[24,200,128]{2,1,0:T(8,128)S(1)} %get-tuple-element.52.rows_ref, f32[21,8,128]{2,1,0:T(8,128)S(1)} %get-tuple-element.40.masks_ref, f32[4,200,128]{2,1,0:T(8,128)S(1)} %get-tuple-element.53.vecs_ref), custom_call_target="tpu_custom_call" | custom-call | flops 3300000000 | bytes 1000000 | tf_op jit(solution)/shard_map/pallas_call | solution.py:415
  29.1 15.3 %all_to_all.23.value_ref = bf16[16,88,128]{2,1,0:T(8,128)(2,1)S(1)} all-to-all(bf16[16,88,128]{2,1,0:T(8,128)(2,1)S(1)} %bitcast.25), channel_id=1, replica_groups=mesh['y'=4,'z'=8,'core'=2,'rep'=4] {'y','rep'}, dimensions={0} | all-to-all | bytes 720896 | tf_op jit(solution)/shard_map/all_to_all | solution.py:437
  44.5 12.2 %all_to_all.24.value_ref = bf16[8,88,128]{2,1,0:T(8,128)(2,1)S(1)} all-to-all(bf16[8,88,128]{2,1,0:T(8,128)(2,1)S(1)} %shard_map.202), channel_id=1, replica_groups=mesh['y'=4,'z'=8,'core'=2,'rep'=4] {'z'}, dimensions={0} | all-to-all | bytes 360448 | tf_op jit(solution)/shard_map/all_to_all | solution.py:437
  56.7 0.8 shard_map.203
  57.5 5.8 %all-to-all-start.2 = ((bf16[16,88,128]{2,1,0:T(8,128)(2,1)}), bf16[16,88,128]{2,1,0:T(8,128)(2,1)S(1)}, u32[]{:S(2)}, u32[]{:S(2)}) async-start(bf16[16,88,128]{2,1,0:T(8,128)(2,1)} %shard_map.203), calls=%async_computation.2 | async-start | bytes 720896 | tf_op jit(solution)/shard_map/all_to_all | solution.py:437
  63.2 1.9 %collective-permute-start.3 = (bf16[200,768]{1,0:T(8,128)(2,1)S(1)}, bf16[200,768]{1,0:T(8,128)(2,1)S(1)}, u32[]{:S(2)}, u32[]{:S(2)}) collective-permute-start(bf16[200,768]{1,0:T(8,128)(2,1)S(1)} %get-tuple-element.49.own_ref), channel_id=1, source_target_pairs={{4,0},{8,4},{12,8},{16,12},{20,16},{24,20},{28,24},{32,28},{36,32}... | collective-permute-start | bytes 921608 | tf_op jit(solution)/shard_map/ppermute | solution.py:433
  65.2 2.4 %collective-permute-start.2 = (bf16[200,768]{1,0:T(8,128)(2,1)S(1)}, bf16[200,768]{1,0:T(8,128)(2,1)S(1)}, u32[]{:S(2)}, u32[]{:S(2)}) collective-permute-start(bf16[200,768]{1,0:T(8,128)(2,1)S(1)} %get-tuple-element.49.own_ref), channel_id=1, source_target_pairs={{0,4},{4,8},{8,12},{12,16},{16,20},{20,24},{24,28},{28,32},{32,36}... | collective-permute-start | bytes 921608 | tf_op jit(solution)/shard_map/ppermute | solution.py:433
  67.6 1.3 %copy-done.9 = bf16[800,768]{1,0:T(8,128)(2,1)S(1)} copy-done((bf16[800,768]{1,0:T(8,128)(2,1)S(1)}, bf16[800,768]{1,0:T(8,128)(2,1)}, u32[]{:S(2)}) %copy-start.9) | copy-done | bytes 1228824
  68.9 1.3 %shard_map.198 = bf16[200,768]{1,0:T(8,128)(2,1)} custom-call(bf16[200,768]{1,0:T(8,128)(2,1)S(1)} %get-tuple-element.36.own_ref, f32[8,768]{1,0:T(8,128)S(1)} %get-tuple-element.37.wet_ref, f32[200,128]{1,0:T(8,128)S(1)} %get-tuple-element.39.table_ref, bf16[800,768]{1,0:T(8,128)(2,1)S(1)} %copy-done.9, bf16[200,800]{1,0:T(8,128)(2,1)S(1)} %bitcast.26), custom_call_target="tpu_custom_call" | custom-call | flops 1650000000 | bytes 1000000 | tf_op jit(solution)/shard_map/pallas_call | solution.py:415
  70.1 0.3 all-to-all-done.2
  70.4 5.1 %collective-permute-done.2.north_ref = bf16[200,768]{1,0:T(8,128)(2,1)S(1)} collective-permute-done((bf16[200,768]{1,0:T(8,128)(2,1)S(1)}, bf16[200,768]{1,0:T(8,128)(2,1)S(1)}, u32[]{:S(2)}, u32[]{:S(2)}) %collective-permute-start.2) | collective-permute-done | bytes 307232 | tf_op jit(solution)/shard_map/ppermute | solution.py:433
  75.4 5.0 %shard_map.199 = bf16[200,768]{1,0:T(8,128)(2,1)} custom-call(s32[1]{0:T(128)} %bitcast.2.slot_ref, s32[1,8]{1,0:T(1,128)} %near_ref.3, bf16[200,768]{1,0:T(8,128)(2,1)S(1)} %get-tuple-element.49.own_ref, bf16[200,768]{1,0:T(8,128)(2,1)S(1)} %collective-permute-done.2.north_ref, bf16[200,768]{1,0:T(8,128)(2,1)S(1)} %collective-permute-done.3.south_ref, ...), custom_call_target="tpu_custom_call" | custom-call | flops 6600000000 | bytes 1000000 | tf_op jit(solution)/shard_map/pallas_call | solution.py:415
  80.4 1.3 %shard_map.204 = (f32[200,800]{1,0:T(8,128)}, f32[200,800]{1,0:T(8,128)}, f32[49,200]{1,0:T(8,128)}, f32[1,200]{1,0:T(1,128)}, f32[1,200]{1,0:T(1,128)}, /*index...) custom-call(s32[1]{0:T(128)} %bitcast.10.core_ref.refs_0_, bf16[1408,128]{1,0:T(8,128)(2,1)S(1)} %bitcast.24, ...), custom_call_target="tpu_custom_call" | custom-call | flops 1100000000 | bytes 1000000 | tf_op jit(solution)/shard_map/pallas_call | solution.py:415
  (32 shorter events, 0.4 us)
Async XLA Ops:
  0.6 10.4 %copy-start.10 = (f32[800]{0:T(1024)S(1)}, f32[800]{0:T(1024)}, u32[]{:S(2)}) copy-start(f32[800]{0:T(1024)} %param.20) | copy-start | bytes 9604
  0.7 10.8 %copy-start = (bf16[200,800]{1,0:T(8,128)(2,1)S(1)}, bf16[200,800]{1,0:T(8,128)(2,1)}, u32[]{:S(2)}) copy-start(bf16[200,800]{1,0:T(8,128)(2,1)} %inw_ref.1) | copy-start | bytes 960004
  0.7 11.3 %copy-start.1 = (bf16[800,200]{0,1:T(8,128)(2,1)S(1)}, bf16[800,200]{0,1:T(8,128)(2,1)}, u32[]{:S(2)}) copy-start(bf16[800,200]{0,1:T(8,128)(2,1)} %param.21) | copy-start | bytes 960004
  1.8 10.3 %copy-start.2 = (bf16[1,1,200,768]{3,2,1,0:T(8,128)(2,1)S(1)}, bf16[1,1,200,768]{3,2,1,0:T(8,128)(2,1)}, u32[]{:S(2)}) copy-start(bf16[1,1,200,768]{3,2,1,0:T(8,128)(2,1)} %param.23) | copy-start | bytes 921604
  1.8 10.3 %copy-start.3 = (f32[200,49]{0,1:T(8,128)S(1)}, f32[200,49]{0,1:T(8,128)}, u32[]{:S(2)}) copy-start(f32[200,49]{0,1:T(8,128)} %param.15) | copy-start | bytes 117604
  1.8 10.3 %copy-start.4 = (f32[200]{0:T(256)S(1)}, f32[200]{0:T(256)}, u32[]{:S(2)}) copy-start(f32[200]{0:T(256)} %param.16) | copy-start | bytes 2404
  1.8 10.3 %copy-start.5 = (f32[200]{0:T(256)S(1)}, f32[200]{0:T(256)}, u32[]{:S(2)}) copy-start(f32[200]{0:T(256)} %param.17) | copy-start | bytes 2404
  1.9 10.3 %copy-start.6 = (f32[200]{0:T(256)S(1)}, f32[200]{0:T(256)}, u32[]{:S(2)}) copy-start(f32[200]{0:T(256)} %param.18) | copy-start | bytes 2404
  1.9 10.3 %copy-start.7 = (f32[200]{0:T(256)S(1)}, f32[200]{0:T(256)}, u32[]{:S(2)}) copy-start(f32[200]{0:T(256)} %param.22) | copy-start | bytes 2404
  1.9 13.7 %collective-permute-start.1 = (bf16[200,768]{1,0:T(8,128)(2,1)S(1)}, bf16[200,768]{1,0:T(8,128)(2,1)S(1)}, u32[]{:S(2)}, u32[]{:S(2)}) collective-permute-start(bf16[200,768]{1,0:T(8,128)(2,1)S(1)} %get-tuple-element.36.own_ref), channel_id=1, source_target_pairs={{4,0},{8,4},{12,8},{16,12},{20,16},{24,20},{28,24},{32,28},{36,32}... | collective-permute-start | bytes 921608 | tf_op jit(solution)/shard_map/ppermute | solution.py:433
  9.1 10.3 %collective-permute-start = (bf16[200,768]{1,0:T(8,128)(2,1)S(1)}, bf16[200,768]{1,0:T(8,128)(2,1)S(1)}, u32[]{:S(2)}, u32[]{:S(2)}) collective-permute-start(bf16[200,768]{1,0:T(8,128)(2,1)S(1)} %get-tuple-element.36.own_ref), channel_id=1, source_target_pairs={{0,4},{4,8},{8,12},{12,16},{16,20},{20,24},{24,28},{28,32},{32,36}... | collective-permute-start | bytes 921608 | tf_op jit(solution)/shard_map/ppermute | solution.py:433
  25.1 3.9 %copy-start.8 = (bf16[800,768]{1,0:T(8,128)(2,1)}, bf16[800,768]{1,0:T(8,128)(2,1)S(1)}, u32[]{:S(2)}) copy-start(bf16[800,768]{1,0:T(8,128)(2,1)S(1)} %get-tuple-element.48.act_ref) | copy-start | bytes 3686404
  25.1 3.9 %collective-permute-start.4 = (bf16[1408,128]{1,0:T(8,128)(2,1)S(1)}, bf16[1408,128]{1,0:T(8,128)(2,1)S(1)}, u32[]{:S(2)}, u32[]{:S(2)}) collective-permute-start(bf16[1408,128]{1,0:T(8,128)(2,1)S(1)} %get-tuple-element.51), channel_id=1, source_target_pairs={{0,4},{4,0},{1,5},{5,1},{2,6},{6,2},{3,7},{7,3},{8,12},{12,8},{9,1... | collective-permute-start | bytes 1081352 | tf_op jit(solution)/shard_map/ppermute | solution.py:471
  57.5 12.9 %all-to-all-start.2 = ((bf16[16,88,128]{2,1,0:T(8,128)(2,1)}), bf16[16,88,128]{2,1,0:T(8,128)(2,1)S(1)}, u32[]{:S(2)}, u32[]{:S(2)}) async-start(bf16[16,88,128]{2,1,0:T(8,128)(2,1)} %shard_map.203), calls=%async_computation.2 | async-start | bytes 720896 | tf_op jit(solution)/shard_map/all_to_all | solution.py:437
  63.2 7.1 %collective-permute-start.3 = (bf16[200,768]{1,0:T(8,128)(2,1)S(1)}, bf16[200,768]{1,0:T(8,128)(2,1)S(1)}, u32[]{:S(2)}, u32[]{:S(2)}) collective-permute-start(bf16[200,768]{1,0:T(8,128)(2,1)S(1)} %get-tuple-element.49.own_ref), channel_id=1, source_target_pairs={{4,0},{8,4},{12,8},{16,12},{20,16},{24,20},{28,24},{32,28},{36,32}... | collective-permute-start | bytes 921608 | tf_op jit(solution)/shard_map/ppermute | solution.py:433
  65.2 10.3 %collective-permute-start.2 = (bf16[200,768]{1,0:T(8,128)(2,1)S(1)}, bf16[200,768]{1,0:T(8,128)(2,1)S(1)}, u32[]{:S(2)}, u32[]{:S(2)}) collective-permute-start(bf16[200,768]{1,0:T(8,128)(2,1)S(1)} %get-tuple-element.49.own_ref), channel_id=1, source_target_pairs={{0,4},{4,8},{8,12},{12,16},{16,20},{20,24},{24,28},{28,32},{32,36}... | collective-permute-start | bytes 921608 | tf_op jit(solution)/shard_map/ppermute | solution.py:433
  67.6 1.3 %copy-start.9 = (bf16[800,768]{1,0:T(8,128)(2,1)S(1)}, bf16[800,768]{1,0:T(8,128)(2,1)}, u32[]{:S(2)}) copy-start(bf16[800,768]{1,0:T(8,128)(2,1)} %copy-done.8) | copy-start | bytes 3686404
  70.4 10.1 %collective-permute-start.5 = (bf16[1408,128]{1,0:T(8,128)(2,1)S(1)}, bf16[1408,128]{1,0:T(8,128)(2,1)S(1)}, u32[]{:S(2)}, u32[]{:S(2)}) collective-permute-start(bf16[1408,128]{1,0:T(8,128)(2,1)S(1)} %bitcast.23), channel_id=1, source_target_pairs={{0,4},{4,0},{1,5},{5,1},{2,6},{6,2},{3,7},{7,3},{8,12},{12,8},{9,1... | collective-permute-start | bytes 1081352 | tf_op jit(solution)/shard_map/ppermute | solution.py:478

commit v7 on v6

--- a/solution.py
+++ b/solution.py
@@ -437,13 +437,6 @@
     return lax.all_to_all(value, axes, 0, 0, tiled=True)
 
 
-def add_kernel(keep_ref, got_ref, small_ref, pair_ref):
-    last = (BLOCKS - 1) * C
-    total = keep_ref[...].astype(f32) + got_ref[...].astype(f32)
-    pair_ref[...] = total.astype(bf16)
-    pair_ref[last : last + C, :] = (total[last : last + C, :] + small_ref[...]).astype(bf16)
-
-
 def fold_kernel(value_ref, copies_ref):
     total = value_ref[0].astype(f32)
     for k in range(1, value_ref.shape[0]):
@@ -469,7 +462,9 @@
 def reduce_pack(keep, send, small):
     swap = [(0, 1), (1, 0)]
     got = lax.ppermute(send, "core", swap)
-    (pair,) = call(add_kernel, [pltpu.VMEM((HALF, COLS), bf16)], 0, [keep, got, small], limit=4)
+    first = (BLOCKS - 1) * C
+    small = jnp.pad(small, ((first, HALF - first - C), (0, 0)))
+    pair = (keep.astype(f32) + got.astype(f32) + small).astype(bf16)
     part = exchange(pair, PLANE)
     part = fold(part, PLANE, "z")
     part = exchange(part, "z")

time: 82.2 us -> 82.2 us (level)
    pallas_call x10 -> x9, Pallas kernels: 22.4 us -> 22.3 us  [call(): pl.pallas_call(kernel, out_shape=outs, in_specs=[SMEM] * n_smem + [VMEM]...]
where the time goes in v7:
time: 82.2 us; the launch traced here: 81.7 us
  blocking collectives  27.5 us (33%)
  Pallas kernels  22.3 us (27%)
  starting transfers between devices  19.3 us (23%)
  waiting for transfers between devices  9.13 us (11%)
  local copies, waits for them, and re-layouts  2.12 us (3%)
  between operations  0.97 us (1%)
    all_to_all x2, blocking collectives, exchange(): return lax.all_to_all(value, axes, 0, 0, tiled=True)  27.5 us
    pallas_call x9, Pallas kernels, call(): pl.pallas_call(kernel, out_shape=outs, in_specs=[SMEM] * n_smem + [VMEM]...  22.3 us
    ppermute x4, starting transfers between devices, shifted(): lax.ppermute(value, TILE_AXES, [(s, s + steps) for s in range(first, last)])  13.5 us
    ppermute x4, waiting for transfers between devices, shifted(): lax.ppermute(value, TILE_AXES, [(s, s + steps) for s in range(first, last)])  8.87 us
    all_to_all x1, starting transfers between devices, exchange(): return lax.all_to_all(value, axes, 0, 0, tiled=True)  5.79 us
    unnamed x24, local copies, waits for them, and re-layouts  1.7 us
  transfers between devices with their start and end apart: 7, of which 3 were waited for; matrix products, arithmetic and copies ran while one was open for 1% of the time, Pallas kernels for 16%

profile of v7, /device:TPU:8, one launch (start us, length us, event | category | flops | bytes accessed | tf_op | source)
XLA Modules:
  0.0 81.7 jit_solution(5576916074317471729)
XLA Ops:
  0.7 1.1 %shard_map.195 = (bf16[200,768]{1,0:T(8,128)(2,1)S(1)}, f32[8,768]{1,0:T(8,128)S(1)}) custom-call(s32[5,1,6]{2,1,0:T(1,128)} %bitcast.35, bf16[200,768]{1,0:T(8,128)(2,1)} %bitcast.34), custom_call_target="tpu_custom_call" | custom-call | flops 1100000000 | bytes 1000000 | tf_op jit(solution)/shard_map/pallas_call | solution.py:415
  1.9 7.2 %collective-permute-start.1 = (bf16[200,768]{1,0:T(8,128)(2,1)S(1)}, bf16[200,768]{1,0:T(8,128)(2,1)S(1)}, u32[]{:S(2)}, u32[]{:S(2)}) collective-permute-start(bf16[200,768]{1,0:T(8,128)(2,1)S(1)} %get-tuple-element.36.own_ref), channel_id=1, source_target_pairs={{4,0},{8,4},{12,8},{16,12},{20,16},{24,20},{28,24},{32,28},{36,32}... | collective-permute-start | bytes 921608 | tf_op jit(solution)/shard_map/ppermute | solution.py:433
  9.1 1.9 %collective-permute-start = (bf16[200,768]{1,0:T(8,128)(2,1)S(1)}, bf16[200,768]{1,0:T(8,128)(2,1)S(1)}, u32[]{:S(2)}, u32[]{:S(2)}) collective-permute-start(bf16[200,768]{1,0:T(8,128)(2,1)S(1)} %get-tuple-element.36.own_ref), channel_id=1, source_target_pairs={{0,4},{4,8},{8,12},{12,16},{16,20},{20,24},{24,28},{28,32},{32,36}... | collective-permute-start | bytes 921608 | tf_op jit(solution)/shard_map/ppermute | solution.py:433
  11.1 0.2 stack.12
  11.2 0.2 stack.13
  11.4 0.2 copy.24
  11.7 0.2 maximum_bitcast_fusion.inwt_ref
  11.9 0.2 copy.27.outw_ref
  12.2 3.4 %shard_map.196 = (f32[200,128]{1,0:T(8,128)S(1)}, f32[21,8,128]{2,1,0:T(8,128)S(1)}, f32[49,200,128]{2,1,0:T(8,128)S(1)}, f32[4,200,128]{2,1,0:T(8,128)S(1)}, f3...) custom-call(s32[1]{0:T(128)} %bitcast.2.slot_ref, ...), custom_call_target="tpu_custom_call" | custom-call | flops 6600000000 | bytes 1000000 | tf_op jit(solution)/shard_map/pallas_call | solution.py:415
  15.6 3.8 %collective-permute-done.north_ref = bf16[200,768]{1,0:T(8,128)(2,1)S(1)} collective-permute-done((bf16[200,768]{1,0:T(8,128)(2,1)S(1)}, bf16[200,768]{1,0:T(8,128)(2,1)S(1)}, u32[]{:S(2)}, u32[]{:S(2)}) %collective-permute-start) | collective-permute-done | bytes 307232 | tf_op jit(solution)/shard_map/ppermute | solution.py:433
  19.4 5.7 %shard_map.197 = (bf16[200,768]{1,0:T(8,128)(2,1)S(1)}, bf16[800,768]{1,0:T(8,128)(2,1)S(1)}, bf16[1408,128]{1,0:T(8,128)(2,1)S(1)}, bf16[1408,128]{1,0:T(8,128)...) custom-call(s32[1]{0:T(128)} %bitcast.10.core_ref.refs_0_, ...), custom_call_target="tpu_custom_call" | custom-call | flops 13200000000 | bytes 1000000 | tf_op jit(solution)/shard_map/pallas_call | solution.py:415
  25.2 3.8 %shard_map.200 = f32[200,128]{1,0:T(8,128)S(1)} custom-call(f32[24,200,128]{2,1,0:T(8,128)S(1)} %get-tuple-element.52.rows_ref, f32[21,8,128]{2,1,0:T(8,128)S(1)} %get-tuple-element.40.masks_ref, f32[4,200,128]{2,1,0:T(8,128)S(1)} %get-tuple-element.53.vecs_ref), custom_call_target="tpu_custom_call" | custom-call | flops 3300000000 | bytes 1000000 | tf_op jit(solution)/shard_map/pallas_call | solution.py:415
  29.1 15.3 %all_to_all.23.value_ref = bf16[16,88,128]{2,1,0:T(8,128)(2,1)S(1)} all-to-all(bf16[16,88,128]{2,1,0:T(8,128)(2,1)S(1)} %bitcast.33), channel_id=1, replica_groups=mesh['y'=4,'z'=8,'core'=2,'rep'=4] {'y','rep'}, dimensions={0} | all-to-all | bytes 720896 | tf_op jit(solution)/shard_map/all_to_all | solution.py:437
  44.5 12.2 %all_to_all.24.value_ref = bf16[8,88,128]{2,1,0:T(8,128)(2,1)S(1)} all-to-all(bf16[8,88,128]{2,1,0:T(8,128)(2,1)S(1)} %shard_map.201), channel_id=1, replica_groups=mesh['y'=4,'z'=8,'core'=2,'rep'=4] {'z'}, dimensions={0} | all-to-all | bytes 360448 | tf_op jit(solution)/shard_map/all_to_all | solution.py:437
  56.7 0.8 shard_map.202
  57.5 5.8 %all-to-all-start.2 = ((bf16[16,88,128]{2,1,0:T(8,128)(2,1)}), bf16[16,88,128]{2,1,0:T(8,128)(2,1)S(1)}, u32[]{:S(2)}, u32[]{:S(2)}) async-start(bf16[16,88,128]{2,1,0:T(8,128)(2,1)} %shard_map.202), calls=%async_computation.2 | async-start | bytes 720896 | tf_op jit(solution)/shard_map/all_to_all | solution.py:437
  63.3 1.9 %collective-permute-start.3 = (bf16[200,768]{1,0:T(8,128)(2,1)S(1)}, bf16[200,768]{1,0:T(8,128)(2,1)S(1)}, u32[]{:S(2)}, u32[]{:S(2)}) collective-permute-start(bf16[200,768]{1,0:T(8,128)(2,1)S(1)} %get-tuple-element.49.own_ref), channel_id=1, source_target_pairs={{4,0},{8,4},{12,8},{16,12},{20,16},{24,20},{28,24},{32,28},{36,32}... | collective-permute-start | bytes 921608 | tf_op jit(solution)/shard_map/ppermute | solution.py:433
  65.2 2.4 %collective-permute-start.2 = (bf16[200,768]{1,0:T(8,128)(2,1)S(1)}, bf16[200,768]{1,0:T(8,128)(2,1)S(1)}, u32[]{:S(2)}, u32[]{:S(2)}) collective-permute-start(bf16[200,768]{1,0:T(8,128)(2,1)S(1)} %get-tuple-element.49.own_ref), channel_id=1, source_target_pairs={{0,4},{4,8},{8,12},{12,16},{16,20},{20,24},{24,28},{28,32},{32,36}... | collective-permute-start | bytes 921608 | tf_op jit(solution)/shard_map/ppermute | solution.py:433
  67.6 1.3 %copy-done.9 = bf16[800,768]{1,0:T(8,128)(2,1)S(1)} copy-done((bf16[800,768]{1,0:T(8,128)(2,1)S(1)}, bf16[800,768]{1,0:T(8,128)(2,1)}, u32[]{:S(2)}) %copy-start.9) | copy-done | bytes 1228824
  68.9 1.3 %shard_map.198 = bf16[200,768]{1,0:T(8,128)(2,1)} custom-call(bf16[200,768]{1,0:T(8,128)(2,1)S(1)} %get-tuple-element.36.own_ref, f32[8,768]{1,0:T(8,128)S(1)} %get-tuple-element.37.wet_ref, f32[200,128]{1,0:T(8,128)S(1)} %get-tuple-element.39.table_ref, bf16[800,768]{1,0:T(8,128)(2,1)S(1)} %copy-done.9, bf16[200,800]{1,0:T(8,128)(2,1)S(1)} %bitcast.25), custom_call_target="tpu_custom_call" | custom-call | flops 1650000000 | bytes 1000000 | tf_op jit(solution)/shard_map/pallas_call | solution.py:415
  70.1 0.3 all-to-all-done.2
  70.4 5.1 %collective-permute-done.2.north_ref = bf16[200,768]{1,0:T(8,128)(2,1)S(1)} collective-permute-done((bf16[200,768]{1,0:T(8,128)(2,1)S(1)}, bf16[200,768]{1,0:T(8,128)(2,1)S(1)}, u32[]{:S(2)}, u32[]{:S(2)}) %collective-permute-start.2) | collective-permute-done | bytes 307232 | tf_op jit(solution)/shard_map/ppermute | solution.py:433
  75.5 5.0 %shard_map.199 = bf16[200,768]{1,0:T(8,128)(2,1)} custom-call(s32[1]{0:T(128)} %bitcast.2.slot_ref, s32[1,8]{1,0:T(1,128)} %near_ref.3, bf16[200,768]{1,0:T(8,128)(2,1)S(1)} %get-tuple-element.49.own_ref, bf16[200,768]{1,0:T(8,128)(2,1)S(1)} %collective-permute-done.2.north_ref, bf16[200,768]{1,0:T(8,128)(2,1)S(1)} %collective-permute-done.3.south_ref, ...), custom_call_target="tpu_custom_call" | custom-call | flops 6600000000 | bytes 1000000 | tf_op jit(solution)/shard_map/pallas_call | solution.py:415
  80.5 1.3 %shard_map.203 = (f32[200,800]{1,0:T(8,128)}, f32[200,800]{1,0:T(8,128)}, f32[49,200]{1,0:T(8,128)}, f32[1,200]{1,0:T(1,128)}, f32[1,200]{1,0:T(1,128)}, /*index...) custom-call(s32[1]{0:T(128)} %bitcast.10.core_ref.refs_0_, bf16[1408,128]{1,0:T(8,128)(2,1)S(1)} %bitcast.24, ...), custom_call_target="tpu_custom_call" | custom-call | flops 1100000000 | bytes 1000000 | tf_op jit(solution)/shard_map/pallas_call | solution.py:415
  (32 shorter events, 0.4 us)
Async XLA Ops:
  0.6 10.4 %copy-start.10 = (f32[800]{0:T(1024)S(1)}, f32[800]{0:T(1024)}, u32[]{:S(2)}) copy-start(f32[800]{0:T(1024)} %param.20) | copy-start | bytes 9604
  0.7 10.8 %copy-start = (bf16[200,800]{1,0:T(8,128)(2,1)S(1)}, bf16[200,800]{1,0:T(8,128)(2,1)}, u32[]{:S(2)}) copy-start(bf16[200,800]{1,0:T(8,128)(2,1)} %inw_ref.1) | copy-start | bytes 960004
  0.7 11.3 %copy-start.1 = (bf16[800,200]{0,1:T(8,128)(2,1)S(1)}, bf16[800,200]{0,1:T(8,128)(2,1)}, u32[]{:S(2)}) copy-start(bf16[800,200]{0,1:T(8,128)(2,1)} %param.21) | copy-start | bytes 960004
  1.8 10.3 %copy-start.2 = (bf16[1,1,200,768]{3,2,1,0:T(8,128)(2,1)S(1)}, bf16[1,1,200,768]{3,2,1,0:T(8,128)(2,1)}, u32[]{:S(2)}) copy-start(bf16[1,1,200,768]{3,2,1,0:T(8,128)(2,1)} %param.23) | copy-start | bytes 921604
  1.8 10.3 %copy-start.3 = (f32[200,49]{0,1:T(8,128)S(1)}, f32[200,49]{0,1:T(8,128)}, u32[]{:S(2)}) copy-start(f32[200,49]{0,1:T(8,128)} %param.15) | copy-start | bytes 117604
  1.8 10.3 %copy-start.4 = (f32[200]{0:T(256)S(1)}, f32[200]{0:T(256)}, u32[]{:S(2)}) copy-start(f32[200]{0:T(256)} %param.16) | copy-start | bytes 2404
  1.8 10.3 %copy-start.5 = (f32[200]{0:T(256)S(1)}, f32[200]{0:T(256)}, u32[]{:S(2)}) copy-start(f32[200]{0:T(256)} %param.17) | copy-start | bytes 2404
  1.9 10.3 %copy-start.6 = (f32[200]{0:T(256)S(1)}, f32[200]{0:T(256)}, u32[]{:S(2)}) copy-start(f32[200]{0:T(256)} %param.18) | copy-start | bytes 2404
  1.9 10.3 %copy-start.7 = (f32[200]{0:T(256)S(1)}, f32[200]{0:T(256)}, u32[]{:S(2)}) copy-start(f32[200]{0:T(256)} %param.22) | copy-start | bytes 2404
  1.9 13.7 %collective-permute-start.1 = (bf16[200,768]{1,0:T(8,128)(2,1)S(1)}, bf16[200,768]{1,0:T(8,128)(2,1)S(1)}, u32[]{:S(2)}, u32[]{:S(2)}) collective-permute-start(bf16[200,768]{1,0:T(8,128)(2,1)S(1)} %get-tuple-element.36.own_ref), channel_id=1, source_target_pairs={{4,0},{8,4},{12,8},{16,12},{20,16},{24,20},{28,24},{32,28},{36,32}... | collective-permute-start | bytes 921608 | tf_op jit(solution)/shard_map/ppermute | solution.py:433
  9.1 10.3 %collective-permute-start = (bf16[200,768]{1,0:T(8,128)(2,1)S(1)}, bf16[200,768]{1,0:T(8,128)(2,1)S(1)}, u32[]{:S(2)}, u32[]{:S(2)}) collective-permute-start(bf16[200,768]{1,0:T(8,128)(2,1)S(1)} %get-tuple-element.36.own_ref), channel_id=1, source_target_pairs={{0,4},{4,8},{8,12},{12,16},{16,20},{20,24},{24,28},{28,32},{32,36}... | collective-permute-start | bytes 921608 | tf_op jit(solution)/shard_map/ppermute | solution.py:433
  25.1 3.9 %copy-start.8 = (bf16[800,768]{1,0:T(8,128)(2,1)}, bf16[800,768]{1,0:T(8,128)(2,1)S(1)}, u32[]{:S(2)}) copy-start(bf16[800,768]{1,0:T(8,128)(2,1)S(1)} %get-tuple-element.48.act_ref) | copy-start | bytes 3686404
  25.1 3.9 %collective-permute-start.4 = (bf16[1408,128]{1,0:T(8,128)(2,1)S(1)}, bf16[1408,128]{1,0:T(8,128)(2,1)S(1)}, u32[]{:S(2)}, u32[]{:S(2)}) collective-permute-start(bf16[1408,128]{1,0:T(8,128)(2,1)S(1)} %get-tuple-element.51), channel_id=1, source_target_pairs={{0,4},{4,0},{1,5},{5,1},{2,6},{6,2},{3,7},{7,3},{8,12},{12,8},{9,1... | collective-permute-start | bytes 1081352 | tf_op jit(solution)/shard_map/ppermute | solution.py:464
  57.5 12.9 %all-to-all-start.2 = ((bf16[16,88,128]{2,1,0:T(8,128)(2,1)}), bf16[16,88,128]{2,1,0:T(8,128)(2,1)S(1)}, u32[]{:S(2)}, u32[]{:S(2)}) async-start(bf16[16,88,128]{2,1,0:T(8,128)(2,1)} %shard_map.202), calls=%async_computation.2 | async-start | bytes 720896 | tf_op jit(solution)/shard_map/all_to_all | solution.py:437
  63.3 7.1 %collective-permute-start.3 = (bf16[200,768]{1,0:T(8,128)(2,1)S(1)}, bf16[200,768]{1,0:T(8,128)(2,1)S(1)}, u32[]{:S(2)}, u32[]{:S(2)}) collective-permute-start(bf16[200,768]{1,0:T(8,128)(2,1)S(1)} %get-tuple-element.49.own_ref), channel_id=1, source_target_pairs={{4,0},{8,4},{12,8},{16,12},{20,16},{24,20},{28,24},{32,28},{36,32}... | collective-permute-start | bytes 921608 | tf_op jit(solution)/shard_map/ppermute | solution.py:433
  65.2 10.3 %collective-permute-start.2 = (bf16[200,768]{1,0:T(8,128)(2,1)S(1)}, bf16[200,768]{1,0:T(8,128)(2,1)S(1)}, u32[]{:S(2)}, u32[]{:S(2)}) collective-permute-start(bf16[200,768]{1,0:T(8,128)(2,1)S(1)} %get-tuple-element.49.own_ref), channel_id=1, source_target_pairs={{0,4},{4,8},{8,12},{12,16},{16,20},{20,24},{24,28},{28,32},{32,36}... | collective-permute-start | bytes 921608 | tf_op jit(solution)/shard_map/ppermute | solution.py:433
  67.6 1.3 %copy-start.9 = (bf16[800,768]{1,0:T(8,128)(2,1)S(1)}, bf16[800,768]{1,0:T(8,128)(2,1)}, u32[]{:S(2)}) copy-start(bf16[800,768]{1,0:T(8,128)(2,1)} %copy-done.8) | copy-start | bytes 3686404
  70.4 10.1 %collective-permute-start.5 = (bf16[1408,128]{1,0:T(8,128)(2,1)S(1)}, bf16[1408,128]{1,0:T(8,128)(2,1)S(1)}, u32[]{:S(2)}, u32[]{:S(2)}) collective-permute-start(bf16[1408,128]{1,0:T(8,128)(2,1)S(1)} %bitcast.23), channel_id=1, source_target_pairs={{0,4},{4,0},{1,5},{5,1},{2,6},{6,2},{3,7},{7,3},{8,12},{12,8},{9,1... | collective-permute-start | bytes 1081352 | tf_op jit(solution)/shard_map/ppermute | solution.py:473
